TPU v7x, 512 devices: a whole 4x8x8 slice. The times are simulated.
512 devices in a mesh: section: 2 (over core), sy: 8 (over y), sx: 8 (over z), mb: 4 (over x).
Axes of the slice: x: 4, y: 8, z: 8, core: 2. Of those that a mesh axis runs over, the one named last changes fastest.
Arguments:
- frames: bfloat16 [4, 512, 512, 128], P('mb', 'sy', 'sx'), may hold values from -6 to 6
- encode_weight: bfloat16 [512, 384], replicated, may hold values from -0.25 to 0.25
- conv_weight: bfloat16 [2, 1, 3456, 384], P('section', None, ('sy', 'sx')), may hold values from -0.109375 to 0.109375
- norm_gain: float32 [2, 1, 384], P('section'), may hold values from 0.1 to 1.9
- head_weight: bfloat16 [384, 256], replicated, may hold values from -0.3125 to 0.3125
- prior_logits: bfloat16 [4, 256, 256, 256], P('mb', 'sy', 'sx'), may hold values from -12 to 249
- target_bins: int32 [4, 256, 256], P('mb', 'sy', 'sx'), may hold values from 0 to 255
Outputs:
- section_features: bfloat16 [2, 4, 256, 256, 384], P('section', 'mb', 'sy', 'sx')
- head_step: float32 [384, 256], P('section')
- mean_loss: float32 [], replicated
All inputs are finite; a program needn't handle non-finite values.
Results may differ from a plain program's by a relative error of at most 0.008.
Values may be sent and summed in bfloat16 or wider, within the bound.
No kernel may reach another device: no remote copies, remote signals or barrier semaphores. Data moves between devices by JAX's collectives and lax.ppermute only.
A program may use at most 64 MiB of HBM per device.

v0:
```python
import jax
import jax.numpy as jnp
from jax import lax
from jax.sharding import PartitionSpec as P

FIRST_DILATION = 1


def padded_2(block, sides, width):
    for axis, dim in sides:
        count = lax.axis_size(axis)
        forward = [(i, i + 1) for i in range(count - 1)]
        backward = [(target, source) for source, target in forward]
        low = lax.ppermute(
            lax.slice_in_dim(block, block.shape[dim] - width, None, axis=dim), axis, forward
        )
        high = lax.ppermute(lax.slice_in_dim(block, 0, width, axis=dim), axis, backward)
        block = jnp.concatenate([low, block, high], axis=dim)
    return block


def from_behind(block, axis, distance):
    devices = range(lax.axis_size(axis))
    route = [(i - distance, i) for i in devices if i - distance in devices]
    return lax.ppermute(block, axis, route)


def norm_gelu(activations, gain):
    values = activations.astype(jnp.float32)
    center = jnp.mean(values, axis=-1, keepdims=True)
    offset = values - center
    spread = jnp.mean(offset * offset, axis=-1, keepdims=True)
    normed = offset * lax.rsqrt(spread + 1e-05) * gain
    return jax.nn.gelu(normed, approximate=False).astype(jnp.bfloat16)


def per_device(
    frames, encode_weight, conv_weight, norm_gain, head_weight, prior_logits, target_bins
):
    first_section = lax.axis_index("section") == 0
    micro_count = frames.shape[0]
    side_cells = frames.shape[1] // 2
    input_width = frames.shape[3]
    channels = encode_weight.shape[1]
    bins_count = head_weight.shape[1]
    parts_y = lax.axis_size("sy")
    parts_x = lax.axis_size("sx")
    cell_count = side_cells * side_cells
    kernel = encode_weight.reshape(2, 2, input_width, channels)
    grad_total = jnp.zeros((channels, bins_count), jnp.float32)
    loss_total = jnp.zeros((), jnp.float32)
    first_out = []
    second_out = []
    handed = None
    for tick_index in range(micro_count + 1):
        if tick_index == 0:
            blocks = frames[0].reshape(side_cells, 2, side_cells, 2, input_width)
            activations = jnp.einsum(
                "apbqc,pqco->abo", blocks, kernel, preferred_element_type=jnp.float32
            ).astype(jnp.bfloat16)
        else:
            activations = handed
        apply_reach = FIRST_DILATION * 2**0
        hidden = norm_gelu(activations, norm_gain[0, 0])
        haloed = padded_2(hidden, (("sy", 0), ("sx", 1)), apply_reach)
        zero_padded = jnp.pad(
            hidden, ((apply_reach, apply_reach), (apply_reach, apply_reach), (0, 0))
        )
        apply_padded = jnp.where(first_section, haloed, zero_padded)
        windows = [
            apply_padded[
                tap_row * apply_reach : tap_row * apply_reach + side_cells,
                tap_column * apply_reach : tap_column * apply_reach + side_cells,
            ]
            for tap_row in range(3)
            for tap_column in range(3)
        ]
        patches = jnp.concatenate(windows, axis=2).reshape(cell_count, 9 * channels)
        summed = jnp.dot(
            patches,
            lax.all_gather(conv_weight[0, 0], ("sy", "sx"), axis=0, tiled=True),
            preferred_element_type=jnp.float32,
        )
        activations = (
            activations.astype(jnp.float32) + summed.reshape(side_cells, side_cells, channels)
        ).astype(jnp.bfloat16)
        if tick_index < micro_count:
            first_out.append(activations)
        rows_y = side_cells // parts_y
        rows_x = side_cells // parts_x
        plain_view = activations.reshape(parts_y, rows_y, parts_x, rows_x, channels)
        spaced = activations.reshape(rows_y, parts_y, rows_x, parts_x, channels).transpose(
            1, 0, 3, 2, 4
        )
        outgoing = jnp.where(first_section, spaced, plain_view)
        arrived = lax.all_to_all(
            lax.all_to_all(outgoing, "sy", split_axis=0, concat_axis=0, tiled=True),
            "sx",
            split_axis=2,
            concat_axis=2,
            tiled=True,
        )
        direct = arrived.reshape(side_cells, side_cells, channels)
        restored = arrived.transpose(1, 0, 3, 2, 4).reshape(side_cells, side_cells, channels)
        moved = jnp.where(first_section, direct, restored)
        if tick_index >= 1:
            second_out.append(moved)
            flat_rows = moved.reshape(cell_count, channels)
            logits = jnp.dot(flat_rows, head_weight, preferred_element_type=jnp.float32)
            logits = logits + prior_logits[tick_index - 1].reshape(cell_count, bins_count).astype(
                jnp.float32
            )
            row_top = jnp.max(logits, axis=1, keepdims=True)
            shifted = logits - row_top
            exp_terms = jnp.exp(shifted)
            exp_total = jnp.sum(exp_terms, axis=1, keepdims=True)
            softmax_rows = exp_terms / exp_total
            onehot = (
                target_bins[tick_index - 1].reshape(cell_count, 1)
                == lax.broadcasted_iota(jnp.int32, (1, bins_count), 1)
            ).astype(jnp.float32)
            loss_sum = jnp.sum(jnp.log(exp_total[:, 0]) - jnp.sum(shifted * onehot, axis=1))
            delta_rows = (softmax_rows - onehot).astype(jnp.bfloat16)
            grad_part = lax.dot_general(
                flat_rows, delta_rows, (((0,), (0,)), ((), ())), preferred_element_type=jnp.float32
            )
            grad_part, loss_sum = (grad_part, loss_sum)
            grad_total = jnp.where(first_section, 0.0, grad_part)
            loss_total = jnp.where(first_section, 0.0, loss_sum)
        if tick_index < micro_count:
            handed = from_behind(moved, "section", 1)
    stacked = jnp.stack([jnp.where(first_section, first_out[0], second_out[0])])[None]
    gradient, loss_all = lax.psum((grad_total, loss_total), ("sy", "sx", "mb"))
    head_full = gradient * lax.rsqrt(jnp.mean(gradient * gradient) + 1e-06)
    mean_local = loss_all / (micro_count * lax.axis_size("mb") * cell_count * parts_y * parts_x)
    half_rows = channels // 2
    sent_rows, sent_loss = (
        from_behind(head_full[:half_rows].astype(jnp.bfloat16), "section", -1).astype(jnp.float32),
        from_behind(mean_local.astype(jnp.bfloat16), "section", -1).astype(mean_local.dtype),
    )
    head_step = jnp.where(first_section, sent_rows, head_full[half_rows:])
    mean_loss = jnp.where(first_section, sent_loss, mean_local)
    return (stacked, head_step, mean_loss)


def solution(mesh):
    placed = (
        P("mb", "sy", "sx", None),
        P(),
        P("section", None, ("sy", "sx"), None),
        P("section", None, None),
        P(),
        P("mb", "sy", "sx", None),
        P("mb", "sy", "sx"),
    )
    return jax.shard_map(
        per_device,
        mesh=mesh,
        in_specs=placed,
        out_specs=(P("section", "mb", "sy", "sx", None), P("section", None), P()),
        check_vma=False,
    )
```

profile of v0, /device:TPU:1, one launch (start us, length us, event | category | flops | bytes accessed | tf_op | source)
XLA Modules:
  0.0 957.4 jit_solution(2720262242174057233)
XLA Ops:
  7.2 1.5 copy.50
  9.5 2.0 convert_reduce_fusion.1
  12.0 3.8 fusion.20
  15.9 4.0 collective-permute-start
  19.9 1.3 collective-permute-start.1
  21.2 3.3 collective-permute-done.1
  24.6 4.0 collective-permute-start.2
  29.9 4.2 collective-permute-done.3
  37.0 1.3 slice_dynamic-update-slice_fusion.15
  42.9 1.4 slice_dynamic-update-slice_fusion.10
  45.5 57.8 %all-gather.3.cloned.1.call-done = bf16[1,1,3456,384]{3,1,0,2:T(2,128)(2,1)} async-done(((bf16[1,1,54,384]{3,1,0,2:T(2,128)(2,1)}), bf16[1,1,3456,384]{3,1,0,2:T(2,128)(2,1)}) %all-gather.3.cloned.1.call-update) | async-done | bytes 2654224 | tf_op jit(solution)/shard_map/all_gather | solution.py:81
  103.3 8.4 fusion.22
  112.4 23.7 %all_to_all.20 = bf16[8,4,8,4,384]{4,3,1,2,0:T(4,128)(2,1)S(1)} all-to-all(bf16[8,4,8,4,384]{4,3,1,2,0:T(4,128)(2,1)S(1)} %bitcast_select_fusion.2), channel_id=1, replica_groups=mesh['section'=2,'sy'=8,'sx'=8,'mb'=4] {'sy'}, dimensions={0} | all-to-all | bytes 1572864 | tf_op jit(solution)/shard_map/all_to_all | solution.py:97
  136.3 19.7 %all_to_all.21 = bf16[8,4,8,4,384]{4,3,1,0,2:T(4,128)(2,1)S(1)} all-to-all(bf16[8,4,8,4,384]{4,3,1,0,2:T(4,128)(2,1)S(1)} %copy.53), channel_id=1, replica_groups=mesh['section'=2,'sy'=8,'sx'=8,'mb'=4] {'sx'}, dimensions={2} | all-to-all | bytes 1572864 | tf_op jit(solution)/shard_map/all_to_all | solution.py:96
  157.3 1.5 collective-permute-start.4
  158.8 9.2 collective-permute-done.4
  168.8 3.8 fusion.13
  172.6 1.4 collective-permute-start.5
  174.0 1.3 collective-permute-start.6
  175.3 3.3 collective-permute-done.6
  178.7 2.2 collective-permute-start.7
  182.2 3.6 collective-permute-done.8
  189.1 3.9 fusion.24
  193.6 24.2 %all_to_all.22 = bf16[8,4,8,4,384]{4,3,1,2,0:T(4,128)(2,1)S(1)} all-to-all(bf16[8,4,8,4,384]{4,3,1,2,0:T(4,128)(2,1)S(1)} %bitcast_select_fusion.1), channel_id=1, replica_groups=mesh['section'=2,'sy'=8,'sx'=8,'mb'=4] {'sy'}, dimensions={0} | all-to-all | bytes 1572864 | tf_op jit(solution)/shard_map/all_to_all | solution.py:97
  219.0 3.5 all-to-all-start.3
  222.9 1.3 copy.63
  225.1 16.5 %all-to-all-done.3 = bf16[8,4,8,4,384]{4,3,1,0,2:T(4,128)(2,1)S(1)} async-done(((bf16[8,4,8,4,384]{4,3,1,0,2:T(4,128)(2,1)}), bf16[8,4,8,4,384]{4,3,1,0,2:T(4,128)(2,1)S(1)}, u32[]{:S(2)}, u32[]{:S(2)}) %all-to-all-start.3) | async-done | bytes 786464 | tf_op jit(solution)/shard_map/all_to_all | solution.py:96
  246.1 1.3 convolution_select_fusion
  248.7 575.3 %psum.15 = f32[]{:T(128)} all-reduce(f32[]{:T(128)S(6)} %select_n.85), channel_id=1, replica_groups=mesh['section'=2,'sy'=8,'sx'=8,'mb'=4] {'sy','sx','mb'}, use_global_device_ids=true, to_apply=%region_10.11 | all-reduce | flops 1 | bytes 8 | tf_op jit(solution)/shard_map/psum | solution.py:133
  824.8 117.5 %collective-permute-start.10 = (bf16[]{:T(256)}, bf16[]{:T(256)}, u32[]{:S(2)}, u32[]{:S(2)}) collective-permute-start(bf16[]{:T(256)} %convert_element_type.60), channel_id=1, source_target_pairs={{256,0},{257,1},{258,2},{259,3},{260,4},{261,5},{262,6},{263,7},{2... | collective-permute-start | bytes 14 | tf_op jit(solution)/shard_map/ppermute | solution.py:25
  942.3 1.7 multiply_reduce_fusion
  945.7 1.3 collective-permute-start.9
  (82 shorter events, 30.0 us)
Async XLA Ops:
  7.2 2.3 copy-start
  7.2 96.1 %all-gather.3.cloned.1.call-start = ((), (), s32[]{:S(2)}) async-start(), calls=%async_computation.5 | async-start | bytes 5391360 | tf_op jit(solution)/shard_map/all_gather | solution.py:81
  15.9 5.3 collective-permute-start
  19.9 4.6 collective-permute-start.1
  24.6 5.3 collective-permute-start.2
  28.6 5.5 collective-permute-start.3
  157.3 10.7 %collective-permute-start.4 = (bf16[32,32,384]{2,1,0:T(8,128)(2,1)S(1)}, bf16[32,32,384]{2,1,0:T(8,128)(2,1)S(1)}, u32[]{:S(2)}, u32[]{:S(2)}) collective-permute-start(bf16[32,32,384]{2,1,0:T(8,128)(2,1)S(1)} %broadcast_select_fusion), channel_id=1, source_target_pairs={{0,256},{1,257},{2,258},{3,259},{4,260},{5,261},{6,262},{7,263},{8... | collective-permute-start | bytes 2359304 | tf_op jit(solution)/shard_map/ppermute | solution.py:25
  172.6 2.7 collective-permute-start.5
  174.0 4.6 collective-permute-start.6
  178.7 3.5 collective-permute-start.7
  180.9 4.9 collective-permute-start.8
  186.3 2.8 slice-start
  187.4 1.7 slice-start.1
  217.8 5.0 copy-start.3
  219.0 22.6 %all-to-all-start.3 = ((bf16[8,4,8,4,384]{4,3,1,0,2:T(4,128)(2,1)}), bf16[8,4,8,4,384]{4,3,1,0,2:T(4,128)(2,1)S(1)}, u32[]{:S(2)}, u32[]{:S(2)}) async-start(bf16[8,4,8,4,384]{4,3,1,0,2:T(4,128)(2,1)} %copy.58), calls=%async_computation.3 | async-start | bytes 1572864 | tf_op jit(solution)/shard_map/all_to_all | solution.py:96
  222.5 719.8 %all-reduce.4.cloned.1.call-start = ((), (), s32[]{:S(2)}) async-start(), calls=%async_computation.4 | async-start | bytes 786432 | tf_op jit(solution)/shard_map/psum | solution.py:133
  243.0 1.1 copy-start.2
  244.1 1.2 copy-start.1
  244.1 1.2 copy-start.4
  824.8 123.2 %collective-permute-start.10 = (bf16[]{:T(256)}, bf16[]{:T(256)}, u32[]{:S(2)}, u32[]{:S(2)}) collective-permute-start(bf16[]{:T(256)} %convert_element_type.60), channel_id=1, source_target_pairs={{256,0},{257,1},{258,2},{259,3},{260,4},{261,5},{262,6},{263,7},{2... | collective-permute-start | bytes 14 | tf_op jit(solution)/shard_map/ppermute | solution.py:25
  945.7 2.9 collective-permute-start.9
Sparse Core Ops, SparseCore 0:
  11.7 91.6 all-gather.2
  247.5 225.9 all-reduce.3
where the time goes:
time: 958 us; the launch traced here: 957 us
  blocking collectives  643 us (67%)
  starting transfers between devices  141 us (15%)
  waiting for transfers between devices  97.9 us (10%)
  local copies, waits for them, and re-layouts  24 us (3%)
  between operations  18.2 us (2%)
  other arithmetic  17.5 us (2%)
  matrix products  16.1 us (2%)
    psum x1, blocking collectives, per_device(): gradient, loss_all = lax.psum((grad_total, loss_total), ('sy', 'sx', 'mb'))  575 us
    ppermute x3, starting transfers between devices, from_behind(): return lax.ppermute(block, axis, route)  120 us
    all_gather x1, waiting for transfers between devices, per_device(): lax.all_gather(conv_weight[0, 0], ('sy', 'sx'), axis=0, tiled=True)  57.8 us
    all_to_all x2, blocking collectives, per_device(): lax.all_to_all(outgoing, 'sy', split_axis=0, concat_axis=0, tiled=True)  47.8 us
    all_to_all x1, blocking collectives, per_device(): lax.all_to_all(lax.all_to_all(outgoing, 'sy', split_axis=0, concat_axis=0...  19.7 us
  transfers between devices with their start and end apart: 14, of which 7 were waited for; matrix products, arithmetic and copies ran while one was open for 3% of the time, Pallas kernels for 0%

commit v1 on v0

v1 whole, which is shorter than its diff:
```python
import jax
import jax.numpy as jnp
from jax import lax
from jax.sharding import PartitionSpec as P

FIRST_DILATION = 1
SECTION_FACTOR = 8


def norm_gelu(activations, gain):
    values = activations.astype(jnp.float32)
    center = jnp.mean(values, axis=-1, keepdims=True)
    offset = values - center
    spread = jnp.mean(offset * offset, axis=-1, keepdims=True)
    normed = offset * lax.rsqrt(spread + 1e-05) * gain
    return jax.nn.gelu(normed, approximate=False).astype(jnp.bfloat16)


def copies_to(block, axes, count):
    return lax.all_to_all(
        jnp.broadcast_to(block[None], (count,) + block.shape), axes, split_axis=0, concat_axis=0, tiled=True
    )


def swap(block):
    return lax.ppermute(block, "section", [(0, 1), (1, 0)])


def patches_of(padded, rows, columns, step):
    channels = padded.shape[-1]
    windows = [
        padded[i * step : i * step + rows, j * step : j * step + columns] for i in range(3) for j in range(3)
    ]
    return jnp.concatenate(windows, axis=2).reshape(rows * columns, 9 * channels)


def split_two(value):
    high = value.astype(jnp.bfloat16)
    low = (value - high.astype(jnp.float32)).astype(jnp.bfloat16)
    return high, low


def per_device(
    frames, encode_weight, conv_weight, norm_gain, head_weight, prior_logits, target_bins
):
    section = lax.axis_index("section")
    first = section == 0
    parts_y = lax.axis_size("sy")
    parts_x = lax.axis_size("sx")
    parts_b = lax.axis_size("mb")
    side = frames.shape[1] // 2
    half = side // 2
    channels = encode_weight.shape[1]
    bins = head_weight.shape[1]
    near = FIRST_DILATION
    far = FIRST_DILATION * SECTION_FACTOR
    reach = near + far

    shard = conv_weight[0, 0]
    strip = copies_to(shard, "sx", parts_x).reshape(parts_x * shard.shape[0], channels)
    weight_own = lax.all_gather(strip, "sy", axis=0, tiled=True)
    gain_own = norm_gain[0, 0]
    gain_other = swap(gain_own)
    gain_0 = jnp.where(first, gain_own, gain_other)
    gain_1 = jnp.where(first, gain_other, gain_own)

    blocks = frames[0].reshape(side, 2, side, 2, frames.shape[3])
    kernel = encode_weight.reshape(2, 2, frames.shape[3], channels)
    encoded = jnp.einsum(
        "apbqc,pqco->abo", blocks, kernel, preferred_element_type=jnp.float32
    ).astype(jnp.bfloat16)

    outgoing = jnp.where(first, encoded[side - reach :], encoded[:reach])
    route = [(y, y + 1) for y in range(parts_y - 1)] + [
        (parts_y + y + 1, parts_y + y) for y in range(parts_y - 1)
    ]
    arrived = lax.ppermute(outgoing, ("section", "sy"), route)
    rows = jnp.where(
        first,
        jnp.concatenate([arrived, encoded[: half + reach]], axis=0),
        jnp.concatenate([encoded[half - reach :], arrived], axis=0),
    )
    forward = [(x, x + 1) for x in range(parts_x - 1)]
    backward = [(x + 1, x) for x in range(parts_x - 1)]
    left = lax.ppermute(rows[:, side - reach :], "sx", forward)
    right = lax.ppermute(rows[:, :reach], "sx", backward)
    haloed = jnp.concatenate([left, rows, right], axis=1)

    tall, wide = half + 2 * far, side + 2 * far
    hidden = norm_gelu(haloed, gain_0)
    patches = patches_of(hidden, tall, wide, near)
    weight_own, patches = lax.optimization_barrier((weight_own, patches))
    weight_other = swap(weight_own)
    weight_0 = jnp.where(first, weight_own, weight_other)
    weight_1 = jnp.where(first, weight_other, weight_own)
    summed = jnp.dot(patches, weight_0, preferred_element_type=jnp.float32)
    features_0 = (
        haloed[near : near + tall, near : near + wide].astype(jnp.float32)
        + summed.reshape(tall, wide, channels)
    ).astype(jnp.bfloat16)

    row_at = lax.axis_index("sy") * side + section * half - far + lax.broadcasted_iota(jnp.int32, (tall, wide, 1), 0)
    column_at = lax.axis_index("sx") * side - far + lax.broadcasted_iota(jnp.int32, (tall, wide, 1), 1)
    inside = (row_at >= 0) & (row_at < side * parts_y) & (column_at >= 0) & (column_at < side * parts_x)
    hidden = jnp.where(inside, norm_gelu(features_0, gain_1), jnp.bfloat16(0))
    patches = patches_of(hidden, half, side, far)
    summed = jnp.dot(patches, weight_1, preferred_element_type=jnp.float32)
    own_0 = features_0[far : far + half, far : far + side]
    own_1 = (own_0.astype(jnp.float32) + summed.reshape(half, side, channels)).astype(jnp.bfloat16)

    cells = half * side
    flat = own_1.reshape(cells, channels)
    prior = lax.dynamic_slice_in_dim(prior_logits[0], section * half, half, axis=0)
    target = lax.dynamic_slice_in_dim(target_bins[0], section * half, half, axis=0)
    logits = jnp.dot(flat, head_weight, preferred_element_type=jnp.float32)
    logits = logits + prior.reshape(cells, bins).astype(jnp.float32)
    row_top = jnp.max(logits, axis=1, keepdims=True)
    shifted = logits - row_top
    exp_terms = jnp.exp(shifted)
    exp_total = jnp.sum(exp_terms, axis=1, keepdims=True)
    softmax_rows = exp_terms / exp_total
    onehot = (
        target.reshape(cells, 1) == lax.broadcasted_iota(jnp.int32, (1, bins), 1)
    ).astype(jnp.float32)
    loss_sum = jnp.sum(jnp.log(exp_total[:, 0]) - jnp.sum(shifted * onehot, axis=1))
    delta_rows = (softmax_rows - onehot).astype(jnp.bfloat16)
    gradient = lax.dot_general(
        flat, delta_rows, (((0,), (0,)), ((), ())), preferred_element_type=jnp.float32
    )

    slots = parts_x * parts_b
    slot_rows = channels // slots

    def with_loss(values, loss):
        high, low = split_two(loss)
        lane = lax.broadcasted_iota(jnp.int32, (1, bins), 1)
        row = jnp.where(lane == 0, high, jnp.where(lane == 1, low, jnp.bfloat16(0)))
        row = jnp.broadcast_to(row, values.shape[:-2] + (1, bins))
        return jnp.concatenate([values.astype(jnp.bfloat16), row], axis=-2)

    packed = with_loss(gradient.reshape(slots, slot_rows, bins), loss_sum)
    packed = lax.all_to_all(packed, ("sx", "mb"), split_axis=0, concat_axis=0, tiled=True)
    partial = jnp.sum(packed.astype(jnp.float32), axis=0)
    packed = with_loss(partial[:slot_rows], partial[slot_rows, 0] + partial[slot_rows, 1])
    packed = copies_to(packed, ("section", "sy"), 2 * parts_y)
    partial = jnp.sum(packed.astype(jnp.float32), axis=0)
    loss_all = partial[slot_rows, 0] + partial[slot_rows, 1]
    gathered = copies_to(partial[:slot_rows].astype(jnp.bfloat16), ("sx", "mb"), slots)
    gradient = gathered.reshape(channels, bins).astype(jnp.float32)
    scale = lax.rsqrt(jnp.mean(gradient * gradient) + 1e-06)
    own_rows = lax.dynamic_slice_in_dim(gradient, section * (channels // 2), channels // 2, axis=0)
    head_step = own_rows * scale
    mean_loss = loss_all / (parts_b * parts_y * parts_x * side * side)

    sent = swap(jnp.where(first, own_1, own_0))
    stacked = jnp.where(
        first, jnp.concatenate([own_0, sent], axis=0), jnp.concatenate([sent, own_1], axis=0)
    )[None, None]
    return (stacked, head_step, mean_loss)


def solution(mesh):
    placed = (
        P("mb", "sy", "sx", None),
        P(),
        P("section", None, ("sy", "sx"), None),
        P("section", None, None),
        P(),
        P("mb", "sy", "sx", None),
        P("mb", "sy", "sx"),
    )
    return jax.shard_map(
        per_device,
        mesh=mesh,
        in_specs=placed,
        out_specs=(P("section", "mb", "sy", "sx", None), P("section", None), P()),
        check_vma=False,
    )
```

time: 958 us -> 195 us (0.20)
  blocking collectives: 643 us -> 20.1 us
  starting transfers between devices: 141 us -> 41.2 us
  waiting for transfers between devices: 97.9 us -> 54 us
    psum x1 -> x0, blocking collectives: 575 us -> none  [per_device(): gradient, loss_all = lax.psum((grad_total, loss_total), ('sy', 'sx', 'mb'))]
    ppermute x11 -> x6, starting transfers between devices: 137 us -> 17.8 us  [the longest x3 10.9 us: swap(): return lax.ppermute(block, 'section', [(0, 1), (1, 0)])]
    all_to_all x3 -> x1, blocking collectives: 67.5 us -> 20.1 us  [per_device(): lax.all_to_all(packed, ('sx', 'mb'), split_axis=0, concat_axis=0, tiled=T...]
    all_gather x1, waiting for transfers between devices: 57.8 us -> 20.3 us  [per_device(): weight_own = lax.all_gather(strip, 'sy', axis=0, tiled=True)]
    all_to_all x1 -> x3, starting transfers between devices: 3.55 us -> 23.4 us  [copies_to(): lax.all_to_all(jnp.broadcast_to(block[None], (count,) + block.shape), axe...]
    ppermute x11 -> x6, waiting for transfers between devices: 23.5 us -> 10.1 us  [the longest x1 5.91 us: per_device(): arrived = lax.ppermute(outgoing, ('section', 'sy'), route)]
    all_to_all x1 -> x3, waiting for transfers between devices: 16.5 us -> 23.5 us  [copies_to(): lax.all_to_all(jnp.broadcast_to(block[None], (count,) + block.shape), axe...]
  transfers between devices with their start and end apart: 14 -> 10, of which waited for: 7 -> 6; matrix products, arithmetic and copies ran while one was open for 3% -> 14% of each run, Pallas kernels for 0% -> 0%
where the time goes in v1:
time: 195 us; the launch traced here: 191 us
  waiting for transfers between devices  54 us (28%)
  starting transfers between devices  41.2 us (21%)
  local copies, waits for them, and re-layouts  21 us (11%)
  other arithmetic  20.7 us (11%)
  between operations  20.3 us (10%)
  blocking collectives  20.1 us (10%)
  matrix products  14.3 us (7%)
    all_to_all x3, waiting for transfers between devices, copies_to(): lax.all_to_all(jnp.broadcast_to(block[None], (count,) + block.shape), axe...  23.5 us
    all_to_all x3, starting transfers between devices, copies_to(): lax.all_to_all(jnp.broadcast_to(block[None], (count,) + block.shape), axe...  23.4 us
    all_gather x1, waiting for transfers between devices, per_device(): weight_own = lax.all_gather(strip, 'sy', axis=0, tiled=True)  20.3 us
    all_to_all x1, blocking collectives, per_device(): lax.all_to_all(packed, ('sx', 'mb'), split_axis=0, concat_axis=0, tiled=T...  20.1 us
    unnamed x30, local copies, waits for them, and re-layouts  14.2 us
    ppermute x3, starting transfers between devices, swap(): return lax.ppermute(block, 'section', [(0, 1), (1, 0)])  10.9 us
    dot_general x1, matrix products, per_device(): summed = jnp.dot(patches, weight_0, preferred_element_type=jnp.float32)  9.26 us
    convert_element_type x1, other arithmetic, norm_gelu(): return jax.nn.gelu(normed, approximate=False).astype(jnp.bfloat16)  6.79 us
  transfers between devices with their start and end apart: 10, of which 6 were waited for; matrix products, arithmetic and copies ran while one was open for 14% of the time, Pallas kernels for 0%

profile of v1, /device:TPU:1, one launch (start us, length us, event | category | flops | bytes accessed | tf_op | source)
XLA Modules:
  0.0 191.5 jit_solution(5893310341925343398)
XLA Ops:
  7.2 2.1 %bitcast_convert_fusion = bf16[32,32,384]{2,1,0:T(8,128)(2,1)S(1)} fusion(bf16[2,2,128,384,1]{3,2,1,0,4:T(8,128)(2,1)} %bitcast.43, bf16[32,2,32,2,128]{4,3,2,1,0:T(2,128)(2,1)} %bitcast.42), kind=kOutput, calls=%fused_computation.66 | convolution fusion | flops 403046400 | bytes 2228224 | tf_op jit(solution)/shard_map/apbqc,pqco->abo/dot_general | solution.py:69
  9.3 1.4 collective-permute-start
  10.9 5.9 %collective-permute-done = bf16[9,32,384]{2,1,0:T(8,128)(2,1)S(1)} collective-permute-done((bf16[9,32,384]{2,1,0:T(8,128)(2,1)S(1)}, bf16[9,32,384]{2,1,0:T(8,128)(2,1)S(1)}, u32[]{:S(2)}, u32[]{:S(2)}) %collective-permute-start) | collective-permute-done | bytes 221216 | tf_op jit(solution)/shard_map/ppermute | solution.py:77
  17.1 4.2 %collective-permute-start.1 = (bf16[34,9,384]{2,1,0:T(8,128)(2,1)S(1)}, bf16[34,9,384]{2,1,0:T(8,128)(2,1)S(1)}, u32[]{:S(2)}, u32[]{:S(2)}) collective-permute-start(bf16[34,9,384]{2,1,0:T(8,128)(2,1)S(1)} %get-tuple-element.16), channel_id=1, source_target_pairs={{0,4},{4,8},{8,12},{12,16},{16,20},{20,24},{24,28},{1,5},{5,9},{9,... | collective-permute-start | bytes 705032 | tf_op jit(solution)/shard_map/ppermute | solution.py:85
  21.3 1.3 collective-permute-start.2
  22.6 3.3 %collective-permute-start.3 = (f32[384]{0:T(512)S(1)}, f32[384]{0:T(512)S(1)}, u32[]{:S(2)}, u32[]{:S(2)}) collective-permute-start(f32[384]{0:T(512)S(1)} %reduce.1), channel_id=1, source_target_pairs={{0,256},{256,0},{1,257},{257,1},{2,258},{258,2},{3,259},{259,3},{4... | collective-permute-start | bytes 4616 | tf_op jit(solution)/shard_map/ppermute | solution.py:26
  26.7 11.3 %all-to-all-start = ((bf16[8,54,384]{2,1,0:T(8,128)(2,1)}), bf16[8,54,384]{2,1,0:T(8,128)(2,1)S(1)}, u32[]{:S(2)}, u32[]{:S(2)}) async-start(bf16[8,54,384]{2,1,0:T(8,128)(2,1)} %broadcast_in_dim.65), calls=%async_computation | async-start | bytes 688128 | tf_op jit(solution)/shard_map/all_to_all | solution.py:20
  38.8 1.7 convert_reduce_fusion
  41.4 10.7 %all-to-all-done = bf16[8,54,384]{2,1,0:T(8,128)(2,1)S(1)} async-done(((bf16[8,54,384]{2,1,0:T(8,128)(2,1)}), bf16[8,54,384]{2,1,0:T(8,128)(2,1)S(1)}, u32[]{:S(2)}, u32[]{:S(2)}) %all-to-all-start) | async-done | bytes 331808 | tf_op jit(solution)/shard_map/all_to_all | solution.py:20
  53.0 6.8 %fusion.7 = bf16[34,50,384]{2,1,0:T(8,128)(2,1)S(1)} fusion(bf16[34,50,384]{2,1,0:T(8,128)(2,1)S(1)} %get-tuple-element.14, f32[384]{0:T(512)S(1)} %get-tuple-element.25, f32[34,50]{1,0:T(8,128)S(1)} %add_rsqrt_fusion, f32[34,50]{1,0:T(8,128)S(1)} %broadcast_multiply_fusion), kind=kLoop, calls=%fused_computation.13 | loop fusion | flops 45043200 | bytes 2626336 | tf_op jit(solution)/shard_map/convert_element_type | solution.py:16
  59.8 1.2 slice_dynamic-update-slice_fusion.8
  61.0 1.6 slice_dynamic-update-slice_fusion.7
  62.6 1.6 slice_dynamic-update-slice_fusion.6
  64.2 1.2 slice_dynamic-update-slice_fusion.5
  65.4 1.6 slice_dynamic-update-slice_fusion.4
  67.0 1.6 slice_dynamic-update-slice_fusion.3
  68.6 1.2 slice_dynamic-update-slice_fusion.2
  69.8 1.6 slice_dynamic-update-slice_fusion.1
  71.5 1.6 slice_dynamic-update-slice_fusion
  73.0 20.3 %all-gather.2.cloned.1.call-done = bf16[3456,384]{1,0:T(8,128)(2,1)} async-done(((bf16[432,384]{1,0:T(8,128)(2,1)}), bf16[3456,384]{1,0:T(8,128)(2,1)}) %all-gather.2.cloned.1.call-update) | async-done | bytes 2654224 | tf_op jit(solution)/shard_map/all_gather | solution.py:61
  93.3 5.6 %collective-permute-start.4 = (bf16[3456,384]{1,0:T(8,128)(2,1)}, bf16[3456,384]{1,0:T(8,128)(2,1)}, u32[]{:S(2)}, u32[]{:S(2)}) collective-permute-start(bf16[3456,384]{1,0:T(8,128)(2,1)} %all-gather.2.cloned.1.call-done), channel_id=1, source_target_pairs={{0,256},{256,0},{1,257},{257,1},{2,258},{258,2},{3,259},{259,3},{4... | collective-permute-start | bytes 7962632 | tf_op jit(solution)/shard_map/ppermute | solution.py:26
  99.4 4.2 %collective-permute-done.4 = bf16[3456,384]{1,0:T(8,128)(2,1)} collective-permute-done((bf16[3456,384]{1,0:T(8,128)(2,1)}, bf16[3456,384]{1,0:T(8,128)(2,1)}, u32[]{:S(2)}, u32[]{:S(2)}) %collective-permute-start.4) | collective-permute-done | bytes 2654240 | tf_op jit(solution)/shard_map/ppermute | solution.py:26
  103.6 9.3 %fusion.25 = f32[1536,384]{1,0:T(8,128)S(1)} fusion(bf16[1536,3456]{1,0:T(8,128)(2,1)} %bitcast.6, bf16[3456,384]{1,0:T(8,128)(2,1)} %all-gather.2.cloned.1.call-done, bf16[3456,384]{1,0:T(8,128)(2,1)} %collective-permute-done.4, pred[]{:T(512)S(6)} %eq.50), kind=kOutput, calls=%fused_computation.37 | convolution fusion | flops 4078190592 | bytes 18284544 | tf_op jit(solution)/shard_map/dot_general | solution.py:96
  114.2 6.2 %fusion.47 = bf16[32,48,384]{2,1,0:T(8,128)(2,1)S(1)} fusion(bf16[32,48,384]{2,1,0:T(8,128)(2,1)S(1)} %get-tuple-element.12, f32[384]{0:T(512)S(1)} %get-tuple-element.24, f32[32,48]{1,0:T(8,128)S(1)} %add_rsqrt_fusion.1, f32[32,48]{1,0:T(8,128)S(1)} %broadcast_multiply_fusion.1, pred[32,48]{1,0:T(8,128)(4,1)S(1)} %and_and_fusion), kind=kLoop, calls=%fused_computation.69 | loop fusion | flops 41287680 | bytes 2374656 | tf_op jit(solution)/shard_map/jit(_where)/select_n | solution.py:105
  121.1 1.2 copy-done.6
  122.3 2.1 %broadcast_select_fusion = (bf16[16,32,384]{2,1,0:T(8,128)(2,1)S(1)}, bf16[16,32,384]{2,1,0:T(8,128)(2,1)S(1)}, bf16[1,1,16,32,384]{4,3,2,1,0:T(8,128)(2,1)S(1)}) fusion(pred[]{:T(512)S(6)} %eq.50, bf16[32,48,384]{2,1,0:T(8,128)(2,1)S(1)} %get-tuple-element.12, bf16[16,32,3456]{2,1,0:T(8,128)(2,1)S(1)} %slice_dynamic-update-slice_fusion.9, ...), kind=kOutput, calls=%fused_computation.100 | convolution fusion | flops 1361068032 | bytes 10421248 | tf_op jit(solution)/shard_map/dot_general | solution.py:107
  127.8 20.1 %all_to_all.20 = bf16[32,13,256]{2,1,0:T(8,128)(2,1)S(1)} all-to-all(bf16[32,13,256]{2,1,0:T(8,128)(2,1)S(1)} %copy.42), channel_id=1, replica_groups=mesh['section'=2,'sy'=8,'sx'=8,'mb'=4] {'sx','mb'}, dimensions={0} | all-to-all | bytes 425984 | tf_op jit(solution)/shard_map/all_to_all | solution.py:142
  150.6 8.3 %all-to-all-start.2 = ((bf16[16,13,256]{2,1,0:T(8,128)(2,1)}), bf16[16,13,256]{2,1,0:T(8,128)(2,1)S(1)}, u32[]{:S(2)}, u32[]{:S(2)}) async-start(bf16[16,13,256]{2,1,0:T(8,128)(2,1)} %broadcast_in_dim.75), calls=%async_computation.2 | async-start | bytes 262144 | tf_op jit(solution)/shard_map/all_to_all | solution.py:20
  158.9 2.0 %collective-permute-start.5 = (bf16[16,32,384]{2,1,0:T(8,128)(2,1)S(1)}, bf16[16,32,384]{2,1,0:T(8,128)(2,1)S(1)}, u32[]{:S(2)}, u32[]{:S(2)}) collective-permute-start(bf16[16,32,384]{2,1,0:T(8,128)(2,1)S(1)} %get-tuple-element.9), channel_id=1, source_target_pairs={{0,256},{256,0},{1,257},{257,1},{2,258},{258,2},{3,259},{259,3},{4... | collective-permute-start | bytes 1179656 | tf_op jit(solution)/shard_map/ppermute | solution.py:26
  160.9 5.3 %all-to-all-done.2 = bf16[16,13,256]{2,1,0:T(8,128)(2,1)S(1)} async-done(((bf16[16,13,256]{2,1,0:T(8,128)(2,1)}), bf16[16,13,256]{2,1,0:T(8,128)(2,1)S(1)}, u32[]{:S(2)}, u32[]{:S(2)}) %all-to-all-start.2) | async-done | bytes 106528 | tf_op jit(solution)/shard_map/all_to_all | solution.py:20
  167.0 3.9 %all-to-all-start.3 = ((bf16[32,12,256]{2,1,0:T(8,128)(2,1)}), bf16[32,12,256]{2,1,0:T(8,128)(2,1)S(1)}, u32[]{:S(2)}, u32[]{:S(2)}) async-start(bf16[32,12,256]{2,1,0:T(8,128)(2,1)} %broadcast_in_dim.76), calls=%async_computation.3 | async-start | bytes 524288 | tf_op jit(solution)/shard_map/all_to_all | solution.py:20
  173.8 7.6 %all-to-all-done.3 = bf16[32,12,256]{2,1,0:T(8,128)(2,1)S(1)} async-done(((bf16[32,12,256]{2,1,0:T(8,128)(2,1)}), bf16[32,12,256]{2,1,0:T(8,128)(2,1)S(1)}, u32[]{:S(2)}, u32[]{:S(2)}) %all-to-all-start.3) | async-done | bytes 196640 | tf_op jit(solution)/shard_map/all_to_all | solution.py:20
  (75 shorter events, 13.3 us)
Async XLA Ops:
  7.2 91.7 %copy-start = (bf16[1,32,32,256]{3,2,1,0:T(8,128)(2,1)S(1)}, bf16[1,32,32,256]{3,2,1,0:T(8,128)(2,1)}, u32[]{:S(2)}) copy-start(bf16[1,32,32,256]{3,2,1,0:T(8,128)(2,1)} %param.12) | copy-start | bytes 1572868
  9.3 13.3 %copy-start.5 = (f32[1,1,384]{2,1,0:T(1,128)S(1)}, f32[1,1,384]{2,1,0:T(1,128)}, u32[]{:S(2)}) copy-start(f32[1,1,384]{2,1,0:T(1,128)} %param.10) | copy-start | bytes 4612
  9.3 16.6 %copy-start.3 = (bf16[1,1,54,384]{3,2,1,0:T(8,128)(2,1)S(1)}, bf16[1,1,54,384]{3,2,1,0:T(8,128)(2,1)}, u32[]{:S(2)}) copy-start(bf16[1,1,54,384]{3,2,1,0:T(8,128)(2,1)} %param.9) | copy-start | bytes 124420
  9.3 7.5 %collective-permute-start = (bf16[9,32,384]{2,1,0:T(8,128)(2,1)S(1)}, bf16[9,32,384]{2,1,0:T(8,128)(2,1)S(1)}, u32[]{:S(2)}, u32[]{:S(2)}) collective-permute-start(bf16[9,32,384]{2,1,0:T(8,128)(2,1)S(1)} %slice_select_fusion), channel_id=1, source_target_pairs={{0,32},{32,64},{64,96},{96,128},{128,160},{160,192},{192,224},{288... | collective-permute-start | bytes 663560 | tf_op jit(solution)/shard_map/ppermute | solution.py:77
  17.1 20.9 %collective-permute-start.1 = (bf16[34,9,384]{2,1,0:T(8,128)(2,1)S(1)}, bf16[34,9,384]{2,1,0:T(8,128)(2,1)S(1)}, u32[]{:S(2)}, u32[]{:S(2)}) collective-permute-start(bf16[34,9,384]{2,1,0:T(8,128)(2,1)S(1)} %get-tuple-element.16), channel_id=1, source_target_pairs={{0,4},{4,8},{8,12},{12,16},{16,20},{20,24},{24,28},{1,5},{5,9},{9,... | collective-permute-start | bytes 705032 | tf_op jit(solution)/shard_map/ppermute | solution.py:85
  21.3 17.5 %collective-permute-start.2 = (bf16[34,9,384]{2,1,0:T(8,128)(2,1)S(1)}, bf16[34,9,384]{2,1,0:T(8,128)(2,1)}, u32[]{:S(2)}, u32[]{:S(2)}) collective-permute-start(bf16[34,9,384]{2,1,0:T(8,128)(2,1)S(1)} %get-tuple-element.17), channel_id=1, source_target_pairs={{4,0},{8,4},{12,8},{16,12},{20,16},{24,20},{28,24},{5,1},{9,5},{13... | collective-permute-start | bytes 705032 | tf_op jit(solution)/shard_map/ppermute | solution.py:86
  22.6 15.4 %collective-permute-start.3 = (f32[384]{0:T(512)S(1)}, f32[384]{0:T(512)S(1)}, u32[]{:S(2)}, u32[]{:S(2)}) collective-permute-start(f32[384]{0:T(512)S(1)} %reduce.1), channel_id=1, source_target_pairs={{0,256},{256,0},{1,257},{257,1},{2,258},{258,2},{3,259},{259,3},{4... | collective-permute-start | bytes 4616 | tf_op jit(solution)/shard_map/ppermute | solution.py:26
  26.7 25.4 %all-to-all-start = ((bf16[8,54,384]{2,1,0:T(8,128)(2,1)}), bf16[8,54,384]{2,1,0:T(8,128)(2,1)S(1)}, u32[]{:S(2)}, u32[]{:S(2)}) async-start(bf16[8,54,384]{2,1,0:T(8,128)(2,1)} %broadcast_in_dim.65), calls=%async_computation | async-start | bytes 688128 | tf_op jit(solution)/shard_map/all_to_all | solution.py:20
  38.0 55.3 %all-gather.2.cloned.1.call-start = ((), (), s32[]{:S(2)}) async-start(), calls=%async_computation.4 | async-start | bytes 2985984 | tf_op jit(solution)/shard_map/all_gather | solution.py:61
  38.1 0.8 copy-start.1
  71.5 27.7 %copy-start.4 = (s32[1,32,32]{2,1,0:T(8,128)S(1)}, s32[1,32,32]{2,1,0:T(8,128)}, u32[]{:S(2)}) copy-start(s32[1,32,32]{2,1,0:T(8,128)} %param.13) | copy-start | bytes 12292
  93.3 10.3 %collective-permute-start.4 = (bf16[3456,384]{1,0:T(8,128)(2,1)}, bf16[3456,384]{1,0:T(8,128)(2,1)}, u32[]{:S(2)}, u32[]{:S(2)}) collective-permute-start(bf16[3456,384]{1,0:T(8,128)(2,1)} %all-gather.2.cloned.1.call-done), channel_id=1, source_target_pairs={{0,256},{256,0},{1,257},{257,1},{2,258},{258,2},{3,259},{259,3},{4... | collective-permute-start | bytes 7962632 | tf_op jit(solution)/shard_map/ppermute | solution.py:26
  120.5 1.8 copy-start.6
  122.3 2.4 %copy-start.2 = (bf16[384,256]{1,0:T(8,128)(2,1)S(1)}, bf16[384,256]{1,0:T(8,128)(2,1)}, u32[]{:S(2)}) copy-start(bf16[384,256]{1,0:T(8,128)(2,1)} %param.11) | copy-start | bytes 589828
  150.6 15.6 %all-to-all-start.2 = ((bf16[16,13,256]{2,1,0:T(8,128)(2,1)}), bf16[16,13,256]{2,1,0:T(8,128)(2,1)S(1)}, u32[]{:S(2)}, u32[]{:S(2)}) async-start(bf16[16,13,256]{2,1,0:T(8,128)(2,1)} %broadcast_in_dim.75), calls=%async_computation.2 | async-start | bytes 262144 | tf_op jit(solution)/shard_map/all_to_all | solution.py:20
  158.9 12.0 %collective-permute-start.5 = (bf16[16,32,384]{2,1,0:T(8,128)(2,1)S(1)}, bf16[16,32,384]{2,1,0:T(8,128)(2,1)S(1)}, u32[]{:S(2)}, u32[]{:S(2)}) collective-permute-start(bf16[16,32,384]{2,1,0:T(8,128)(2,1)S(1)} %get-tuple-element.9), channel_id=1, source_target_pairs={{0,256},{256,0},{1,257},{257,1},{2,258},{258,2},{3,259},{259,3},{4... | collective-permute-start | bytes 1179656 | tf_op jit(solution)/shard_map/ppermute | solution.py:26
  167.0 14.4 %all-to-all-start.3 = ((bf16[32,12,256]{2,1,0:T(8,128)(2,1)}), bf16[32,12,256]{2,1,0:T(8,128)(2,1)S(1)}, u32[]{:S(2)}, u32[]{:S(2)}) async-start(bf16[32,12,256]{2,1,0:T(8,128)(2,1)} %broadcast_in_dim.76), calls=%async_computation.3 | async-start | bytes 524288 | tf_op jit(solution)/shard_map/all_to_all | solution.py:20
Sparse Core Ops, SparseCore 0:
  53.1 40.1 all-gather.1

commit v2 on v1

v2 whole, which is shorter than its diff:
```python
import functools

import jax
import jax.numpy as jnp
from jax import lax
from jax.experimental import pallas as pl
from jax.experimental.pallas import tpu as pltpu
from jax.sharding import PartitionSpec as P

FIRST_DILATION = 1
SECTION_FACTOR = 8


def norm_gelu(activations, gain):
    values = activations.astype(jnp.float32)
    center = jnp.mean(values, axis=-1, keepdims=True)
    offset = values - center
    spread = jnp.mean(offset * offset, axis=-1, keepdims=True)
    normed = offset * lax.rsqrt(spread + 1e-05) * gain
    return jax.nn.gelu(normed, approximate=False).astype(jnp.bfloat16)


def copies_to(block, axes, count):
    return lax.all_to_all(
        jnp.broadcast_to(block[None], (count,) + block.shape), axes, split_axis=0, concat_axis=0, tiled=True
    )


def swap(block):
    return lax.ppermute(block, "section", [(0, 1), (1, 0)])


def columns_of(padded, wide, step):
    return jnp.concatenate([padded[:, j * step : j * step + wide] for j in range(3)], axis=2)


def erf(value):
    top = 3.832506856900711
    value = jnp.clip(value, -top, top)
    square = value * value
    over = jnp.float32(0.00022905065861350646)
    for term in (0.0034082910107109506, 0.050955695062380861, 0.18520832239976145, 1.128379143519084):
        over = over * square + term
    under = jnp.float32(-1.1791602954361697e-7)
    for term in (
        0.000023547966471313185,
        0.0010179625278914885,
        0.014070470171167667,
        0.11098505178285362,
        0.49746925110067538,
        1.0,
    ):
        under = under * square + term
    return value * over / under


def layers_kernel(
    sizes,
    stacked_hbm,
    center_ref,
    own_ref,
    other_ref,
    gain_ref,
    head_ref,
    prior_ref,
    target_ref,
    out_0_ref,
    out_1_ref,
    packed_ref,
    stacked_ref,
    weight_0,
    weight_1,
    hidden_ref,
    sem_s,
    sem_0,
    sem_1,
):
    far, half, side, band, slots, parts_y, parts_x = sizes
    tall, wide, taps = stacked_ref.shape[0] - 2, stacked_ref.shape[1], stacked_ref.shape[2]
    channels = taps // 3
    bins = head_ref.shape[1]
    section = lax.axis_index("section")

    def strip(t):
        low = 0 if t == 0 else t * band + 2
        at = pl.ds(low, t * band + band + 2 - low)
        return pltpu.make_async_copy(stacked_hbm.at[at], stacked_ref.at[at], sem_s.at[t])

    strip(0).start()

    def fetch(source, target, sems):
        for i in range(3):
            at = pl.ds(i * taps, taps)
            pltpu.make_async_copy(source.at[at], target.at[at], sems.at[i]).start()

    @pl.when(section == 0)
    def _():
        fetch(own_ref, weight_0, sem_0)

    @pl.when(section != 0)
    def _():
        fetch(other_ref, weight_0, sem_0)

    for t in range(1, tall // band):
        strip(t).start()

    @pl.when(section == 0)
    def _():
        fetch(other_ref, weight_1, sem_1)

    @pl.when(section != 0)
    def _():
        fetch(own_ref, weight_1, sem_1)

    def arrive(target, sems, i):
        at = pl.ds(i * taps, taps)
        pltpu.make_async_copy(own_ref.at[at], target.at[at], sems.at[i]).wait()

    row_start = lax.axis_index("sy") * side + section * half - far
    column_at = lax.axis_index("sx") * side - far + lax.broadcasted_iota(jnp.int32, (band, wide, 1), 1)
    column_in = (column_at >= 0) & (column_at < side * parts_x)
    gain = gain_ref[...].reshape(1, 1, channels)
    for t in range(tall // band):
        strip(t).wait()
        total = jnp.zeros((band * wide, channels), jnp.float32)
        for i in range(3):
            if t == 0:
                arrive(weight_0, sem_0, i)
            total += jnp.dot(
                stacked_ref[t * band + i : t * band + i + band].reshape(band * wide, taps),
                weight_0[i * taps : (i + 1) * taps],
                preferred_element_type=jnp.float32,
            )
        total = total.reshape(band, wide, channels) + center_ref[t * band : (t + 1) * band].astype(jnp.float32)
        values = total.astype(jnp.bfloat16).astype(jnp.float32)
        if far <= t * band < far + half:
            out_0_ref[t * band - far : (t + 1) * band - far] = values[:, far : far + side].astype(jnp.bfloat16)
        mean = jnp.mean(values, axis=-1, keepdims=True)
        offset = values - mean
        spread = jnp.mean(offset * offset, axis=-1, keepdims=True)
        row_at = row_start + t * band + lax.broadcasted_iota(jnp.int32, (band, wide, 1), 0)
        inside = column_in & (row_at >= 0) & (row_at < side * parts_y)
        normed = offset * jnp.where(inside, lax.rsqrt(spread + 1e-05), 0.0) * gain
        active = 0.5 * normed * (1.0 + erf(normed * 0.7071067811865476))
        for j in range(3):
            hidden_ref[t * band : (t + 1) * band, :, j * channels : (j + 1) * channels] = active[
                :, j * far : j * far + side
            ].astype(jnp.bfloat16)

    cells = half * side
    total = jnp.zeros((cells, channels), jnp.float32)
    for i in range(3):
        arrive(weight_1, sem_1, i)
        total += jnp.dot(
            hidden_ref[i * far : i * far + half].reshape(cells, taps),
            weight_1[i * taps : (i + 1) * taps],
            preferred_element_type=jnp.float32,
        )
    flat = (total + out_0_ref[...].reshape(cells, channels).astype(jnp.float32)).astype(jnp.bfloat16)
    out_1_ref[...] = flat.reshape(half, side, channels)
    logits = jnp.dot(flat, head_ref[...], preferred_element_type=jnp.float32)
    logits = logits + prior_ref[...].astype(jnp.float32)
    shifted = logits - jnp.max(logits, axis=1, keepdims=True)
    exp_terms = jnp.exp(shifted)
    exp_total = jnp.sum(exp_terms, axis=1, keepdims=True)
    hit = target_ref[...] == lax.broadcasted_iota(jnp.int32, (cells, bins), 1)
    picked = jnp.sum(jnp.where(hit, shifted, 0.0), axis=1, keepdims=True)
    loss = jnp.sum(jnp.log(exp_total) - picked, axis=0, keepdims=True)
    delta = (exp_terms / exp_total - hit.astype(jnp.float32)).astype(jnp.bfloat16)
    gradient = lax.dot_general(
        flat, delta, (((0,), (0,)), ((), ())), preferred_element_type=jnp.float32
    )
    loss = jnp.broadcast_to(loss, (8, 128))
    deep = channels * bins // (128 * slots)
    across = channels // deep
    for s in range(slots):
        row, lane = (s % across) * deep, (s // across) * 128
        chunk = jnp.concatenate([gradient[row : row + deep, lane : lane + 128], loss], axis=0)
        packed_ref[s] = chunk.astype(jnp.bfloat16)


def per_device(
    frames, encode_weight, conv_weight, norm_gain, head_weight, prior_logits, target_bins
):
    section = lax.axis_index("section")
    first = section == 0
    parts_y = lax.axis_size("sy")
    parts_x = lax.axis_size("sx")
    parts_b = lax.axis_size("mb")
    side = frames.shape[1] // 2
    half = side // 2
    channels = encode_weight.shape[1]
    bins = head_weight.shape[1]
    near = FIRST_DILATION
    far = FIRST_DILATION * SECTION_FACTOR
    reach = near + far

    shard = conv_weight[0, 0]
    strip = copies_to(shard, "sx", parts_x)
    gain_own = norm_gain[0, 0]
    gain_other = swap(gain_own)
    gain_0 = jnp.where(first, gain_own, gain_other)
    gain_1 = jnp.where(first, gain_other, gain_own)

    blocks = frames[0].reshape(side, 2, side, 2, frames.shape[3])
    kernel = encode_weight.reshape(2, 2, frames.shape[3], channels)
    encoded = jnp.einsum(
        "apbqc,pqco->abo", blocks, kernel, preferred_element_type=jnp.float32
    ).astype(jnp.bfloat16)

    strip, encoded = lax.optimization_barrier((strip, encoded))
    weight_own = lax.all_gather(
        strip.reshape(parts_x * shard.shape[0], channels), "sy", axis=0, tiled=True
    )

    outgoing = jnp.where(first, encoded[side - reach :], encoded[:reach])
    route = [(y, y + 1) for y in range(parts_y - 1)] + [
        (parts_y + y + 1, parts_y + y) for y in range(parts_y - 1)
    ]
    arrived = lax.ppermute(outgoing, ("section", "sy"), route)
    rows = jnp.where(
        first,
        jnp.concatenate([arrived, encoded[: half + reach]], axis=0),
        jnp.concatenate([encoded[half - reach :], arrived], axis=0),
    )
    forward = [(x, x + 1) for x in range(parts_x - 1)]
    backward = [(x + 1, x) for x in range(parts_x - 1)]
    left = lax.ppermute(rows[:, side - reach :], "sx", forward)
    right = lax.ppermute(rows[:, :reach], "sx", backward)
    haloed = jnp.concatenate([left, rows, right], axis=1)

    tall, wide = half + 2 * far, side + 2 * far
    cells = half * side
    stacked = columns_of(norm_gelu(haloed, gain_0), wide, near)
    center = haloed[near : near + tall, near : near + wide]
    prior = lax.dynamic_slice_in_dim(prior_logits[0], section * half, half, axis=0).reshape(cells, bins)
    target = lax.dynamic_slice_in_dim(target_bins[0], section * half, half, axis=0).reshape(cells, 1)
    weight_own, stacked, center, prior, target = lax.optimization_barrier(
        (weight_own, stacked, center, prior, target)
    )
    weight_other = swap(weight_own)
    slots = parts_x * parts_b
    deep = channels * bins // (128 * slots)
    vmem = pl.BlockSpec(memory_space=pltpu.VMEM)
    anywhere = pl.BlockSpec(memory_space=pl.ANY)
    taps = 3 * channels
    own_0, own_1, packed = pl.pallas_call(
        functools.partial(layers_kernel, (far, half, side, 8, slots, parts_y, parts_x)),
        out_shape=(
            jax.ShapeDtypeStruct((half, side, channels), jnp.bfloat16),
            jax.ShapeDtypeStruct((half, side, channels), jnp.bfloat16),
            jax.ShapeDtypeStruct((slots, deep + 8, 128), jnp.bfloat16),
        ),
        in_specs=[anywhere, vmem, anywhere, anywhere, vmem, vmem, vmem, vmem],
        out_specs=(vmem, vmem, vmem),
        scratch_shapes=[
            pltpu.VMEM((tall + 2 * near, wide, taps), jnp.bfloat16),
            pltpu.VMEM((3 * taps, channels), jnp.bfloat16),
            pltpu.VMEM((3 * taps, channels), jnp.bfloat16),
            pltpu.VMEM((tall, side, taps), jnp.bfloat16),
            pltpu.SemaphoreType.DMA((tall // 8,)),
            pltpu.SemaphoreType.DMA((3,)),
            pltpu.SemaphoreType.DMA((3,)),
        ],
        compiler_params=pltpu.CompilerParams(vmem_limit_bytes=52 * 2**20),
        cost_estimate=pl.CostEstimate(
            flops=2 * (tall * wide + cells) * 3 * taps * channels,
            bytes_accessed=6 * taps * channels * 2,
            transcendentals=0,
        ),
    )(stacked, center, weight_own, weight_other, gain_1.reshape(1, channels), head_weight, prior, target)

    packed = lax.all_to_all(packed, ("sx", "mb"), split_axis=0, concat_axis=0, tiled=True)
    partial = jnp.sum(packed.astype(jnp.float32), axis=0).astype(jnp.bfloat16)
    packed = copies_to(partial, ("section", "sy"), 2 * parts_y)
    partial = jnp.sum(packed.astype(jnp.float32), axis=0)
    loss_all = partial[deep, 0]
    gathered = copies_to(partial[:deep].astype(jnp.bfloat16), ("sx", "mb"), slots)
    scale = lax.rsqrt(jnp.mean(jnp.square(gathered.astype(jnp.float32))) + 1e-06)
    halves = bins // 128
    by_half = gathered.reshape(halves, channels, 128)
    own_rows = lax.dynamic_slice_in_dim(by_half, section * (channels // 2), channels // 2, axis=1)
    head_step = jnp.concatenate(
        [own_rows[h].astype(jnp.float32) * scale for h in range(halves)], axis=1
    )
    mean_loss = loss_all / (parts_b * parts_y * parts_x * side * side)

    sent = swap(jnp.where(first, own_1, own_0))
    grids = jnp.where(
        first, jnp.concatenate([own_0, sent], axis=0), jnp.concatenate([sent, own_1], axis=0)
    )[None, None]
    return (grids, head_step, mean_loss)


def solution(mesh):
    placed = (
        P("mb", "sy", "sx", None),
        P(),
        P("section", None, ("sy", "sx"), None),
        P("section", None, None),
        P(),
        P("mb", "sy", "sx", None),
        P("mb", "sy", "sx"),
    )
    return jax.shard_map(
        per_device,
        mesh=mesh,
        in_specs=placed,
        out_specs=(P("section", "mb", "sy", "sx", None), P("section", None), P()),
        check_vma=False,
    )
```

time: 195 us -> 163 us (0.84)
  Pallas kernels: 0 us -> 16.9 us
  local copies, waits for them, and re-layouts: 21 us -> 8.03 us
  matrix products: 14.3 us -> 2.01 us
  waiting for transfers between devices: 54 us -> 46.3 us
  other arithmetic: 20.7 us -> 13.8 us
  starting transfers between devices: 41.2 us -> 35.9 us
  between operations: 20.3 us -> 16.7 us
    pallas_call x0 -> x1, Pallas kernels: none -> 16.9 us  [per_device(): pl.pallas_call(functools.partial(layers_kernel, (far, half, side, 8, slot...]
    unnamed x30 -> x6, local copies, waits for them, and re-layouts: 14.2 us -> 0.02 us
    dot_general x4 -> x0, matrix products: 12.2 us -> none  [the longest x1 9.26 us: per_device(): summed = jnp.dot(patches, weight_0, preferred_element_type=jnp.float32)]
    all_gather x1, waiting for transfers between devices: 20.3 us -> 8.65 us  [per_device(): lax.all_gather(strip.reshape(parts_x * shard.shape[0], channels), 'sy', a...]
    select_n x3 -> x1, other arithmetic: 6.26 us -> 0.05 us  [per_device(): sent = swap(jnp.where(first, own_1, own_0))]
    ppermute x1, waiting for transfers between devices: 0.01 us -> 4.43 us  [per_device(): left = lax.ppermute(rows[:, side - reach:], 'sx', forward)]
    all_to_all x3, waiting for transfers between devices: 23.5 us -> 19.7 us  [copies_to(): lax.all_to_all(jnp.broadcast_to(block[None], (count,) + block.shape), axe...]
    ppermute x1, waiting for transfers between devices: 0.01 us -> 3.65 us  [per_device(): right = lax.ppermute(rows[:, :reach], 'sx', backward)]
  transfers between devices with their start and end apart: 10 -> 10, of which waited for: 6 -> 8; matrix products, arithmetic and copies ran while one was open for 14% -> 12% of each run, Pallas kernels for 0% -> 0%
where the time goes in v2:
time: 163 us; the launch traced here: 161 us
  waiting for transfers between devices  46.3 us (28%)
  starting transfers between devices  35.9 us (22%)
  blocking collectives  21.1 us (13%)
  Pallas kernels  16.9 us (10%)
  between operations  16.7 us (10%)
  other arithmetic  13.8 us (8%)
  local copies, waits for them, and re-layouts  8.03 us (5%)
  matrix products  2.01 us (1%)
    all_to_all x3, starting transfers between devices, copies_to(): lax.all_to_all(jnp.broadcast_to(block[None], (count,) + block.shape), axe...  21.6 us
    all_to_all x1, blocking collectives, per_device(): lax.all_to_all(packed, ('sx', 'mb'), split_axis=0, concat_axis=0, tiled=T...  21.1 us
    all_to_all x3, waiting for transfers between devices, copies_to(): lax.all_to_all(jnp.broadcast_to(block[None], (count,) + block.shape), axe...  19.7 us
    pallas_call x1, Pallas kernels, per_device(): pl.pallas_call(functools.partial(layers_kernel, (far, half, side, 8, slot...  16.9 us
    ppermute x3, starting transfers between devices, swap(): return lax.ppermute(block, 'section', [(0, 1), (1, 0)])  10.4 us
    all_gather x1, waiting for transfers between devices, per_device(): lax.all_gather(strip.reshape(parts_x * shard.shape[0], channels), 'sy', a...  8.65 us
    convert_element_type x1, other arithmetic, norm_gelu(): return jax.nn.gelu(normed, approximate=False).astype(jnp.bfloat16)  6.79 us
    ppermute x1, waiting for transfers between devices, per_device(): arrived = lax.ppermute(outgoing, ('section', 'sy'), route)  5.26 us
  transfers between devices with their start and end apart: 10, of which 8 were waited for; matrix products, arithmetic and copies ran while one was open for 12% of the time, Pallas kernels for 0%

profile of v2, /device:TPU:1, one launch (start us, length us, event | category | flops | bytes accessed | tf_op | source)
XLA Modules:
  0.0 160.8 jit_solution(14939622578615922568)
XLA Ops:
  7.2 1.6 broadcast_in_dim.9
  8.8 10.9 %all-to-all-start = ((bf16[8,54,384]{2,1,0:T(8,128)(2,1)}), bf16[8,54,384]{2,1,0:T(8,128)(2,1)S(1)}, u32[]{:S(2)}, u32[]{:S(2)}) async-start(bf16[8,54,384]{2,1,0:T(8,128)(2,1)} %broadcast_in_dim.9), calls=%async_computation | async-start | bytes 688128 | tf_op jit(solution)/shard_map/all_to_all | solution.py:24
  19.7 0.7 reduce.1
  20.4 2.9 %collective-permute-start.3 = (f32[384]{0:T(512)S(1)}, f32[384]{0:T(512)S(1)}, u32[]{:S(2)}, u32[]{:S(2)}) collective-permute-start(f32[384]{0:T(512)S(1)} %reduce.1), channel_id=1, source_target_pairs={{0,256},{256,0},{1,257},{257,1},{2,258},{258,2},{3,259},{259,3},{4... | collective-permute-start | bytes 4616 | tf_op jit(solution)/shard_map/ppermute | solution.py:30
  23.3 2.0 %bitcast_convert_fusion = bf16[32,32,384]{2,1,0:T(8,128)(2,1)S(1)} fusion(bf16[2,2,128,384,1]{3,2,1,0,4:T(8,128)(2,1)} %bitcast.27, bf16[32,2,32,2,128]{4,3,2,1,0:T(2,128)(2,1)} %bitcast.26), kind=kOutput, calls=%fused_computation.30 | convolution fusion | flops 403046400 | bytes 2228224 | tf_op jit(solution)/shard_map/apbqc,pqco->abo/dot_general | solution.py:207
  25.3 6.7 %all-to-all-done = bf16[8,54,384]{2,1,0:T(8,128)(2,1)S(1)} async-done(((bf16[8,54,384]{2,1,0:T(8,128)(2,1)}), bf16[8,54,384]{2,1,0:T(8,128)(2,1)S(1)}, u32[]{:S(2)}, u32[]{:S(2)}) %all-to-all-start) | async-done | bytes 331808 | tf_op jit(solution)/shard_map/all_to_all | solution.py:24
  32.0 0.8 reshape.108
  32.9 1.3 collective-permute-start
  34.3 5.3 %collective-permute-done = bf16[9,32,384]{2,1,0:T(8,128)(2,1)S(1)} collective-permute-done((bf16[9,32,384]{2,1,0:T(8,128)(2,1)S(1)}, bf16[9,32,384]{2,1,0:T(8,128)(2,1)S(1)}, u32[]{:S(2)}, u32[]{:S(2)}) %collective-permute-start) | collective-permute-done | bytes 221216 | tf_op jit(solution)/shard_map/ppermute | solution.py:220
  39.8 0.9 fusion.22
  40.7 1.3 collective-permute-start.1
  42.0 1.3 collective-permute-start.2
  43.4 4.4 %collective-permute-done.1 = bf16[34,9,384]{2,1,0:T(8,128)(2,1)S(1)} collective-permute-done((bf16[34,9,384]{2,1,0:T(8,128)(2,1)}, bf16[34,9,384]{2,1,0:T(8,128)(2,1)S(1)}, u32[]{:S(2)}, u32[]{:S(2)}) %collective-permute-start.1) | collective-permute-done | bytes 235040 | tf_op jit(solution)/shard_map/ppermute | solution.py:228
  47.8 3.6 %collective-permute-done.2 = bf16[34,9,384]{2,1,0:T(8,128)(2,1)S(1)} collective-permute-done((bf16[34,9,384]{2,1,0:T(8,128)(2,1)S(1)}, bf16[34,9,384]{2,1,0:T(8,128)(2,1)S(1)}, u32[]{:S(2)}, u32[]{:S(2)}) %collective-permute-start.2) | collective-permute-done | bytes 235040 | tf_op jit(solution)/shard_map/ppermute | solution.py:229
  52.1 1.5 slice.62.center_ref
  53.6 0.8 fusion.2
  54.5 6.8 %fusion.7 = bf16[34,50,384]{2,1,0:T(8,128)(2,1)S(1)} fusion(bf16[34,50,384]{2,1,0:T(8,128)(2,1)S(1)} %get-tuple-element.24, f32[384]{0:T(512)S(1)} %get-tuple-element.35, f32[34,50]{1,0:T(8,128)S(1)} %add_rsqrt_fusion, f32[34,50]{1,0:T(8,128)S(1)} %broadcast_multiply_fusion), kind=kLoop, calls=%fused_computation.11 | loop fusion | flops 45043200 | bytes 2626336 | tf_op jit(solution)/shard_map/convert_element_type | solution.py:20
  61.3 0.9 fusion.21
  62.2 2.0 %pad_maximum_fusion.stacked_hbm = bf16[34,48,1152]{2,1,0:T(8,128)(2,1)} fusion(bf16[34,48,384]{2,1,0:T(8,128)(2,1)S(1)} %get-tuple-element.26, bf16[34,48,384]{2,1,0:T(8,128)(2,1)S(1)} %get-tuple-element.27, bf16[34,48,384]{2,1,0:T(8,128)(2,1)S(1)} %get-tuple-element.25), kind=kLoop, calls=%fused_computation.1 | loop fusion | flops 11280384 | bytes 7520256 | tf_op jit(solution)/shard_map/concatenate | solution.py:34
  64.2 8.7 %all-gather.2.cloned.1.call-done.own_ref = bf16[3456,384]{1,0:T(8,128)(2,1)} async-done(((bf16[432,384]{1,0:T(8,128)(2,1)}), bf16[3456,384]{1,0:T(8,128)(2,1)}) %all-gather.2.cloned.1.call-update) | async-done | bytes 2654224 | tf_op jit(solution)/shard_map/all_gather | solution.py:212
  72.9 5.6 %collective-permute-start.4 = (bf16[3456,384]{1,0:T(8,128)(2,1)}, bf16[3456,384]{1,0:T(8,128)(2,1)}, u32[]{:S(2)}, u32[]{:S(2)}) collective-permute-start(bf16[3456,384]{1,0:T(8,128)(2,1)} %all-gather.2.cloned.1.call-done.own_ref), channel_id=1, source_target_pairs={{0,256},{256,0},{1,257},{257,1},{2,258},{258,2},{3,259},{259,3},{4... | collective-permute-start | bytes 7962632 | tf_op jit(solution)/shard_map/ppermute | solution.py:30
  78.6 4.6 %collective-permute-done.4.other_ref = bf16[3456,384]{1,0:T(8,128)(2,1)} collective-permute-done((bf16[3456,384]{1,0:T(8,128)(2,1)}, bf16[3456,384]{1,0:T(8,128)(2,1)}, u32[]{:S(2)}, u32[]{:S(2)}) %collective-permute-start.4) | collective-permute-done | bytes 2654240 | tf_op jit(solution)/shard_map/ppermute | solution.py:30
  83.2 16.9 %shard_map.94 = (bf16[16,32,384]{2,1,0:T(8,128)(2,1)S(1)}, bf16[16,32,384]{2,1,0:T(8,128)(2,1)S(1)}, bf16[32,32,128]{2,1,0:T(8,128)(2,1)S(1)}) custom-call(bf16[34,48,1152]{2,1,0:T(8,128)(2,1)} %pad_maximum_fusion.stacked_hbm, bf16[32,48,384]{2,1,0:T(8,128)(2,1)} %slice.62.center_ref, bf16[3456,384]{1,0:T(8,128)(2,1)} %all-gather.2.cloned.1.call-done.own_ref, ...), custom_call_target="tpu_custom_call" | custom-call | flops 5435817984 | bytes 5308416 | tf_op jit(solution)/shard_map/pallas_call | solution.py:247
  100.1 21.1 %all_to_all.20 = bf16[32,32,128]{2,1,0:T(8,128)(2,1)S(1)} all-to-all(bf16[32,32,128]{2,1,0:T(8,128)(2,1)S(1)} %get-tuple-element.22), channel_id=1, replica_groups=mesh['section'=2,'sy'=8,'sx'=8,'mb'=4] {'sx','mb'}, dimensions={0} | all-to-all | bytes 524288 | tf_op jit(solution)/shard_map/all_to_all | solution.py:273
  121.9 6.9 %all-to-all-start.2 = ((bf16[16,32,128]{2,1,0:T(8,128)(2,1)}), bf16[16,32,128]{2,1,0:T(8,128)(2,1)S(1)}, u32[]{:S(2)}, u32[]{:S(2)}) async-start(bf16[16,32,128]{2,1,0:T(8,128)(2,1)} %broadcast_in_dim.10), calls=%async_computation.2 | async-start | bytes 262144 | tf_op jit(solution)/shard_map/all_to_all | solution.py:24
  128.8 2.0 %collective-permute-start.5 = (bf16[16,32,384]{2,1,0:T(8,128)(2,1)S(1)}, bf16[16,32,384]{2,1,0:T(8,128)(2,1)S(1)}, u32[]{:S(2)}, u32[]{:S(2)}) collective-permute-start(bf16[16,32,384]{2,1,0:T(8,128)(2,1)S(1)} %broadcast_select_fusion), channel_id=1, source_target_pairs={{0,256},{256,0},{1,257},{257,1},{2,258},{258,2},{3,259},{259,3},{4... | collective-permute-start | bytes 1179656 | tf_op jit(solution)/shard_map/ppermute | solution.py:30
  130.9 5.2 %all-to-all-done.2 = bf16[16,32,128]{2,1,0:T(8,128)(2,1)S(1)} async-done(((bf16[16,32,128]{2,1,0:T(8,128)(2,1)}), bf16[16,32,128]{2,1,0:T(8,128)(2,1)S(1)}, u32[]{:S(2)}, u32[]{:S(2)}) %all-to-all-start.2) | async-done | bytes 131104 | tf_op jit(solution)/shard_map/all_to_all | solution.py:24
  136.1 0.7 broadcast_in_dim.11
  136.8 3.9 %all-to-all-start.3 = ((bf16[32,24,128]{2,1,0:T(8,128)(2,1)}), bf16[32,24,128]{2,1,0:T(8,128)(2,1)S(1)}, u32[]{:S(2)}, u32[]{:S(2)}) async-start(bf16[32,24,128]{2,1,0:T(8,128)(2,1)} %broadcast_in_dim.11), calls=%async_computation.3 | async-start | bytes 393216 | tf_op jit(solution)/shard_map/all_to_all | solution.py:24
  140.7 1.0 maximum_select_fusion.1
  142.9 7.8 %all-to-all-done.3 = bf16[32,24,128]{2,1,0:T(8,128)(2,1)S(1)} async-done(((bf16[32,24,128]{2,1,0:T(8,128)(2,1)}), bf16[32,24,128]{2,1,0:T(8,128)(2,1)S(1)}, u32[]{:S(2)}, u32[]{:S(2)}) %all-to-all-start.3) | async-done | bytes 196640 | tf_op jit(solution)/shard_map/all_to_all | solution.py:24
  150.7 0.7 multiply_reduce_fusion
  (30 shorter events, 3.3 us)
Async XLA Ops:
  7.2 16.1 %copy-start = (bf16[1,32,32,256]{3,2,1,0:T(8,128)(2,1)S(1)}, bf16[1,32,32,256]{3,2,1,0:T(8,128)(2,1)}, u32[]{:S(2)}) copy-start(bf16[1,32,32,256]{3,2,1,0:T(8,128)(2,1)} %param.12) | copy-start | bytes 1572868
  8.8 23.2 %all-to-all-start = ((bf16[8,54,384]{2,1,0:T(8,128)(2,1)}), bf16[8,54,384]{2,1,0:T(8,128)(2,1)S(1)}, u32[]{:S(2)}, u32[]{:S(2)}) async-start(bf16[8,54,384]{2,1,0:T(8,128)(2,1)} %broadcast_in_dim.9), calls=%async_computation | async-start | bytes 688128 | tf_op jit(solution)/shard_map/all_to_all | solution.py:24
  19.6 53.2 %all-gather.2.cloned.1.call-start = ((), (), s32[]{:S(2)}) async-start(), calls=%async_computation.4 | async-start | bytes 2985984 | tf_op jit(solution)/shard_map/all_gather | solution.py:212
  20.4 23.0 %collective-permute-start.3 = (f32[384]{0:T(512)S(1)}, f32[384]{0:T(512)S(1)}, u32[]{:S(2)}, u32[]{:S(2)}) collective-permute-start(f32[384]{0:T(512)S(1)} %reduce.1), channel_id=1, source_target_pairs={{0,256},{256,0},{1,257},{257,1},{2,258},{258,2},{3,259},{259,3},{4... | collective-permute-start | bytes 4616 | tf_op jit(solution)/shard_map/ppermute | solution.py:30
  32.9 10.4 %copy-start.2 = (s32[1,32,32]{2,1,0:T(8,128)S(1)}, s32[1,32,32]{2,1,0:T(8,128)}, u32[]{:S(2)}) copy-start(s32[1,32,32]{2,1,0:T(8,128)} %param.13) | copy-start | bytes 12292
  32.9 6.7 %collective-permute-start = (bf16[9,32,384]{2,1,0:T(8,128)(2,1)S(1)}, bf16[9,32,384]{2,1,0:T(8,128)(2,1)S(1)}, u32[]{:S(2)}, u32[]{:S(2)}) collective-permute-start(bf16[9,32,384]{2,1,0:T(8,128)(2,1)S(1)} %slice_select_fusion), channel_id=1, source_target_pairs={{0,32},{32,64},{64,96},{96,128},{128,160},{160,192},{192,224},{288... | collective-permute-start | bytes 663560 | tf_op jit(solution)/shard_map/ppermute | solution.py:220
  40.7 7.2 %collective-permute-start.1 = (bf16[34,9,384]{2,1,0:T(8,128)(2,1)}, bf16[34,9,384]{2,1,0:T(8,128)(2,1)S(1)}, u32[]{:S(2)}, u32[]{:S(2)}) collective-permute-start(bf16[34,9,384]{2,1,0:T(8,128)(2,1)} %get-tuple-element.28), channel_id=1, source_target_pairs={{0,4},{4,8},{8,12},{12,16},{16,20},{20,24},{24,28},{1,5},{5,9},{9,... | collective-permute-start | bytes 705032 | tf_op jit(solution)/shard_map/ppermute | solution.py:228
  42.0 9.5 %collective-permute-start.2 = (bf16[34,9,384]{2,1,0:T(8,128)(2,1)S(1)}, bf16[34,9,384]{2,1,0:T(8,128)(2,1)S(1)}, u32[]{:S(2)}, u32[]{:S(2)}) collective-permute-start(bf16[34,9,384]{2,1,0:T(8,128)(2,1)S(1)} %get-tuple-element.29), channel_id=1, source_target_pairs={{4,0},{8,4},{12,8},{16,12},{20,16},{24,20},{28,24},{5,1},{9,5},{13... | collective-permute-start | bytes 705032 | tf_op jit(solution)/shard_map/ppermute | solution.py:229
  62.2 21.0 %copy-start.1 = (bf16[384,256]{1,0:T(8,128)(2,1)S(1)}, bf16[384,256]{1,0:T(8,128)(2,1)}, u32[]{:S(2)}) copy-start(bf16[384,256]{1,0:T(8,128)(2,1)} %head_ref.1) | copy-start | bytes 589828
  72.9 10.3 %collective-permute-start.4 = (bf16[3456,384]{1,0:T(8,128)(2,1)}, bf16[3456,384]{1,0:T(8,128)(2,1)}, u32[]{:S(2)}, u32[]{:S(2)}) collective-permute-start(bf16[3456,384]{1,0:T(8,128)(2,1)} %all-gather.2.cloned.1.call-done.own_ref), channel_id=1, source_target_pairs={{0,256},{256,0},{1,257},{257,1},{2,258},{258,2},{3,259},{259,3},{4... | collective-permute-start | bytes 7962632 | tf_op jit(solution)/shard_map/ppermute | solution.py:30
  121.9 14.2 %all-to-all-start.2 = ((bf16[16,32,128]{2,1,0:T(8,128)(2,1)}), bf16[16,32,128]{2,1,0:T(8,128)(2,1)S(1)}, u32[]{:S(2)}, u32[]{:S(2)}) async-start(bf16[16,32,128]{2,1,0:T(8,128)(2,1)} %broadcast_in_dim.10), calls=%async_computation.2 | async-start | bytes 262144 | tf_op jit(solution)/shard_map/all_to_all | solution.py:24
  128.8 11.9 %collective-permute-start.5 = (bf16[16,32,384]{2,1,0:T(8,128)(2,1)S(1)}, bf16[16,32,384]{2,1,0:T(8,128)(2,1)S(1)}, u32[]{:S(2)}, u32[]{:S(2)}) collective-permute-start(bf16[16,32,384]{2,1,0:T(8,128)(2,1)S(1)} %broadcast_select_fusion), channel_id=1, source_target_pairs={{0,256},{256,0},{1,257},{257,1},{2,258},{258,2},{3,259},{259,3},{4... | collective-permute-start | bytes 1179656 | tf_op jit(solution)/shard_map/ppermute | solution.py:30
  136.8 13.8 %all-to-all-start.3 = ((bf16[32,24,128]{2,1,0:T(8,128)(2,1)}), bf16[32,24,128]{2,1,0:T(8,128)(2,1)S(1)}, u32[]{:S(2)}, u32[]{:S(2)}) async-start(bf16[32,24,128]{2,1,0:T(8,128)(2,1)} %broadcast_in_dim.11), calls=%async_computation.3 | async-start | bytes 393216 | tf_op jit(solution)/shard_map/all_to_all | solution.py:24
Sparse Core Ops, SparseCore 0:
  33.0 39.8 all-gather.1

commit v3 on v2

--- a/solution.py
+++ b/solution.py
@@ -58,8 +58,7 @@
     sizes,
     stacked_hbm,
     center_ref,
-    own_ref,
-    other_ref,
+    weights_ref,
     gain_ref,
     head_ref,
     prior_ref,
@@ -72,8 +71,7 @@
     weight_1,
     hidden_ref,
     sem_s,
-    sem_0,
-    sem_1,
+    sem_w,
 ):
     far, half, side, band, slots, parts_y, parts_x = sizes
     tall, wide, taps = stacked_ref.shape[0] - 2, stacked_ref.shape[1], stacked_ref.shape[2]
@@ -88,33 +86,14 @@
 
     strip(0).start()
 
-    def fetch(source, target, sems):
-        for i in range(3):
-            at = pl.ds(i * taps, taps)
-            pltpu.make_async_copy(source.at[at], target.at[at], sems.at[i]).start()
-
-    @pl.when(section == 0)
-    def _():
-        fetch(own_ref, weight_0, sem_0)
-
-    @pl.when(section != 0)
-    def _():
-        fetch(other_ref, weight_0, sem_0)
-
+    def weights(layer, target, sem):
+        return pltpu.make_async_copy(weights_ref.at[pl.ds(layer * 3 * taps, 3 * taps)], target, sem)
+
+    fetch_0, fetch_1 = weights(0, weight_0, sem_w.at[0]), weights(1, weight_1, sem_w.at[1])
+    fetch_0.start()
     for t in range(1, tall // band):
         strip(t).start()
-
-    @pl.when(section == 0)
-    def _():
-        fetch(other_ref, weight_1, sem_1)
-
-    @pl.when(section != 0)
-    def _():
-        fetch(own_ref, weight_1, sem_1)
-
-    def arrive(target, sems, i):
-        at = pl.ds(i * taps, taps)
-        pltpu.make_async_copy(own_ref.at[at], target.at[at], sems.at[i]).wait()
+    fetch_1.start()
 
     row_start = lax.axis_index("sy") * side + section * half - far
     column_at = lax.axis_index("sx") * side - far + lax.broadcasted_iota(jnp.int32, (band, wide, 1), 1)
@@ -122,15 +101,15 @@
     gain = gain_ref[...].reshape(1, 1, channels)
     for t in range(tall // band):
         strip(t).wait()
-        total = jnp.zeros((band * wide, channels), jnp.float32)
-        for i in range(3):
-            if t == 0:
-                arrive(weight_0, sem_0, i)
-            total += jnp.dot(
-                stacked_ref[t * band + i : t * band + i + band].reshape(band * wide, taps),
-                weight_0[i * taps : (i + 1) * taps],
-                preferred_element_type=jnp.float32,
-            )
+        if t == 0:
+            fetch_0.wait()
+        total = jnp.dot(
+            jnp.concatenate(
+                [stacked_ref[t * band + i : t * band + i + band] for i in range(3)], axis=2
+            ).reshape(band * wide, 3 * taps),
+            weight_0[...],
+            preferred_element_type=jnp.float32,
+        )
         total = total.reshape(band, wide, channels) + center_ref[t * band : (t + 1) * band].astype(jnp.float32)
         values = total.astype(jnp.bfloat16).astype(jnp.float32)
         if far <= t * band < far + half:
@@ -148,14 +127,12 @@
             ].astype(jnp.bfloat16)
 
     cells = half * side
-    total = jnp.zeros((cells, channels), jnp.float32)
-    for i in range(3):
-        arrive(weight_1, sem_1, i)
-        total += jnp.dot(
-            hidden_ref[i * far : i * far + half].reshape(cells, taps),
-            weight_1[i * taps : (i + 1) * taps],
-            preferred_element_type=jnp.float32,
-        )
+    fetch_1.wait()
+    total = jnp.dot(
+        jnp.concatenate([hidden_ref[i * far : i * far + half] for i in range(3)], axis=2).reshape(cells, 3 * taps),
+        weight_1[...],
+        preferred_element_type=jnp.float32,
+    )
     flat = (total + out_0_ref[...].reshape(cells, channels).astype(jnp.float32)).astype(jnp.bfloat16)
     out_1_ref[...] = flat.reshape(half, side, channels)
     logits = jnp.dot(flat, head_ref[...], preferred_element_type=jnp.float32)
@@ -197,7 +174,10 @@
 
     shard = conv_weight[0, 0]
     strip = copies_to(shard, "sx", parts_x)
-    gain_own = norm_gain[0, 0]
+    strip, encode_weight, gain_own = lax.optimization_barrier((strip, encode_weight, norm_gain[0, 0]))
+    weights = lax.all_gather(
+        strip.reshape(parts_x * shard.shape[0], channels), ("section", "sy"), axis=0, tiled=True
+    )
     gain_other = swap(gain_own)
     gain_0 = jnp.where(first, gain_own, gain_other)
     gain_1 = jnp.where(first, gain_other, gain_own)
@@ -207,11 +187,6 @@
     encoded = jnp.einsum(
         "apbqc,pqco->abo", blocks, kernel, preferred_element_type=jnp.float32
     ).astype(jnp.bfloat16)
-
-    strip, encoded = lax.optimization_barrier((strip, encoded))
-    weight_own = lax.all_gather(
-        strip.reshape(parts_x * shard.shape[0], channels), "sy", axis=0, tiled=True
-    )
 
     outgoing = jnp.where(first, encoded[side - reach :], encoded[:reach])
     route = [(y, y + 1) for y in range(parts_y - 1)] + [
@@ -235,10 +210,6 @@
     center = haloed[near : near + tall, near : near + wide]
     prior = lax.dynamic_slice_in_dim(prior_logits[0], section * half, half, axis=0).reshape(cells, bins)
     target = lax.dynamic_slice_in_dim(target_bins[0], section * half, half, axis=0).reshape(cells, 1)
-    weight_own, stacked, center, prior, target = lax.optimization_barrier(
-        (weight_own, stacked, center, prior, target)
-    )
-    weight_other = swap(weight_own)
     slots = parts_x * parts_b
     deep = channels * bins // (128 * slots)
     vmem = pl.BlockSpec(memory_space=pltpu.VMEM)
@@ -251,7 +222,7 @@
             jax.ShapeDtypeStruct((half, side, channels), jnp.bfloat16),
             jax.ShapeDtypeStruct((slots, deep + 8, 128), jnp.bfloat16),
         ),
-        in_specs=[anywhere, vmem, anywhere, anywhere, vmem, vmem, vmem, vmem],
+        in_specs=[anywhere, vmem, anywhere, vmem, vmem, vmem, vmem],
         out_specs=(vmem, vmem, vmem),
         scratch_shapes=[
             pltpu.VMEM((tall + 2 * near, wide, taps), jnp.bfloat16),
@@ -259,8 +230,7 @@
             pltpu.VMEM((3 * taps, channels), jnp.bfloat16),
             pltpu.VMEM((tall, side, taps), jnp.bfloat16),
             pltpu.SemaphoreType.DMA((tall // 8,)),
-            pltpu.SemaphoreType.DMA((3,)),
-            pltpu.SemaphoreType.DMA((3,)),
+            pltpu.SemaphoreType.DMA((2,)),
         ],
         compiler_params=pltpu.CompilerParams(vmem_limit_bytes=52 * 2**20),
         cost_estimate=pl.CostEstimate(
@@ -268,7 +238,7 @@
             bytes_accessed=6 * taps * channels * 2,
             transcendentals=0,
         ),
-    )(stacked, center, weight_own, weight_other, gain_1.reshape(1, channels), head_weight, prior, target)
+    )(stacked, center, weights, gain_1.reshape(1, channels), head_weight, prior, target)
 
     packed = lax.all_to_all(packed, ("sx", "mb"), split_axis=0, concat_axis=0, tiled=True)
     partial = jnp.sum(packed.astype(jnp.float32), axis=0).astype(jnp.bfloat16)

time: 163 us -> 156 us (0.957)
  waiting for transfers between devices: 46.3 us -> 40 us
    ppermute x1, waiting for transfers between devices: 5.26 us -> 0.01 us  [per_device(): arrived = lax.ppermute(outgoing, ('section', 'sy'), route)]
    all_to_all x3, waiting for transfers between devices: 19.7 us -> 24.7 us  [copies_to(): lax.all_to_all(jnp.broadcast_to(block[None], (count,) + block.shape), axe...]
    ppermute x3 -> x2, waiting for transfers between devices: 4.56 us -> 0.01 us  [swap(): return lax.ppermute(block, 'section', [(0, 1), (1, 0)])]
    all_gather x1, waiting for transfers between devices: 8.65 us -> 5.26 us  [per_device(): lax.all_gather(strip.reshape(parts_x * shard.shape[0], channels), ('secti...]
    ppermute x3 -> x2, starting transfers between devices: 10.4 us -> 8.34 us  [swap(): return lax.ppermute(block, 'section', [(0, 1), (1, 0)])]
    ppermute x1, waiting for transfers between devices: 4.43 us -> 6.21 us  [per_device(): left = lax.ppermute(rows[:, side - reach:], 'sx', forward)]
  transfers between devices with their start and end apart: 10 -> 9, of which waited for: 8 -> 6; matrix products, arithmetic and copies ran while one was open for 12% -> 14% of each run, Pallas kernels for 0% -> 0%
where the time goes in v3:
time: 156 us; the launch traced here: 154 us
  waiting for transfers between devices  40 us (26%)
  starting transfers between devices  34.7 us (22%)
  blocking collectives  20.9 us (13%)
  between operations  16.7 us (11%)
  Pallas kernels  15.9 us (10%)
  other arithmetic  14.8 us (9%)
  local copies, waits for them, and re-layouts  9.14 us (6%)
  matrix products  1.7 us (1%)
    all_to_all x3, waiting for transfers between devices, copies_to(): lax.all_to_all(jnp.broadcast_to(block[None], (count,) + block.shape), axe...  24.7 us
    all_to_all x3, starting transfers between devices, copies_to(): lax.all_to_all(jnp.broadcast_to(block[None], (count,) + block.shape), axe...  21.5 us
    all_to_all x1, blocking collectives, per_device(): lax.all_to_all(packed, ('sx', 'mb'), split_axis=0, concat_axis=0, tiled=T...  20.9 us
    pallas_call x1, Pallas kernels, per_device(): pl.pallas_call(functools.partial(layers_kernel, (far, half, side, 8, slot...  15.9 us
    ppermute x2, starting transfers between devices, swap(): return lax.ppermute(block, 'section', [(0, 1), (1, 0)])  8.34 us
    convert_element_type x1, other arithmetic, norm_gelu(): return jax.nn.gelu(normed, approximate=False).astype(jnp.bfloat16)  6.8 us
    ppermute x1, waiting for transfers between devices, per_device(): left = lax.ppermute(rows[:, side - reach:], 'sx', forward)  6.21 us
    all_gather x1, waiting for transfers between devices, per_device(): lax.all_gather(strip.reshape(parts_x * shard.shape[0], channels), ('secti...  5.26 us
  transfers between devices with their start and end apart: 9, of which 6 were waited for; matrix products, arithmetic and copies ran while one was open for 14% of the time, Pallas kernels for 0%

profile of v3, /device:TPU:1, one launch (start us, length us, event | category | flops | bytes accessed | tf_op | source)
XLA Modules:
  0.0 154.0 jit_solution(13779781143357117603)
XLA Ops:
  7.2 1.6 %broadcast_in_dim.9 = bf16[8,54,384]{2,1,0:T(8,128)(2,1)} broadcast(bf16[54,384]{1,0:T(8,128)(2,1)} %bitcast.32), dimensions={1,2} | broadcast | bytes 373248 | tf_op jit(solution)/shard_map/broadcast_in_dim | solution.py:25
  8.8 10.9 %all-to-all-start = ((bf16[8,54,384]{2,1,0:T(8,128)(2,1)}), bf16[8,54,384]{2,1,0:T(8,128)(2,1)S(1)}, u32[]{:S(2)}, u32[]{:S(2)}) async-start(bf16[8,54,384]{2,1,0:T(8,128)(2,1)} %broadcast_in_dim.9), calls=%async_computation | async-start | bytes 688128 | tf_op jit(solution)/shard_map/all_to_all | solution.py:24
  19.7 0.7 reduce.1
  20.4 11.6 %all-to-all-done = bf16[8,54,384]{2,1,0:T(8,128)(2,1)S(1)} async-done(((bf16[8,54,384]{2,1,0:T(8,128)(2,1)}), bf16[8,54,384]{2,1,0:T(8,128)(2,1)S(1)}, u32[]{:S(2)}, u32[]{:S(2)}) %all-to-all-start) | async-done | bytes 331808 | tf_op jit(solution)/shard_map/all_to_all | solution.py:24
  32.0 0.8 reshape.108
  32.9 1.0 constant_dynamic-slice_fusion.1
  33.9 1.7 %fusion.20 = bf16[32,32,384]{2,1,0:T(8,128)(2,1)S(1)} fusion(bf16[2,2,128,384,1]{3,2,1,4,0:T(8,128)(2,1)} %bitcast.33, bf16[32,2,32,2,128]{4,3,2,1,0:T(2,128)(2,1)S(1)} %bitcast.26), kind=kOutput, calls=%fused_computation.32 | convolution fusion | flops 403046400 | bytes 2228224 | tf_op jit(solution)/shard_map/apbqc,pqco->abo/dot_general | solution.py:187
  35.7 1.3 collective-permute-start
  37.0 6.3 %collective-permute-start.3 = (f32[384]{0:T(512)S(1)}, f32[384]{0:T(512)S(1)}, u32[]{:S(2)}, u32[]{:S(2)}) collective-permute-start(f32[384]{0:T(512)S(1)} %reduce.1), channel_id=1, source_target_pairs={{0,256},{256,0},{1,257},{257,1},{2,258},{258,2},{3,259},{259,3},{4... | collective-permute-start | bytes 4616 | tf_op jit(solution)/shard_map/ppermute | solution.py:30
  43.6 1.0 fusion.23
  44.6 2.2 %collective-permute-start.1 = (bf16[34,9,384]{2,1,0:T(8,128)(2,1)}, bf16[34,9,384]{2,1,0:T(8,128)(2,1)S(1)}, u32[]{:S(2)}, u32[]{:S(2)}) collective-permute-start(bf16[34,9,384]{2,1,0:T(8,128)(2,1)} %get-tuple-element.20), channel_id=1, source_target_pairs={{0,4},{4,8},{8,12},{12,16},{16,20},{20,24},{24,28},{1,5},{5,9},{9,... | collective-permute-start | bytes 705032 | tf_op jit(solution)/shard_map/ppermute | solution.py:203
  46.8 1.3 collective-permute-start.2
  48.4 6.2 %collective-permute-done.1 = bf16[34,9,384]{2,1,0:T(8,128)(2,1)S(1)} collective-permute-done((bf16[34,9,384]{2,1,0:T(8,128)(2,1)}, bf16[34,9,384]{2,1,0:T(8,128)(2,1)S(1)}, u32[]{:S(2)}, u32[]{:S(2)}) %collective-permute-start.1) | collective-permute-done | bytes 235040 | tf_op jit(solution)/shard_map/ppermute | solution.py:203
  54.7 3.9 %collective-permute-done.2 = bf16[34,9,384]{2,1,0:T(8,128)(2,1)} collective-permute-done((bf16[34,9,384]{2,1,0:T(8,128)(2,1)}, bf16[34,9,384]{2,1,0:T(8,128)(2,1)}, u32[]{:S(2)}, u32[]{:S(2)}) %collective-permute-start.2) | collective-permute-done | bytes 235040 | tf_op jit(solution)/shard_map/ppermute | solution.py:204
  58.5 1.6 %convert_reduce_fusion = (f32[34,50]{1,0:T(8,128)S(1)}, bf16[34,50,384]{2,1,0:T(8,128)(2,1)S(1)}) fusion(bf16[34,9,384]{2,1,0:T(8,128)(2,1)} %collective-permute-done.2, bf16[34,32,384]{2,1,0:T(8,128)(2,1)S(1)} %maximum_select_fusion, bf16[34,9,384]{2,1,0:T(8,128)(2,1)S(1)} %collective-permute-done.1), kind=kLoop, calls=%fused_computation.3 | loop fusion | flops 5220700 | bytes 2618000 | tf_op jit(solution)/shard_map/reduce_sum | solution.py:16
  60.1 1.5 %slice.66.center_ref = bf16[32,48,384]{2,1,0:T(8,128)(2,1)} slice(bf16[34,50,384]{2,1,0:T(8,128)(2,1)S(1)} %get-tuple-element.16), slice={[1:33], [1:49], [0:384]} | slice | bytes 2359296 | tf_op jit(solution)/shard_map/slice | solution.py:210
  61.7 0.8 fusion.2
  62.5 6.8 %fusion.7 = bf16[34,50,384]{2,1,0:T(8,128)(2,1)S(1)} fusion(bf16[34,50,384]{2,1,0:T(8,128)(2,1)S(1)} %get-tuple-element.16, f32[384]{0:T(512)S(1)} %get-tuple-element.27, f32[34,50]{1,0:T(8,128)S(1)} %add_rsqrt_fusion, f32[34,50]{1,0:T(8,128)S(1)} %broadcast_multiply_fusion), kind=kLoop, calls=%fused_computation.11 | loop fusion | flops 45043200 | bytes 2626336 | tf_op jit(solution)/shard_map/convert_element_type | solution.py:20
  69.3 0.8 fusion.22
  70.2 2.1 %pad_maximum_fusion.stacked_hbm = bf16[34,48,1152]{2,1,0:T(8,128)(2,1)} fusion(bf16[34,48,384]{2,1,0:T(8,128)(2,1)S(1)} %get-tuple-element.18, bf16[34,48,384]{2,1,0:T(8,128)(2,1)S(1)} %get-tuple-element.19, bf16[34,48,384]{2,1,0:T(8,128)(2,1)S(1)} %get-tuple-element.17), kind=kLoop, calls=%fused_computation.1 | loop fusion | flops 11280384 | bytes 7520256 | tf_op jit(solution)/shard_map/concatenate | solution.py:34
  72.3 5.3 %all-gather.2.cloned.1.call-done.weights_ref = bf16[6912,384]{1,0:T(8,128)(2,1)} async-done(((bf16[432,384]{1,0:T(8,128)(2,1)}), bf16[6912,384]{1,0:T(8,128)(2,1)}) %all-gather.2.cloned.1.call-update) | async-done | bytes 5308432 | tf_op jit(solution)/shard_map/all_gather | solution.py:178
  77.6 15.9 %shard_map.94 = (bf16[16,32,384]{2,1,0:T(8,128)(2,1)S(1)}, bf16[16,32,384]{2,1,0:T(8,128)(2,1)S(1)}, bf16[32,32,128]{2,1,0:T(8,128)(2,1)S(1)}) custom-call(bf16[34,48,1152]{2,1,0:T(8,128)(2,1)} %pad_maximum_fusion.stacked_hbm, bf16[32,48,384]{2,1,0:T(8,128)(2,1)} %slice.66.center_ref, bf16[6912,384]{1,0:T(8,128)(2,1)} %all-gather.2.cloned.1.call-done.weights_ref, ...), custom_call_target="tpu_custom_call" | custom-call | flops 5435817984 | bytes 5308416 | tf_op jit(solution)/shard_map/pallas_call | solution.py:218
  93.4 20.9 %all_to_all.20 = bf16[32,32,128]{2,1,0:T(8,128)(2,1)S(1)} all-to-all(bf16[32,32,128]{2,1,0:T(8,128)(2,1)S(1)} %get-tuple-element.14), channel_id=1, replica_groups=mesh['section'=2,'sy'=8,'sx'=8,'mb'=4] {'sx','mb'}, dimensions={0} | all-to-all | bytes 524288 | tf_op jit(solution)/shard_map/all_to_all | solution.py:243
  115.1 6.8 %all-to-all-start.2 = ((bf16[16,32,128]{2,1,0:T(8,128)(2,1)}), bf16[16,32,128]{2,1,0:T(8,128)(2,1)S(1)}, u32[]{:S(2)}, u32[]{:S(2)}) async-start(bf16[16,32,128]{2,1,0:T(8,128)(2,1)} %broadcast_in_dim.10), calls=%async_computation.2 | async-start | bytes 262144 | tf_op jit(solution)/shard_map/all_to_all | solution.py:24
  122.0 2.0 %collective-permute-start.4 = (bf16[16,32,384]{2,1,0:T(8,128)(2,1)S(1)}, bf16[16,32,384]{2,1,0:T(8,128)(2,1)S(1)}, u32[]{:S(2)}, u32[]{:S(2)}) collective-permute-start(bf16[16,32,384]{2,1,0:T(8,128)(2,1)S(1)} %broadcast_select_fusion), channel_id=1, source_target_pairs={{0,256},{256,0},{1,257},{257,1},{2,258},{258,2},{3,259},{259,3},{4... | collective-permute-start | bytes 1179656 | tf_op jit(solution)/shard_map/ppermute | solution.py:30
  124.0 5.2 %all-to-all-done.2 = bf16[16,32,128]{2,1,0:T(8,128)(2,1)S(1)} async-done(((bf16[16,32,128]{2,1,0:T(8,128)(2,1)}), bf16[16,32,128]{2,1,0:T(8,128)(2,1)S(1)}, u32[]{:S(2)}, u32[]{:S(2)}) %all-to-all-start.2) | async-done | bytes 131104 | tf_op jit(solution)/shard_map/all_to_all | solution.py:24
  129.3 0.7 broadcast_in_dim.11
  130.0 3.9 %all-to-all-start.3 = ((bf16[32,24,128]{2,1,0:T(8,128)(2,1)}), bf16[32,24,128]{2,1,0:T(8,128)(2,1)S(1)}, u32[]{:S(2)}, u32[]{:S(2)}) async-start(bf16[32,24,128]{2,1,0:T(8,128)(2,1)} %broadcast_in_dim.11), calls=%async_computation.3 | async-start | bytes 393216 | tf_op jit(solution)/shard_map/all_to_all | solution.py:24
  133.8 1.0 maximum_select_fusion.1
  136.0 7.8 %all-to-all-done.3 = bf16[32,24,128]{2,1,0:T(8,128)(2,1)S(1)} async-done(((bf16[32,24,128]{2,1,0:T(8,128)(2,1)}), bf16[32,24,128]{2,1,0:T(8,128)(2,1)S(1)}, u32[]{:S(2)}, u32[]{:S(2)}) %all-to-all-start.3) | async-done | bytes 196640 | tf_op jit(solution)/shard_map/all_to_all | solution.py:24
  143.9 0.7 multiply_reduce_fusion
  145.3 0.7 pad_maximum_fusion.2
  (27 shorter events, 2.0 us)
Async XLA Ops:
  7.2 26.7 %copy-start = (bf16[1,64,64,128]{3,2,1,0:T(8,128)(2,1)S(1)}, bf16[1,64,64,128]{3,2,1,0:T(8,128)(2,1)}, u32[]{:S(2)}) copy-start(bf16[1,64,64,128]{3,2,1,0:T(8,128)(2,1)} %param.7) | copy-start | bytes 3145732
  8.8 23.2 %all-to-all-start = ((bf16[8,54,384]{2,1,0:T(8,128)(2,1)}), bf16[8,54,384]{2,1,0:T(8,128)(2,1)S(1)}, u32[]{:S(2)}, u32[]{:S(2)}) async-start(bf16[8,54,384]{2,1,0:T(8,128)(2,1)} %broadcast_in_dim.9), calls=%async_computation | async-start | bytes 688128 | tf_op jit(solution)/shard_map/all_to_all | solution.py:24
  19.7 57.9 %all-gather.2.cloned.1.call-start = ((), (), s32[]{:S(2)}) async-start(), calls=%async_computation.4 | async-start | bytes 5640192 | tf_op jit(solution)/shard_map/all_gather | solution.py:178
  35.6 12.5 %copy-start.2 = (s32[1,32,32]{2,1,0:T(8,128)S(1)}, s32[1,32,32]{2,1,0:T(8,128)}, u32[]{:S(2)}) copy-start(s32[1,32,32]{2,1,0:T(8,128)} %param.13) | copy-start | bytes 12292
  35.7 7.8 %collective-permute-start = (bf16[9,32,384]{2,1,0:T(8,128)(2,1)S(1)}, bf16[9,32,384]{2,1,0:T(8,128)(2,1)S(1)}, u32[]{:S(2)}, u32[]{:S(2)}) collective-permute-start(bf16[9,32,384]{2,1,0:T(8,128)(2,1)S(1)} %slice_select_fusion), channel_id=1, source_target_pairs={{0,32},{32,64},{64,96},{96,128},{128,160},{160,192},{192,224},{288... | collective-permute-start | bytes 663560 | tf_op jit(solution)/shard_map/ppermute | solution.py:195
  37.0 11.5 %collective-permute-start.3 = (f32[384]{0:T(512)S(1)}, f32[384]{0:T(512)S(1)}, u32[]{:S(2)}, u32[]{:S(2)}) collective-permute-start(f32[384]{0:T(512)S(1)} %reduce.1), channel_id=1, source_target_pairs={{0,256},{256,0},{1,257},{257,1},{2,258},{258,2},{3,259},{259,3},{4... | collective-permute-start | bytes 4616 | tf_op jit(solution)/shard_map/ppermute | solution.py:30
  44.6 10.0 %collective-permute-start.1 = (bf16[34,9,384]{2,1,0:T(8,128)(2,1)}, bf16[34,9,384]{2,1,0:T(8,128)(2,1)S(1)}, u32[]{:S(2)}, u32[]{:S(2)}) collective-permute-start(bf16[34,9,384]{2,1,0:T(8,128)(2,1)} %get-tuple-element.20), channel_id=1, source_target_pairs={{0,4},{4,8},{8,12},{12,16},{16,20},{20,24},{24,28},{1,5},{5,9},{9,... | collective-permute-start | bytes 705032 | tf_op jit(solution)/shard_map/ppermute | solution.py:203
  46.8 11.7 %collective-permute-start.2 = (bf16[34,9,384]{2,1,0:T(8,128)(2,1)}, bf16[34,9,384]{2,1,0:T(8,128)(2,1)}, u32[]{:S(2)}, u32[]{:S(2)}) collective-permute-start(bf16[34,9,384]{2,1,0:T(8,128)(2,1)} %get-tuple-element.21), channel_id=1, source_target_pairs={{4,0},{8,4},{12,8},{16,12},{20,16},{24,20},{28,24},{5,1},{9,5},{13... | collective-permute-start | bytes 705032 | tf_op jit(solution)/shard_map/ppermute | solution.py:204
  70.2 7.4 %copy-start.1 = (bf16[384,256]{1,0:T(8,128)(2,1)S(1)}, bf16[384,256]{1,0:T(8,128)(2,1)}, u32[]{:S(2)}) copy-start(bf16[384,256]{1,0:T(8,128)(2,1)} %head_ref.1) | copy-start | bytes 589828
  115.1 14.1 %all-to-all-start.2 = ((bf16[16,32,128]{2,1,0:T(8,128)(2,1)}), bf16[16,32,128]{2,1,0:T(8,128)(2,1)S(1)}, u32[]{:S(2)}, u32[]{:S(2)}) async-start(bf16[16,32,128]{2,1,0:T(8,128)(2,1)} %broadcast_in_dim.10), calls=%async_computation.2 | async-start | bytes 262144 | tf_op jit(solution)/shard_map/all_to_all | solution.py:24
  122.0 11.9 %collective-permute-start.4 = (bf16[16,32,384]{2,1,0:T(8,128)(2,1)S(1)}, bf16[16,32,384]{2,1,0:T(8,128)(2,1)S(1)}, u32[]{:S(2)}, u32[]{:S(2)}) collective-permute-start(bf16[16,32,384]{2,1,0:T(8,128)(2,1)S(1)} %broadcast_select_fusion), channel_id=1, source_target_pairs={{0,256},{256,0},{1,257},{257,1},{2,258},{258,2},{3,259},{259,3},{4... | collective-permute-start | bytes 1179656 | tf_op jit(solution)/shard_map/ppermute | solution.py:30
  130.0 13.9 %all-to-all-start.3 = ((bf16[32,24,128]{2,1,0:T(8,128)(2,1)}), bf16[32,24,128]{2,1,0:T(8,128)(2,1)S(1)}, u32[]{:S(2)}, u32[]{:S(2)}) async-start(bf16[32,24,128]{2,1,0:T(8,128)(2,1)} %broadcast_in_dim.11), calls=%async_computation.3 | async-start | bytes 393216 | tf_op jit(solution)/shard_map/all_to_all | solution.py:24
Sparse Core Ops, SparseCore 0:
  33.0 44.5 all-gather.1

commit v4 on v3

--- a/solution.py
+++ b/solution.py
@@ -99,10 +99,10 @@
     column_at = lax.axis_index("sx") * side - far + lax.broadcasted_iota(jnp.int32, (band, wide, 1), 1)
     column_in = (column_at >= 0) & (column_at < side * parts_x)
     gain = gain_ref[...].reshape(1, 1, channels)
+    fetch_0.wait()
     for t in range(tall // band):
         strip(t).wait()
-        if t == 0:
-            fetch_0.wait()
+    for t in range(tall // band):
         total = jnp.dot(
             jnp.concatenate(
                 [stacked_ref[t * band + i : t * band + i + band] for i in range(3)], axis=2
@@ -174,7 +174,10 @@
 
     shard = conv_weight[0, 0]
     strip = copies_to(shard, "sx", parts_x)
-    strip, encode_weight, gain_own = lax.optimization_barrier((strip, encode_weight, norm_gain[0, 0]))
+    strip, encode_weight, norm_gain, prior_logits, target_bins, head_weight = lax.optimization_barrier(
+        (strip, encode_weight, norm_gain, prior_logits, target_bins, head_weight)
+    )
+    gain_own = norm_gain[0, 0]
     weights = lax.all_gather(
         strip.reshape(parts_x * shard.shape[0], channels), ("section", "sy"), axis=0, tiled=True
     )

time: 156 us -> 154 us (0.987)
  blocking collectives: 20.9 us -> 44.4 us
  waiting for transfers between devices: 40 us -> 28.8 us
  starting transfers between devices: 34.7 us -> 23.9 us
  local copies, waits for them, and re-layouts: 9.14 us -> 7.47 us
    all_to_all x0 -> x1, blocking collectives: none -> 23 us  [copies_to(): lax.all_to_all(jnp.broadcast_to(block[None], (count,) + block.shape), axe...]
    all_to_all x3 -> x2, waiting for transfers between devices: 24.7 us -> 13.1 us  [copies_to(): lax.all_to_all(jnp.broadcast_to(block[None], (count,) + block.shape), axe...]
    all_to_all x3 -> x2, starting transfers between devices: 21.5 us -> 10.7 us  [copies_to(): lax.all_to_all(jnp.broadcast_to(block[None], (count,) + block.shape), axe...]
  transfers between devices with their start and end apart: 9 -> 8, of which waited for: 6 -> 5; matrix products, arithmetic and copies ran while one was open for 14% -> 13% of each run, Pallas kernels for 0% -> 0%
where the time goes in v4:
time: 154 us; the launch traced here: 152 us
  blocking collectives  44.4 us (29%)
  waiting for transfers between devices  28.8 us (19%)
  starting transfers between devices  23.9 us (16%)
  between operations  16.8 us (11%)
  Pallas kernels  15.1 us (10%)
  other arithmetic  14.2 us (9%)
  local copies, waits for them, and re-layouts  7.47 us (5%)
  matrix products  1.76 us (1%)
    all_to_all x1, blocking collectives, copies_to(): lax.all_to_all(jnp.broadcast_to(block[None], (count,) + block.shape), axe...  23 us
    all_to_all x1, blocking collectives, per_device(): lax.all_to_all(packed, ('sx', 'mb'), split_axis=0, concat_axis=0, tiled=T...  21.4 us
    pallas_call x1, Pallas kernels, per_device(): pl.pallas_call(functools.partial(layers_kernel, (far, half, side, 8, slot...  15.1 us
    all_to_all x2, waiting for transfers between devices, copies_to(): lax.all_to_all(jnp.broadcast_to(block[None], (count,) + block.shape), axe...  13.1 us
    all_to_all x2, starting transfers between devices, copies_to(): lax.all_to_all(jnp.broadcast_to(block[None], (count,) + block.shape), axe...  10.7 us
    ppermute x2, starting transfers between devices, swap(): return lax.ppermute(block, 'section', [(0, 1), (1, 0)])  8.33 us
    convert_element_type x1, other arithmetic, norm_gelu(): return jax.nn.gelu(normed, approximate=False).astype(jnp.bfloat16)  6.8 us
    ppermute x1, waiting for transfers between devices, per_device(): left = lax.ppermute(rows[:, side - reach:], 'sx', forward)  6.29 us
  transfers between devices with their start and end apart: 8, of which 5 were waited for; matrix products, arithmetic and copies ran while one was open for 13% of the time, Pallas kernels for 0%

profile of v4, /device:TPU:1, one launch (start us, length us, event | category | flops | bytes accessed | tf_op | source)
XLA Modules:
  0.0 152.3 jit_solution(7452153592451422215)
XLA Ops:
  7.2 0.9 broadcast_in_dim.9
  8.1 23.0 %all_to_all.20 = bf16[8,54,384]{2,1,0:T(8,128)(2,1)S(1)} all-to-all(bf16[8,54,384]{2,1,0:T(8,128)(2,1)S(1)} %broadcast_in_dim.9), channel_id=1, replica_groups=mesh['section'=2,'sy'=8,'sx'=8,'mb'=4] {'sx'}, dimensions={0} | all-to-all | bytes 663552 | tf_op jit(solution)/shard_map/all_to_all | solution.py:24
  31.2 0.8 reshape.108
  32.1 1.8 %fusion.20 = bf16[32,32,384]{2,1,0:T(8,128)(2,1)S(1)} fusion(bf16[2,2,128,384,1]{3,2,1,4,0:T(8,128)(2,1)} %bitcast.33, bf16[32,2,32,2,128]{4,3,2,1,0:T(2,128)(2,1)S(1)} %bitcast.26), kind=kOutput, calls=%fused_computation.32 | convolution fusion | flops 403046400 | bytes 2228224 | tf_op jit(solution)/shard_map/apbqc,pqco->abo/dot_general | solution.py:190
  33.9 1.3 collective-permute-start
  35.2 6.3 %collective-permute-start.3 = (f32[384]{0:T(512)S(1)}, f32[384]{0:T(512)S(1)}, u32[]{:S(2)}, u32[]{:S(2)}) collective-permute-start(f32[384]{0:T(512)S(1)} %reduce.1), channel_id=1, source_target_pairs={{0,256},{256,0},{1,257},{257,1},{2,258},{258,2},{3,259},{259,3},{4... | collective-permute-start | bytes 4616 | tf_op jit(solution)/shard_map/ppermute | solution.py:30
  41.9 1.0 fusion.23
  42.9 2.2 %collective-permute-start.1 = (bf16[34,9,384]{2,1,0:T(8,128)(2,1)}, bf16[34,9,384]{2,1,0:T(8,128)(2,1)S(1)}, u32[]{:S(2)}, u32[]{:S(2)}) collective-permute-start(bf16[34,9,384]{2,1,0:T(8,128)(2,1)} %get-tuple-element.26), channel_id=1, source_target_pairs={{0,4},{4,8},{8,12},{12,16},{16,20},{20,24},{24,28},{1,5},{5,9},{9,... | collective-permute-start | bytes 705032 | tf_op jit(solution)/shard_map/ppermute | solution.py:206
  45.1 1.3 collective-permute-start.2
  46.4 0.3 reshape.115.target_ref
  46.7 6.3 %collective-permute-done.1 = bf16[34,9,384]{2,1,0:T(8,128)(2,1)S(1)} collective-permute-done((bf16[34,9,384]{2,1,0:T(8,128)(2,1)}, bf16[34,9,384]{2,1,0:T(8,128)(2,1)S(1)}, u32[]{:S(2)}, u32[]{:S(2)}) %collective-permute-start.1) | collective-permute-done | bytes 235040 | tf_op jit(solution)/shard_map/ppermute | solution.py:206
  53.0 3.9 %collective-permute-done.2 = bf16[34,9,384]{2,1,0:T(8,128)(2,1)} collective-permute-done((bf16[34,9,384]{2,1,0:T(8,128)(2,1)}, bf16[34,9,384]{2,1,0:T(8,128)(2,1)}, u32[]{:S(2)}, u32[]{:S(2)}) %collective-permute-start.2) | collective-permute-done | bytes 235040 | tf_op jit(solution)/shard_map/ppermute | solution.py:207
  56.9 1.6 %convert_reduce_fusion = (f32[34,50]{1,0:T(8,128)S(1)}, bf16[34,50,384]{2,1,0:T(8,128)(2,1)S(1)}) fusion(bf16[34,9,384]{2,1,0:T(8,128)(2,1)} %collective-permute-done.2, bf16[34,32,384]{2,1,0:T(8,128)(2,1)S(1)} %maximum_select_fusion, bf16[34,9,384]{2,1,0:T(8,128)(2,1)S(1)} %collective-permute-done.1), kind=kLoop, calls=%fused_computation.3 | loop fusion | flops 5220700 | bytes 2618000 | tf_op jit(solution)/shard_map/reduce_sum | solution.py:16
  58.5 1.5 %slice.66.center_ref = bf16[32,48,384]{2,1,0:T(8,128)(2,1)} slice(bf16[34,50,384]{2,1,0:T(8,128)(2,1)S(1)} %get-tuple-element.22), slice={[1:33], [1:49], [0:384]} | slice | bytes 2359296 | tf_op jit(solution)/shard_map/slice | solution.py:213
  60.0 0.8 fusion.2
  60.9 6.8 %fusion.7 = bf16[34,50,384]{2,1,0:T(8,128)(2,1)S(1)} fusion(bf16[34,50,384]{2,1,0:T(8,128)(2,1)S(1)} %get-tuple-element.22, f32[384]{0:T(512)S(1)} %get-tuple-element.33, f32[34,50]{1,0:T(8,128)S(1)} %add_rsqrt_fusion, f32[34,50]{1,0:T(8,128)S(1)} %broadcast_multiply_fusion), kind=kLoop, calls=%fused_computation.11 | loop fusion | flops 45043200 | bytes 2626336 | tf_op jit(solution)/shard_map/convert_element_type | solution.py:20
  67.7 0.8 fusion.22
  68.6 2.1 %pad_maximum_fusion.stacked_hbm = bf16[34,48,1152]{2,1,0:T(8,128)(2,1)} fusion(bf16[34,48,384]{2,1,0:T(8,128)(2,1)S(1)} %get-tuple-element.24, bf16[34,48,384]{2,1,0:T(8,128)(2,1)S(1)} %get-tuple-element.25, bf16[34,48,384]{2,1,0:T(8,128)(2,1)S(1)} %get-tuple-element.23), kind=kLoop, calls=%fused_computation.1 | loop fusion | flops 11280384 | bytes 7520256 | tf_op jit(solution)/shard_map/concatenate | solution.py:34
  70.7 5.5 %all-gather.2.cloned.1.call-done.weights_ref = bf16[6912,384]{1,0:T(8,128)(2,1)} async-done(((bf16[432,384]{1,0:T(8,128)(2,1)}), bf16[6912,384]{1,0:T(8,128)(2,1)}) %all-gather.2.cloned.1.call-update) | async-done | bytes 5308432 | tf_op jit(solution)/shard_map/all_gather | solution.py:181
  76.3 15.1 %shard_map.94 = (bf16[16,32,384]{2,1,0:T(8,128)(2,1)S(1)}, bf16[16,32,384]{2,1,0:T(8,128)(2,1)S(1)}, bf16[32,32,128]{2,1,0:T(8,128)(2,1)S(1)}) custom-call(bf16[34,48,1152]{2,1,0:T(8,128)(2,1)} %pad_maximum_fusion.stacked_hbm, bf16[32,48,384]{2,1,0:T(8,128)(2,1)} %slice.66.center_ref, bf16[6912,384]{1,0:T(8,128)(2,1)} %all-gather.2.cloned.1.call-done.weights_ref, ...), custom_call_target="tpu_custom_call" | custom-call | flops 5435817984 | bytes 5308416 | tf_op jit(solution)/shard_map/pallas_call | solution.py:221
  91.4 21.4 %all_to_all.21 = bf16[32,32,128]{2,1,0:T(8,128)(2,1)S(1)} all-to-all(bf16[32,32,128]{2,1,0:T(8,128)(2,1)S(1)} %get-tuple-element.20), channel_id=1, replica_groups=mesh['section'=2,'sy'=8,'sx'=8,'mb'=4] {'sx','mb'}, dimensions={0} | all-to-all | bytes 524288 | tf_op jit(solution)/shard_map/all_to_all | solution.py:246
  112.8 0.7 broadcast_in_dim.10
  113.4 6.8 %all-to-all-start.2 = ((bf16[16,32,128]{2,1,0:T(8,128)(2,1)}), bf16[16,32,128]{2,1,0:T(8,128)(2,1)S(1)}, u32[]{:S(2)}, u32[]{:S(2)}) async-start(bf16[16,32,128]{2,1,0:T(8,128)(2,1)} %broadcast_in_dim.10), calls=%async_computation.2 | async-start | bytes 262144 | tf_op jit(solution)/shard_map/all_to_all | solution.py:24
  120.3 2.0 %collective-permute-start.4 = (bf16[16,32,384]{2,1,0:T(8,128)(2,1)S(1)}, bf16[16,32,384]{2,1,0:T(8,128)(2,1)S(1)}, u32[]{:S(2)}, u32[]{:S(2)}) collective-permute-start(bf16[16,32,384]{2,1,0:T(8,128)(2,1)S(1)} %broadcast_select_fusion), channel_id=1, source_target_pairs={{0,256},{256,0},{1,257},{257,1},{2,258},{258,2},{3,259},{259,3},{4... | collective-permute-start | bytes 1179656 | tf_op jit(solution)/shard_map/ppermute | solution.py:30
  122.3 5.2 %all-to-all-done.2 = bf16[16,32,128]{2,1,0:T(8,128)(2,1)S(1)} async-done(((bf16[16,32,128]{2,1,0:T(8,128)(2,1)}), bf16[16,32,128]{2,1,0:T(8,128)(2,1)S(1)}, u32[]{:S(2)}, u32[]{:S(2)}) %all-to-all-start.2) | async-done | bytes 131104 | tf_op jit(solution)/shard_map/all_to_all | solution.py:24
  127.6 0.7 broadcast_in_dim.11
  128.3 3.9 %all-to-all-start.3 = ((bf16[32,24,128]{2,1,0:T(8,128)(2,1)}), bf16[32,24,128]{2,1,0:T(8,128)(2,1)S(1)}, u32[]{:S(2)}, u32[]{:S(2)}) async-start(bf16[32,24,128]{2,1,0:T(8,128)(2,1)} %broadcast_in_dim.11), calls=%async_computation.3 | async-start | bytes 393216 | tf_op jit(solution)/shard_map/all_to_all | solution.py:24
  132.2 1.0 maximum_select_fusion.1
  133.2 0.5 slice.68
  134.4 7.8 %all-to-all-done.3 = bf16[32,24,128]{2,1,0:T(8,128)(2,1)S(1)} async-done(((bf16[32,24,128]{2,1,0:T(8,128)(2,1)}), bf16[32,24,128]{2,1,0:T(8,128)(2,1)S(1)}, u32[]{:S(2)}, u32[]{:S(2)}) %all-to-all-start.3) | async-done | bytes 196640 | tf_op jit(solution)/shard_map/all_to_all | solution.py:24
  142.2 0.7 multiply_reduce_fusion
  143.6 0.7 pad_maximum_fusion.2
  (30 shorter events, 0.6 us)
Async XLA Ops:
  7.2 24.9 %copy-start = (bf16[1,64,64,128]{3,2,1,0:T(8,128)(2,1)S(1)}, bf16[1,64,64,128]{3,2,1,0:T(8,128)(2,1)}, u32[]{:S(2)}) copy-start(bf16[1,64,64,128]{3,2,1,0:T(8,128)(2,1)} %param.7) | copy-start | bytes 3145732
  7.2 69.1 %all-gather.2.cloned.1.call-start = ((), (), s32[]{:S(2)}) async-start(), calls=%async_computation.4 | async-start | bytes 5640192 | tf_op jit(solution)/shard_map/all_gather | solution.py:181
  32.0 3.1 %copy-start.4 = (f32[1,1,384]{2,1,0:T(1,128)S(1)}, f32[1,1,384]{2,1,0:T(1,128)}, u32[]{:S(2)}) copy-start(f32[1,1,384]{2,1,0:T(1,128)} %param.10) | copy-start | bytes 4612
  32.1 9.5 %copy-start.2 = (bf16[1,32,32,256]{3,2,1,0:T(8,128)(2,1)S(1)}, bf16[1,32,32,256]{3,2,1,0:T(8,128)(2,1)}, u32[]{:S(2)}) copy-start(bf16[1,32,32,256]{3,2,1,0:T(8,128)(2,1)} %param.12) | copy-start | bytes 1572868
  33.9 7.8 %collective-permute-start = (bf16[9,32,384]{2,1,0:T(8,128)(2,1)S(1)}, bf16[9,32,384]{2,1,0:T(8,128)(2,1)S(1)}, u32[]{:S(2)}, u32[]{:S(2)}) collective-permute-start(bf16[9,32,384]{2,1,0:T(8,128)(2,1)S(1)} %slice_select_fusion), channel_id=1, source_target_pairs={{0,32},{32,64},{64,96},{96,128},{128,160},{160,192},{192,224},{288... | collective-permute-start | bytes 663560 | tf_op jit(solution)/shard_map/ppermute | solution.py:198
  35.2 11.5 %collective-permute-start.3 = (f32[384]{0:T(512)S(1)}, f32[384]{0:T(512)S(1)}, u32[]{:S(2)}, u32[]{:S(2)}) collective-permute-start(f32[384]{0:T(512)S(1)} %reduce.1), channel_id=1, source_target_pairs={{0,256},{256,0},{1,257},{257,1},{2,258},{258,2},{3,259},{259,3},{4... | collective-permute-start | bytes 4616 | tf_op jit(solution)/shard_map/ppermute | solution.py:30
  41.6 4.8 %copy-start.3 = (s32[1,32,32]{2,1,0:T(8,128)S(1)}, s32[1,32,32]{2,1,0:T(8,128)}, u32[]{:S(2)}) copy-start(s32[1,32,32]{2,1,0:T(8,128)} %param.13) | copy-start | bytes 12292
  42.9 10.1 %collective-permute-start.1 = (bf16[34,9,384]{2,1,0:T(8,128)(2,1)}, bf16[34,9,384]{2,1,0:T(8,128)(2,1)S(1)}, u32[]{:S(2)}, u32[]{:S(2)}) collective-permute-start(bf16[34,9,384]{2,1,0:T(8,128)(2,1)} %get-tuple-element.26), channel_id=1, source_target_pairs={{0,4},{4,8},{8,12},{12,16},{16,20},{20,24},{24,28},{1,5},{5,9},{9,... | collective-permute-start | bytes 705032 | tf_op jit(solution)/shard_map/ppermute | solution.py:206
  45.1 11.8 %collective-permute-start.2 = (bf16[34,9,384]{2,1,0:T(8,128)(2,1)}, bf16[34,9,384]{2,1,0:T(8,128)(2,1)}, u32[]{:S(2)}, u32[]{:S(2)}) collective-permute-start(bf16[34,9,384]{2,1,0:T(8,128)(2,1)} %get-tuple-element.27), channel_id=1, source_target_pairs={{4,0},{8,4},{12,8},{16,12},{20,16},{24,20},{28,24},{5,1},{9,5},{13... | collective-permute-start | bytes 705032 | tf_op jit(solution)/shard_map/ppermute | solution.py:207
  68.6 7.7 %copy-start.1 = (bf16[384,256]{1,0:T(8,128)(2,1)S(1)}, bf16[384,256]{1,0:T(8,128)(2,1)}, u32[]{:S(2)}) copy-start(bf16[384,256]{1,0:T(8,128)(2,1)} %head_ref) | copy-start | bytes 589828
  113.4 14.1 %all-to-all-start.2 = ((bf16[16,32,128]{2,1,0:T(8,128)(2,1)}), bf16[16,32,128]{2,1,0:T(8,128)(2,1)S(1)}, u32[]{:S(2)}, u32[]{:S(2)}) async-start(bf16[16,32,128]{2,1,0:T(8,128)(2,1)} %broadcast_in_dim.10), calls=%async_computation.2 | async-start | bytes 262144 | tf_op jit(solution)/shard_map/all_to_all | solution.py:24
  120.3 11.9 %collective-permute-start.4 = (bf16[16,32,384]{2,1,0:T(8,128)(2,1)S(1)}, bf16[16,32,384]{2,1,0:T(8,128)(2,1)S(1)}, u32[]{:S(2)}, u32[]{:S(2)}) collective-permute-start(bf16[16,32,384]{2,1,0:T(8,128)(2,1)S(1)} %broadcast_select_fusion), channel_id=1, source_target_pairs={{0,256},{256,0},{1,257},{257,1},{2,258},{258,2},{3,259},{259,3},{4... | collective-permute-start | bytes 1179656 | tf_op jit(solution)/shard_map/ppermute | solution.py:30
  128.3 13.9 %all-to-all-start.3 = ((bf16[32,24,128]{2,1,0:T(8,128)(2,1)}), bf16[32,24,128]{2,1,0:T(8,128)(2,1)S(1)}, u32[]{:S(2)}, u32[]{:S(2)}) async-start(bf16[32,24,128]{2,1,0:T(8,128)(2,1)} %broadcast_in_dim.11), calls=%async_computation.3 | async-start | bytes 393216 | tf_op jit(solution)/shard_map/all_to_all | solution.py:24
Sparse Core Ops, SparseCore 0:
  32.1 44.0 all-gather.1

commit v5 on v4

--- a/solution.py
+++ b/solution.py
@@ -66,10 +66,12 @@
     out_0_ref,
     out_1_ref,
     packed_ref,
+    loss_ref,
     stacked_ref,
     weight_0,
     weight_1,
     hidden_ref,
+    gradient_ref,
     sem_s,
     sem_w,
 ):
@@ -144,16 +146,54 @@
     picked = jnp.sum(jnp.where(hit, shifted, 0.0), axis=1, keepdims=True)
     loss = jnp.sum(jnp.log(exp_total) - picked, axis=0, keepdims=True)
     delta = (exp_terms / exp_total - hit.astype(jnp.float32)).astype(jnp.bfloat16)
-    gradient = lax.dot_general(
+    gradient_ref[...] = lax.dot_general(
         flat, delta, (((0,), (0,)), ((), ())), preferred_element_type=jnp.float32
     )
-    loss = jnp.broadcast_to(loss, (8, 128))
-    deep = channels * bins // (128 * slots)
-    across = channels // deep
+    loss_ref[...] = jnp.broadcast_to(loss, loss_ref.shape)
+    piece = packed_ref.shape[1] // 2
+    across = channels // (2 * piece)
     for s in range(slots):
-        row, lane = (s % across) * deep, (s // across) * 128
-        chunk = jnp.concatenate([gradient[row : row + deep, lane : lane + 128], loss], axis=0)
+        row, lane = (s % across) * piece, (s // across) * 128
+        chunk = jnp.concatenate(
+            [
+                gradient_ref[h * channels // 2 + row : h * channels // 2 + row + piece, lane : lane + 128]
+                for h in range(2)
+            ],
+            axis=0,
+        )
         packed_ref[s] = chunk.astype(jnp.bfloat16)
+
+
+def spread_kernel(arrived_ref, loss_ref, copies_ref):
+    total = jnp.sum(arrived_ref[...].astype(jnp.float32), axis=0)
+    total = jnp.concatenate([total, loss_ref[...]], axis=0).astype(jnp.bfloat16)
+    copies_ref[...] = jnp.broadcast_to(total[None], copies_ref.shape)
+
+
+def share_kernel(arrived_ref, copies_ref):
+    total = jnp.sum(arrived_ref[...].astype(jnp.float32), axis=0)
+    deep = total.shape[0] - 8
+    piece = deep // 2
+    values, loss = total[:deep], total[deep : deep + 1]
+    squares = jnp.sum(jnp.sum(values * values, axis=1, keepdims=True), axis=0, keepdims=True)
+    squares = jnp.broadcast_to(squares, (1, 128))
+    own = jnp.where(lax.axis_index("section") == 0, values[:piece], values[piece:])
+    rest = copies_ref.shape[1] - piece
+    below = jnp.where(lax.broadcasted_iota(jnp.int32, (rest, 128), 0) == 0, squares, loss)
+    block = jnp.concatenate([own, below], axis=0).astype(jnp.bfloat16)
+    copies_ref[...] = jnp.broadcast_to(block[None], copies_ref.shape)
+
+
+def finish_kernel(sizes, arrived_ref, step_ref, loss_ref):
+    piece, entries, cells = sizes
+    arrived = arrived_ref[...].astype(jnp.float32)
+    tails = jnp.sum(arrived, axis=0)
+    scale = lax.rsqrt(tails[piece : piece + 1] * (1.0 / entries) + 1e-06)
+    loss_ref[...] = tails[piece + 1 : piece + 2] * (1.0 / cells)
+    across = step_ref.shape[0] // piece
+    for s in range(arrived_ref.shape[0]):
+        row, lane = (s % across) * piece, (s // across) * 128
+        step_ref[row : row + piece, lane : lane + 128] = arrived[s, :piece] * scale
 
 
 def per_device(
@@ -218,20 +258,22 @@
     vmem = pl.BlockSpec(memory_space=pltpu.VMEM)
     anywhere = pl.BlockSpec(memory_space=pl.ANY)
     taps = 3 * channels
-    own_0, own_1, packed = pl.pallas_call(
+    own_0, own_1, packed, loss = pl.pallas_call(
         functools.partial(layers_kernel, (far, half, side, 8, slots, parts_y, parts_x)),
         out_shape=(
             jax.ShapeDtypeStruct((half, side, channels), jnp.bfloat16),
             jax.ShapeDtypeStruct((half, side, channels), jnp.bfloat16),
-            jax.ShapeDtypeStruct((slots, deep + 8, 128), jnp.bfloat16),
+            jax.ShapeDtypeStruct((slots, deep, 128), jnp.bfloat16),
+            jax.ShapeDtypeStruct((8, 128), jnp.float32),
         ),
         in_specs=[anywhere, vmem, anywhere, vmem, vmem, vmem, vmem],
-        out_specs=(vmem, vmem, vmem),
+        out_specs=(vmem, vmem, vmem, vmem),
         scratch_shapes=[
             pltpu.VMEM((tall + 2 * near, wide, taps), jnp.bfloat16),
             pltpu.VMEM((3 * taps, channels), jnp.bfloat16),
             pltpu.VMEM((3 * taps, channels), jnp.bfloat16),
             pltpu.VMEM((tall, side, taps), jnp.bfloat16),
+            pltpu.VMEM((channels, bins), jnp.float32),
             pltpu.SemaphoreType.DMA((tall // 8,)),
             pltpu.SemaphoreType.DMA((2,)),
         ],
@@ -243,20 +285,30 @@
         ),
     )(stacked, center, weights, gain_1.reshape(1, channels), head_weight, prior, target)
 
-    packed = lax.all_to_all(packed, ("sx", "mb"), split_axis=0, concat_axis=0, tiled=True)
-    partial = jnp.sum(packed.astype(jnp.float32), axis=0).astype(jnp.bfloat16)
-    packed = copies_to(partial, ("section", "sy"), 2 * parts_y)
-    partial = jnp.sum(packed.astype(jnp.float32), axis=0)
-    loss_all = partial[deep, 0]
-    gathered = copies_to(partial[:deep].astype(jnp.bfloat16), ("sx", "mb"), slots)
-    scale = lax.rsqrt(jnp.mean(jnp.square(gathered.astype(jnp.float32))) + 1e-06)
-    halves = bins // 128
-    by_half = gathered.reshape(halves, channels, 128)
-    own_rows = lax.dynamic_slice_in_dim(by_half, section * (channels // 2), channels // 2, axis=1)
-    head_step = jnp.concatenate(
-        [own_rows[h].astype(jnp.float32) * scale for h in range(halves)], axis=1
-    )
-    mean_loss = loss_all / (parts_b * parts_y * parts_x * side * side)
+    def exchange(blocks, axes):
+        return lax.all_to_all(blocks, axes, split_axis=0, concat_axis=0, tiled=True)
+
+    small = pltpu.CompilerParams(vmem_limit_bytes=4 * 2**20)
+    packed = exchange(packed, ("sx", "mb"))
+    packed = pl.pallas_call(
+        spread_kernel, out_shape=jax.ShapeDtypeStruct((2 * parts_y, deep + 8, 128), jnp.bfloat16), compiler_params=small
+    )(packed, loss)
+    packed = exchange(packed, ("section", "sy"))
+    packed = pl.pallas_call(
+        share_kernel, out_shape=jax.ShapeDtypeStruct((slots, deep // 2 + 4, 128), jnp.bfloat16), compiler_params=small
+    )(packed)
+    packed = exchange(packed, ("sx", "mb"))
+    head_step, loss = pl.pallas_call(
+        functools.partial(
+            finish_kernel, (deep // 2, channels * bins, parts_b * parts_y * parts_x * side * side)
+        ),
+        out_shape=(
+            jax.ShapeDtypeStruct((channels // 2, bins), jnp.float32),
+            jax.ShapeDtypeStruct((1, 128), jnp.float32),
+        ),
+        compiler_params=small,
+    )(packed)
+    mean_loss = loss[0, 0]
 
     sent = swap(jnp.where(first, own_1, own_0))
     grids = jnp.where(

time: 154 us -> 149 us (0.968)
  blocking collectives: 44.4 us -> 36.6 us
  starting transfers between devices: 23.9 us -> 27.4 us
  waiting for transfers between devices: 28.8 us -> 32.2 us
  between operations: 16.8 us -> 14.3 us
  Pallas kernels: 15.1 us -> 17.3 us
  local copies, waits for them, and re-layouts: 7.47 us -> 5.57 us
    all_to_all x1, blocking collectives: 21.4 us -> 13.6 us  [exchange(): return lax.all_to_all(blocks, axes, split_axis=0, concat_axis=0, tiled=True)]
    all_to_all x2, waiting for transfers between devices: 13.1 us -> 16.5 us  [exchange(): return lax.all_to_all(blocks, axes, split_axis=0, concat_axis=0, tiled=True)]
    all_to_all x2, starting transfers between devices: 10.7 us -> 13.8 us  [exchange(): return lax.all_to_all(blocks, axes, split_axis=0, concat_axis=0, tiled=True)]
    pallas_call x0 -> x3, Pallas kernels: none -> 1.56 us  [the longest x1 0.77 us: per_device(): pl.pallas_call(share_kernel, out_shape=jax.ShapeDtypeStruct((slots, deep...]
  transfers between devices with their start and end apart: 8 -> 8, of which waited for: 5 -> 5; matrix products, arithmetic and copies ran while one was open for 13% -> 12% of each run, Pallas kernels for 0% -> 1%
where the time goes in v5:
time: 149 us; the launch traced here: 148 us
  blocking collectives  36.6 us (25%)
  waiting for transfers between devices  32.2 us (22%)
  starting transfers between devices  27.4 us (18%)
  Pallas kernels  17.3 us (12%)
  between operations  14.3 us (10%)
  other arithmetic  12.7 us (9%)
  local copies, waits for them, and re-layouts  5.57 us (4%)
  matrix products  1.76 us (1%)
    all_to_all x1, blocking collectives, copies_to(): lax.all_to_all(jnp.broadcast_to(block[None], (count,) + block.shape), axe...  23 us
    all_to_all x2, waiting for transfers between devices, exchange(): return lax.all_to_all(blocks, axes, split_axis=0, concat_axis=0, tiled=True)  16.5 us
    pallas_call x1, Pallas kernels, per_device(): pl.pallas_call(functools.partial(layers_kernel, (far, half, side, 8, slot...  15.8 us
    all_to_all x2, starting transfers between devices, exchange(): return lax.all_to_all(blocks, axes, split_axis=0, concat_axis=0, tiled=True)  13.8 us
    all_to_all x1, blocking collectives, exchange(): return lax.all_to_all(blocks, axes, split_axis=0, concat_axis=0, tiled=True)  13.6 us
    ppermute x2, starting transfers between devices, swap(): return lax.ppermute(block, 'section', [(0, 1), (1, 0)])  8.77 us
    convert_element_type x1, other arithmetic, norm_gelu(): return jax.nn.gelu(normed, approximate=False).astype(jnp.bfloat16)  6.8 us
    ppermute x1, waiting for transfers between devices, per_device(): left = lax.ppermute(rows[:, side - reach:], 'sx', forward)  6.29 us
  transfers between devices with their start and end apart: 8, of which 5 were waited for; matrix products, arithmetic and copies ran while one was open for 12% of the time, Pallas kernels for 1%

profile of v5, /device:TPU:1, one launch (start us, length us, event | category | flops | bytes accessed | tf_op | source)
XLA Modules:
  0.0 147.9 jit_solution(14482380432574612441)
XLA Ops:
  7.2 0.9 broadcast_in_dim.5
  8.1 23.0 %all_to_all.20 = bf16[8,54,384]{2,1,0:T(8,128)(2,1)S(1)} all-to-all(bf16[8,54,384]{2,1,0:T(8,128)(2,1)S(1)} %broadcast_in_dim.5), channel_id=1, replica_groups=mesh['section'=2,'sy'=8,'sx'=8,'mb'=4] {'sx'}, dimensions={0} | all-to-all | bytes 663552 | tf_op jit(solution)/shard_map/all_to_all | solution.py:24
  31.2 0.8 reshape.95
  32.1 1.8 %fusion.20 = bf16[32,32,384]{2,1,0:T(8,128)(2,1)S(1)} fusion(bf16[2,2,128,384,1]{3,2,1,4,0:T(8,128)(2,1)} %bitcast.28, bf16[32,2,32,2,128]{4,3,2,1,0:T(2,128)(2,1)S(1)} %bitcast.22), kind=kOutput, calls=%fused_computation.32 | convolution fusion | flops 403046400 | bytes 2228224 | tf_op jit(solution)/shard_map/apbqc,pqco->abo/dot_general | solution.py:230
  33.9 1.3 collective-permute-start
  35.2 6.3 %collective-permute-start.3 = (f32[384]{0:T(512)S(1)}, f32[384]{0:T(512)S(1)}, u32[]{:S(2)}, u32[]{:S(2)}) collective-permute-start(f32[384]{0:T(512)S(1)} %reduce), channel_id=1, source_target_pairs={{0,256},{256,0},{1,257},{257,1},{2,258},{258,2},{3,259},{259,3},{4... | collective-permute-start | bytes 4616 | tf_op jit(solution)/shard_map/ppermute | solution.py:30
  41.6 0.1 fusion.24
  41.7 0.2 maximum_select_fusion
  41.9 1.0 fusion.23
  42.9 2.2 %collective-permute-start.1 = (bf16[34,9,384]{2,1,0:T(8,128)(2,1)}, bf16[34,9,384]{2,1,0:T(8,128)(2,1)S(1)}, u32[]{:S(2)}, u32[]{:S(2)}) collective-permute-start(bf16[34,9,384]{2,1,0:T(8,128)(2,1)} %get-tuple-element.32), channel_id=1, source_target_pairs={{0,4},{4,8},{8,12},{12,16},{16,20},{20,24},{24,28},{1,5},{5,9},{9,... | collective-permute-start | bytes 705032 | tf_op jit(solution)/shard_map/ppermute | solution.py:246
  45.1 1.3 collective-permute-start.2
  46.4 0.3 reshape.101.target_ref
  46.7 6.3 %collective-permute-done.1 = bf16[34,9,384]{2,1,0:T(8,128)(2,1)S(1)} collective-permute-done((bf16[34,9,384]{2,1,0:T(8,128)(2,1)}, bf16[34,9,384]{2,1,0:T(8,128)(2,1)S(1)}, u32[]{:S(2)}, u32[]{:S(2)}) %collective-permute-start.1) | collective-permute-done | bytes 235040 | tf_op jit(solution)/shard_map/ppermute | solution.py:246
  53.0 3.9 %collective-permute-done.2 = bf16[34,9,384]{2,1,0:T(8,128)(2,1)} collective-permute-done((bf16[34,9,384]{2,1,0:T(8,128)(2,1)}, bf16[34,9,384]{2,1,0:T(8,128)(2,1)}, u32[]{:S(2)}, u32[]{:S(2)}) %collective-permute-start.2) | collective-permute-done | bytes 235040 | tf_op jit(solution)/shard_map/ppermute | solution.py:247
  56.9 1.6 %convert_reduce_fusion = (f32[34,50]{1,0:T(8,128)S(1)}, bf16[34,50,384]{2,1,0:T(8,128)(2,1)S(1)}) fusion(bf16[34,9,384]{2,1,0:T(8,128)(2,1)} %collective-permute-done.2, bf16[34,32,384]{2,1,0:T(8,128)(2,1)S(1)} %maximum_select_fusion, bf16[34,9,384]{2,1,0:T(8,128)(2,1)S(1)} %collective-permute-done.1), kind=kLoop, calls=%fused_computation.3 | loop fusion | flops 5220700 | bytes 2618000 | tf_op jit(solution)/shard_map/reduce_sum | solution.py:16
  58.5 1.5 %slice.53.center_ref = bf16[32,48,384]{2,1,0:T(8,128)(2,1)} slice(bf16[34,50,384]{2,1,0:T(8,128)(2,1)S(1)} %get-tuple-element.28), slice={[1:33], [1:49], [0:384]} | slice | bytes 2359296 | tf_op jit(solution)/shard_map/slice | solution.py:253
  60.0 0.8 fusion.2
  60.9 6.8 %fusion.7 = bf16[34,50,384]{2,1,0:T(8,128)(2,1)S(1)} fusion(bf16[34,50,384]{2,1,0:T(8,128)(2,1)S(1)} %get-tuple-element.28, f32[384]{0:T(512)S(1)} %get-tuple-element.37, f32[34,50]{1,0:T(8,128)S(1)} %add_rsqrt_fusion, f32[34,50]{1,0:T(8,128)S(1)} %broadcast_multiply_fusion), kind=kLoop, calls=%fused_computation.11 | loop fusion | flops 45043200 | bytes 2626336 | tf_op jit(solution)/shard_map/convert_element_type | solution.py:20
  67.7 0.8 fusion.22
  68.6 2.1 %pad_maximum_fusion.stacked_hbm = bf16[34,48,1152]{2,1,0:T(8,128)(2,1)} fusion(bf16[34,48,384]{2,1,0:T(8,128)(2,1)S(1)} %get-tuple-element.30, bf16[34,48,384]{2,1,0:T(8,128)(2,1)S(1)} %get-tuple-element.31, bf16[34,48,384]{2,1,0:T(8,128)(2,1)S(1)} %get-tuple-element.29), kind=kLoop, calls=%fused_computation.1 | loop fusion | flops 11280384 | bytes 7520256 | tf_op jit(solution)/shard_map/concatenate | solution.py:34
  70.7 5.6 %all-gather.2.cloned.1.call-done.weights_ref = bf16[6912,384]{1,0:T(8,128)(2,1)} async-done(((bf16[432,384]{1,0:T(8,128)(2,1)}), bf16[6912,384]{1,0:T(8,128)(2,1)}) %all-gather.2.cloned.1.call-update) | async-done | bytes 5308432 | tf_op jit(solution)/shard_map/all_gather | solution.py:221
  76.2 15.8 %shard_map.94 = (bf16[16,32,384]{2,1,0:T(8,128)(2,1)S(1)}, bf16[16,32,384]{2,1,0:T(8,128)(2,1)S(1)}, bf16[32,24,128]{2,1,0:T(8,128)(2,1)}, f32[8,128]{1,0:T(8,128)S(1)}) custom-call(bf16[34,48,1152]{2,1,0:T(8,128)(2,1)} %pad_maximum_fusion.stacked_hbm, bf16[32,48,384]{2,1,0:T(8,128)(2,1)} %slice.53.center_ref, ...), custom_call_target="tpu_custom_call" | custom-call | flops 5435817984 | bytes 5308416 | tf_op jit(solution)/shard_map/pallas_call | solution.py:261
  92.0 9.9 %all-to-all-start.1 = ((bf16[32,24,128]{2,1,0:T(8,128)(2,1)}), bf16[32,24,128]{2,1,0:T(8,128)(2,1)S(1)}, u32[]{:S(2)}, u32[]{:S(2)}) async-start(bf16[32,24,128]{2,1,0:T(8,128)(2,1)} %get-tuple-element.23), calls=%async_computation.1 | async-start | bytes 393216 | tf_op jit(solution)/shard_map/all_to_all | solution.py:289
  102.0 0.1 broadcast_select_fusion
  102.0 2.4 %collective-permute-start.4 = (bf16[16,32,384]{2,1,0:T(8,128)(2,1)S(1)}, bf16[16,32,384]{2,1,0:T(8,128)(2,1)S(1)}, u32[]{:S(2)}, u32[]{:S(2)}) collective-permute-start(bf16[16,32,384]{2,1,0:T(8,128)(2,1)S(1)} %broadcast_select_fusion), channel_id=1, source_target_pairs={{0,256},{256,0},{1,257},{257,1},{2,258},{258,2},{3,259},{259,3},{4... | collective-permute-start | bytes 1179656 | tf_op jit(solution)/shard_map/ppermute | solution.py:30
  104.5 8.1 %all-to-all-done.1.arrived_ref = bf16[32,24,128]{2,1,0:T(8,128)(2,1)S(1)} async-done(((bf16[32,24,128]{2,1,0:T(8,128)(2,1)}), bf16[32,24,128]{2,1,0:T(8,128)(2,1)S(1)}, u32[]{:S(2)}, u32[]{:S(2)}) %all-to-all-start.1) | async-done | bytes 196640 | tf_op jit(solution)/shard_map/all_to_all | solution.py:289
  112.7 13.6 %all_to_all.21.arrived_ref = bf16[16,32,128]{2,1,0:T(8,128)(2,1)S(1)} all-to-all(bf16[16,32,128]{2,1,0:T(8,128)(2,1)S(1)} %shard_map.95), channel_id=1, replica_groups=mesh['section'=2,'sy'=8,'sx'=8,'mb'=4] {'section','sy'}, dimensions={0} | all-to-all | bytes 262144 | tf_op jit(solution)/shard_map/all_to_all | solution.py:289
  126.2 0.8 shard_map.96
  127.0 3.9 %all-to-all-start.3 = ((bf16[32,16,128]{2,1,0:T(8,128)(2,1)}), bf16[32,16,128]{2,1,0:T(8,128)(2,1)S(1)}, u32[]{:S(2)}, u32[]{:S(2)}) async-start(bf16[32,16,128]{2,1,0:T(8,128)(2,1)} %shard_map.96), calls=%async_computation.3 | async-start | bytes 262144 | tf_op jit(solution)/shard_map/all_to_all | solution.py:289
  130.9 1.1 maximum_select_fusion.1
  131.9 8.3 %all-to-all-done.3.arrived_ref = bf16[32,16,128]{2,1,0:T(8,128)(2,1)S(1)} async-done(((bf16[32,16,128]{2,1,0:T(8,128)(2,1)}), bf16[32,16,128]{2,1,0:T(8,128)(2,1)S(1)}, u32[]{:S(2)}, u32[]{:S(2)}) %all-to-all-start.3) | async-done | bytes 131104 | tf_op jit(solution)/shard_map/all_to_all | solution.py:289
  140.3 0.7 shard_map.97
  (24 shorter events, 0.3 us)
Async XLA Ops:
  7.2 24.9 %copy-start = (bf16[1,64,64,128]{3,2,1,0:T(8,128)(2,1)S(1)}, bf16[1,64,64,128]{3,2,1,0:T(8,128)(2,1)}, u32[]{:S(2)}) copy-start(bf16[1,64,64,128]{3,2,1,0:T(8,128)(2,1)} %param.7) | copy-start | bytes 3145732
  7.2 69.1 %all-gather.2.cloned.1.call-start = ((), (), s32[]{:S(2)}) async-start(), calls=%async_computation.4 | async-start | bytes 5640192 | tf_op jit(solution)/shard_map/all_gather | solution.py:221
  32.0 3.1 %copy-start.4 = (f32[1,1,384]{2,1,0:T(1,128)S(1)}, f32[1,1,384]{2,1,0:T(1,128)}, u32[]{:S(2)}) copy-start(f32[1,1,384]{2,1,0:T(1,128)} %param.10) | copy-start | bytes 4612
  32.0 9.5 %copy-start.2 = (bf16[1,32,32,256]{3,2,1,0:T(8,128)(2,1)S(1)}, bf16[1,32,32,256]{3,2,1,0:T(8,128)(2,1)}, u32[]{:S(2)}) copy-start(bf16[1,32,32,256]{3,2,1,0:T(8,128)(2,1)} %param.12) | copy-start | bytes 1572868
  33.9 7.8 %collective-permute-start = (bf16[9,32,384]{2,1,0:T(8,128)(2,1)S(1)}, bf16[9,32,384]{2,1,0:T(8,128)(2,1)S(1)}, u32[]{:S(2)}, u32[]{:S(2)}) collective-permute-start(bf16[9,32,384]{2,1,0:T(8,128)(2,1)S(1)} %slice_select_fusion), channel_id=1, source_target_pairs={{0,32},{32,64},{64,96},{96,128},{128,160},{160,192},{192,224},{288... | collective-permute-start | bytes 663560 | tf_op jit(solution)/shard_map/ppermute | solution.py:238
  35.2 11.5 %collective-permute-start.3 = (f32[384]{0:T(512)S(1)}, f32[384]{0:T(512)S(1)}, u32[]{:S(2)}, u32[]{:S(2)}) collective-permute-start(f32[384]{0:T(512)S(1)} %reduce), channel_id=1, source_target_pairs={{0,256},{256,0},{1,257},{257,1},{2,258},{258,2},{3,259},{259,3},{4... | collective-permute-start | bytes 4616 | tf_op jit(solution)/shard_map/ppermute | solution.py:30
  41.6 4.8 %copy-start.3 = (s32[1,32,32]{2,1,0:T(8,128)S(1)}, s32[1,32,32]{2,1,0:T(8,128)}, u32[]{:S(2)}) copy-start(s32[1,32,32]{2,1,0:T(8,128)} %param.13) | copy-start | bytes 12292
  42.9 10.1 %collective-permute-start.1 = (bf16[34,9,384]{2,1,0:T(8,128)(2,1)}, bf16[34,9,384]{2,1,0:T(8,128)(2,1)S(1)}, u32[]{:S(2)}, u32[]{:S(2)}) collective-permute-start(bf16[34,9,384]{2,1,0:T(8,128)(2,1)} %get-tuple-element.32), channel_id=1, source_target_pairs={{0,4},{4,8},{8,12},{12,16},{16,20},{20,24},{24,28},{1,5},{5,9},{9,... | collective-permute-start | bytes 705032 | tf_op jit(solution)/shard_map/ppermute | solution.py:246
  45.1 11.8 %collective-permute-start.2 = (bf16[34,9,384]{2,1,0:T(8,128)(2,1)}, bf16[34,9,384]{2,1,0:T(8,128)(2,1)}, u32[]{:S(2)}, u32[]{:S(2)}) collective-permute-start(bf16[34,9,384]{2,1,0:T(8,128)(2,1)} %get-tuple-element.33), channel_id=1, source_target_pairs={{4,0},{8,4},{12,8},{16,12},{20,16},{24,20},{28,24},{5,1},{9,5},{13... | collective-permute-start | bytes 705032 | tf_op jit(solution)/shard_map/ppermute | solution.py:247
  68.6 7.7 %copy-start.1 = (bf16[384,256]{1,0:T(8,128)(2,1)S(1)}, bf16[384,256]{1,0:T(8,128)(2,1)}, u32[]{:S(2)}) copy-start(bf16[384,256]{1,0:T(8,128)(2,1)} %head_ref) | copy-start | bytes 589828
  92.0 20.6 %all-to-all-start.1 = ((bf16[32,24,128]{2,1,0:T(8,128)(2,1)}), bf16[32,24,128]{2,1,0:T(8,128)(2,1)S(1)}, u32[]{:S(2)}, u32[]{:S(2)}) async-start(bf16[32,24,128]{2,1,0:T(8,128)(2,1)} %get-tuple-element.23), calls=%async_computation.1 | async-start | bytes 393216 | tf_op jit(solution)/shard_map/all_to_all | solution.py:289
  102.0 28.8 %collective-permute-start.4 = (bf16[16,32,384]{2,1,0:T(8,128)(2,1)S(1)}, bf16[16,32,384]{2,1,0:T(8,128)(2,1)S(1)}, u32[]{:S(2)}, u32[]{:S(2)}) collective-permute-start(bf16[16,32,384]{2,1,0:T(8,128)(2,1)S(1)} %broadcast_select_fusion), channel_id=1, source_target_pairs={{0,256},{256,0},{1,257},{257,1},{2,258},{258,2},{3,259},{259,3},{4... | collective-permute-start | bytes 1179656 | tf_op jit(solution)/shard_map/ppermute | solution.py:30
  127.0 13.3 %all-to-all-start.3 = ((bf16[32,16,128]{2,1,0:T(8,128)(2,1)}), bf16[32,16,128]{2,1,0:T(8,128)(2,1)S(1)}, u32[]{:S(2)}, u32[]{:S(2)}) async-start(bf16[32,16,128]{2,1,0:T(8,128)(2,1)} %shard_map.96), calls=%async_computation.3 | async-start | bytes 262144 | tf_op jit(solution)/shard_map/all_to_all | solution.py:289
Sparse Core Ops, SparseCore 0:
  32.1 44.0 all-gather.1

commit v6 on v5

--- a/solution.py
+++ b/solution.py
@@ -11,15 +11,6 @@
 SECTION_FACTOR = 8
 
 
-def norm_gelu(activations, gain):
-    values = activations.astype(jnp.float32)
-    center = jnp.mean(values, axis=-1, keepdims=True)
-    offset = values - center
-    spread = jnp.mean(offset * offset, axis=-1, keepdims=True)
-    normed = offset * lax.rsqrt(spread + 1e-05) * gain
-    return jax.nn.gelu(normed, approximate=False).astype(jnp.bfloat16)
-
-
 def copies_to(block, axes, count):
     return lax.all_to_all(
         jnp.broadcast_to(block[None], (count,) + block.shape), axes, split_axis=0, concat_axis=0, tiled=True
@@ -28,10 +19,6 @@
 
 def swap(block):
     return lax.ppermute(block, "section", [(0, 1), (1, 0)])
-
-
-def columns_of(padded, wide, step):
-    return jnp.concatenate([padded[:, j * step : j * step + wide] for j in range(3)], axis=2)
 
 
 def erf(value):
@@ -57,7 +44,7 @@
 def layers_kernel(
     sizes,
     stacked_hbm,
-    center_ref,
+    center_hbm,
     weights_ref,
     gain_ref,
     head_ref,
@@ -68,10 +55,10 @@
     packed_ref,
     loss_ref,
     stacked_ref,
+    center_ref,
     weight_0,
     weight_1,
     hidden_ref,
-    gradient_ref,
     sem_s,
     sem_w,
 ):
@@ -95,6 +82,8 @@
     fetch_0.start()
     for t in range(1, tall // band):
         strip(t).start()
+    fetch_center = pltpu.make_async_copy(center_hbm, center_ref, sem_w.at[2])
+    fetch_center.start()
     fetch_1.start()
 
     row_start = lax.axis_index("sy") * side + section * half - far
@@ -112,6 +101,8 @@
             weight_0[...],
             preferred_element_type=jnp.float32,
         )
+        if t == 0:
+            fetch_center.wait()
         total = total.reshape(band, wide, channels) + center_ref[t * band : (t + 1) * band].astype(jnp.float32)
         values = total.astype(jnp.bfloat16).astype(jnp.float32)
         if far <= t * band < far + half:
@@ -146,22 +137,24 @@
     picked = jnp.sum(jnp.where(hit, shifted, 0.0), axis=1, keepdims=True)
     loss = jnp.sum(jnp.log(exp_total) - picked, axis=0, keepdims=True)
     delta = (exp_terms / exp_total - hit.astype(jnp.float32)).astype(jnp.bfloat16)
-    gradient_ref[...] = lax.dot_general(
+    gradient = lax.dot_general(
         flat, delta, (((0,), (0,)), ((), ())), preferred_element_type=jnp.float32
     )
     loss_ref[...] = jnp.broadcast_to(loss, loss_ref.shape)
-    piece = packed_ref.shape[1] // 2
-    across = channels // (2 * piece)
-    for s in range(slots):
-        row, lane = (s % across) * piece, (s // across) * 128
-        chunk = jnp.concatenate(
-            [
-                gradient_ref[h * channels // 2 + row : h * channels // 2 + row + piece, lane : lane + 128]
-                for h in range(2)
-            ],
-            axis=0,
+    deep = packed_ref.shape[1]
+    middle = channels // 2
+    across = middle // deep
+    left = lax.broadcasted_iota(jnp.int32, (middle, 128), 1) < 64
+    for q in range(bins // 128):
+        upper = gradient[:middle, q * 128 : (q + 1) * 128]
+        lower = gradient[middle:, q * 128 : (q + 1) * 128]
+        pair = (
+            jnp.where(left, upper, pltpu.roll(lower, 64, 1)),
+            jnp.where(left, pltpu.roll(upper, 64, 1), lower),
         )
-        packed_ref[s] = chunk.astype(jnp.bfloat16)
+        for p in range(2):
+            for r in range(across):
+                packed_ref[(2 * q + p) * across + r] = pair[p][r * deep : (r + 1) * deep].astype(jnp.bfloat16)
 
 
 def spread_kernel(arrived_ref, loss_ref, copies_ref):
@@ -173,27 +166,61 @@
 def share_kernel(arrived_ref, copies_ref):
     total = jnp.sum(arrived_ref[...].astype(jnp.float32), axis=0)
     deep = total.shape[0] - 8
-    piece = deep // 2
-    values, loss = total[:deep], total[deep : deep + 1]
+    values, loss = total[:deep], total[deep : deep + 8]
     squares = jnp.sum(jnp.sum(values * values, axis=1, keepdims=True), axis=0, keepdims=True)
-    squares = jnp.broadcast_to(squares, (1, 128))
-    own = jnp.where(lax.axis_index("section") == 0, values[:piece], values[piece:])
-    rest = copies_ref.shape[1] - piece
-    below = jnp.where(lax.broadcasted_iota(jnp.int32, (rest, 128), 0) == 0, squares, loss)
-    block = jnp.concatenate([own, below], axis=0).astype(jnp.bfloat16)
-    copies_ref[...] = jnp.broadcast_to(block[None], copies_ref.shape)
+    turned = pltpu.roll(values, 64, 1)
+    first = lax.axis_index("section") == 0
+    own_left = jnp.where(first, values, turned)
+    own_right = jnp.where(first, turned, values)
+    tail = jnp.where(lax.broadcasted_iota(jnp.int32, (8, 128), 0) == 0, squares, loss)
+    left = lax.broadcasted_iota(jnp.int32, (16, 128), 1) < 64
+    block = jnp.where(left, own_left[:16], jnp.concatenate([own_right[16:deep], tail], axis=0))
+    copies_ref[...] = jnp.broadcast_to(block.astype(jnp.bfloat16)[None], copies_ref.shape)
 
 
 def finish_kernel(sizes, arrived_ref, step_ref, loss_ref):
-    piece, entries, cells = sizes
+    entries, cells = sizes
     arrived = arrived_ref[...].astype(jnp.float32)
-    tails = jnp.sum(arrived, axis=0)
-    scale = lax.rsqrt(tails[piece : piece + 1] * (1.0 / entries) + 1e-06)
-    loss_ref[...] = tails[piece + 1 : piece + 2] * (1.0 / cells)
-    across = step_ref.shape[0] // piece
-    for s in range(arrived_ref.shape[0]):
-        row, lane = (s % across) * piece, (s // across) * 128
-        step_ref[row : row + piece, lane : lane + 128] = arrived[s, :piece] * scale
+    tails = jnp.sum(arrived[:, 8:], axis=0)
+    scale = lax.rsqrt(tails[0:1, 127:128] * (1.0 / entries) + 1e-06)
+    loss_ref[...] = jnp.broadcast_to(tails[1:2, 127:128] * (1.0 / cells), loss_ref.shape)
+    deep = 24
+    across = step_ref.shape[0] // deep
+    left = lax.broadcasted_iota(jnp.int32, (deep, 128), 1) < 64
+
+    def piece(s):
+        block = arrived[s]
+        return jnp.concatenate([block, pltpu.roll(block[:8], 64, 1)], axis=0)
+
+    for q in range(step_ref.shape[1] // 128):
+        for r in range(across):
+            right = pltpu.roll(piece((2 * q + 1) * across + r), 64, 1)
+            both = jnp.where(left, piece(2 * q * across + r), right) * scale
+            step_ref[r * deep : (r + 1) * deep, q * 128 : (q + 1) * 128] = both
+
+
+def window_kernel(sizes, left_ref, rows_ref, right_ref, gain_ref, stacked_ref, center_ref, grid_ref, active_ref):
+    near, band = sizes
+    rows, side, channels = rows_ref.shape
+    reach = left_ref.shape[1]
+    wide = side + 2 * (reach - near)
+    grid_ref[...] = jnp.zeros(grid_ref.shape, jnp.float32)
+    grid_ref[:, :reach] = left_ref[...].astype(jnp.float32)
+    grid_ref[:, reach : reach + side] = rows_ref[...].astype(jnp.float32)
+    grid_ref[:, reach + side : 2 * reach + side] = right_ref[...].astype(jnp.float32)
+    gain = gain_ref[...].reshape(1, 1, channels)
+    for t in range(rows // band):
+        at = slice(t * band, (t + 1) * band)
+        values = grid_ref[at]
+        offset = values - jnp.mean(values, axis=-1, keepdims=True)
+        spread = jnp.mean(offset * offset, axis=-1, keepdims=True)
+        normed = offset * lax.rsqrt(spread + 1e-05) * gain
+        active_ref[...] = 0.5 * normed * (1.0 + erf(normed * 0.7071067811865476))
+        for j in range(3):
+            stacked_ref[at, :, j * channels : (j + 1) * channels] = active_ref[
+                :, j * near : j * near + wide
+            ].astype(jnp.bfloat16)
+    center_ref[...] = grid_ref[near : rows - near, near : near + wide].astype(jnp.bfloat16)
 
 
 def per_device(
@@ -245,12 +272,22 @@
     backward = [(x + 1, x) for x in range(parts_x - 1)]
     left = lax.ppermute(rows[:, side - reach :], "sx", forward)
     right = lax.ppermute(rows[:, :reach], "sx", backward)
-    haloed = jnp.concatenate([left, rows, right], axis=1)
 
     tall, wide = half + 2 * far, side + 2 * far
     cells = half * side
-    stacked = columns_of(norm_gelu(haloed, gain_0), wide, near)
-    center = haloed[near : near + tall, near : near + wide]
+    columns = -(-(side + 2 * reach) // 8) * 8
+    stacked, center = pl.pallas_call(
+        functools.partial(window_kernel, (near, 2)),
+        out_shape=(
+            jax.ShapeDtypeStruct((tall + 2 * near, wide, 3 * channels), jnp.bfloat16),
+            jax.ShapeDtypeStruct((tall, wide, channels), jnp.bfloat16),
+        ),
+        scratch_shapes=[
+            pltpu.VMEM((tall + 2 * near, columns, channels), jnp.float32),
+            pltpu.VMEM((2, columns, channels), jnp.float32),
+        ],
+        compiler_params=pltpu.CompilerParams(vmem_limit_bytes=32 * 2**20),
+    )(left, rows, right, gain_0.reshape(1, channels))
     prior = lax.dynamic_slice_in_dim(prior_logits[0], section * half, half, axis=0).reshape(cells, bins)
     target = lax.dynamic_slice_in_dim(target_bins[0], section * half, half, axis=0).reshape(cells, 1)
     slots = parts_x * parts_b
@@ -266,16 +303,16 @@
             jax.ShapeDtypeStruct((slots, deep, 128), jnp.bfloat16),
             jax.ShapeDtypeStruct((8, 128), jnp.float32),
         ),
-        in_specs=[anywhere, vmem, anywhere, vmem, vmem, vmem, vmem],
+        in_specs=[anywhere, anywhere, anywhere, vmem, vmem, vmem, vmem],
         out_specs=(vmem, vmem, vmem, vmem),
         scratch_shapes=[
             pltpu.VMEM((tall + 2 * near, wide, taps), jnp.bfloat16),
+            pltpu.VMEM((tall, wide, channels), jnp.bfloat16),
             pltpu.VMEM((3 * taps, channels), jnp.bfloat16),
             pltpu.VMEM((3 * taps, channels), jnp.bfloat16),
             pltpu.VMEM((tall, side, taps), jnp.bfloat16),
-            pltpu.VMEM((channels, bins), jnp.float32),
             pltpu.SemaphoreType.DMA((tall // 8,)),
-            pltpu.SemaphoreType.DMA((2,)),
+            pltpu.SemaphoreType.DMA((3,)),
         ],
         compiler_params=pltpu.CompilerParams(vmem_limit_bytes=52 * 2**20),
         cost_estimate=pl.CostEstimate(
@@ -295,12 +332,12 @@
     )(packed, loss)
     packed = exchange(packed, ("section", "sy"))
     packed = pl.pallas_call(
-        share_kernel, out_shape=jax.ShapeDtypeStruct((slots, deep // 2 + 4, 128), jnp.bfloat16), compiler_params=small
+        share_kernel, out_shape=jax.ShapeDtypeStruct((slots, 16, 128), jnp.bfloat16), compiler_params=small
     )(packed)
     packed = exchange(packed, ("sx", "mb"))
     head_step, loss = pl.pallas_call(
         functools.partial(
-            finish_kernel, (deep // 2, channels * bins, parts_b * parts_y * parts_x * side * side)
+            finish_kernel, (channels * bins, parts_b * parts_y * parts_x * side * side)
         ),
         out_shape=(
             jax.ShapeDtypeStruct((channels // 2, bins), jnp.float32),

time: 149 us -> 149 us (level)
  other arithmetic: 12.7 us -> 1.31 us
  waiting for transfers between devices: 32.2 us -> 37.9 us
  Pallas kernels: 17.3 us -> 22.4 us
    convert_element_type x1 -> x0, other arithmetic: 6.8 us -> none  [norm_gelu(): return jax.nn.gelu(normed, approximate=False).astype(jnp.bfloat16)]
    all_gather x1, waiting for transfers between devices: 5.57 us -> 11.3 us  [per_device(): lax.all_gather(strip.reshape(parts_x * shard.shape[0], channels), ('secti...]
    pallas_call x2 -> x3, Pallas kernels: 1.52 us -> 6.92 us  [the longest x1 5.3 us: per_device(): pl.pallas_call(functools.partial(window_kernel, (near, 2)), out_shape=(ja...]
    unnamed x10 -> x14, local copies, waits for them, and re-layouts: 0.03 us -> 2.9 us
    reduce_sum x2 -> x0, other arithmetic: 2.46 us -> none  [the longest x1 1.61 us: norm_gelu(): center = jnp.mean(values, axis=-1, keepdims=True)]
    slice x3 -> x1, local copies, waits for them, and re-layouts: 3.4 us -> 1.02 us  [per_device(): right = lax.ppermute(rows[:, :reach], 'sx', backward)]
    concatenate x1 -> x0, other arithmetic: 2.1 us -> none  [columns_of(): jnp.concatenate([padded[:, j * step:j * step + wide] for j in range(3)],...]
  transfers between devices with their start and end apart: 8 -> 8, of which waited for: 5 -> 5; matrix products, arithmetic and copies ran while one was open for 12% -> 3% of each run, Pallas kernels for 1% -> 4%
where the time goes in v6:
time: 149 us; the launch traced here: 148 us
  waiting for transfers between devices  37.9 us (25%)
  blocking collectives  36.6 us (25%)
  starting transfers between devices  27.3 us (18%)
  Pallas kernels  22.4 us (15%)
  between operations  14.3 us (10%)
  local copies, waits for them, and re-layouts  6.06 us (4%)
  matrix products  1.7 us (1%)
    all_to_all x1, blocking collectives, copies_to(): lax.all_to_all(jnp.broadcast_to(block[None], (count,) + block.shape), axe...  23 us
    all_to_all x2, waiting for transfers between devices, exchange(): return lax.all_to_all(blocks, axes, split_axis=0, concat_axis=0, tiled=True)  16.5 us
    pallas_call x1, Pallas kernels, per_device(): pl.pallas_call(functools.partial(layers_kernel, (far, half, side, 8, slot...  15.4 us
    all_to_all x2, starting transfers between devices, exchange(): return lax.all_to_all(blocks, axes, split_axis=0, concat_axis=0, tiled=True)  13.8 us
    all_to_all x1, blocking collectives, exchange(): return lax.all_to_all(blocks, axes, split_axis=0, concat_axis=0, tiled=True)  13.6 us
    all_gather x1, waiting for transfers between devices, per_device(): lax.all_gather(strip.reshape(parts_x * shard.shape[0], channels), ('secti...  11.3 us
    ppermute x2, starting transfers between devices, swap(): return lax.ppermute(block, 'section', [(0, 1), (1, 0)])  8.76 us
    ppermute x1, waiting for transfers between devices, per_device(): left = lax.ppermute(rows[:, side - reach:], 'sx', forward)  6.28 us
  transfers between devices with their start and end apart: 8, of which 5 were waited for; matrix products, arithmetic and copies ran while one was open for 3% of the time, Pallas kernels for 4%

profile of v6, /device:TPU:1, one launch (start us, length us, event | category | flops | bytes accessed | tf_op | source)
XLA Modules:
  0.0 147.6 jit_solution(10114450033609736455)
XLA Ops:
  7.2 0.0 copy-start
  7.2 0.0 all-gather.2.cloned.1.call-start
  7.2 0.9 broadcast_in_dim.9
  8.1 23.0 %all_to_all.20 = bf16[8,54,384]{2,1,0:T(8,128)(2,1)S(1)} all-to-all(bf16[8,54,384]{2,1,0:T(8,128)(2,1)S(1)} %broadcast_in_dim.9), channel_id=1, replica_groups=mesh['section'=2,'sy'=8,'sx'=8,'mb'=4] {'sx'}, dimensions={0} | all-to-all | bytes 663552 | tf_op jit(solution)/shard_map/all_to_all | solution.py:15
  31.2 0.8 reshape.86
  32.0 0.0 all-gather.2.cloned.1.call-update
  32.0 1.7 %fusion = bf16[32,32,384]{2,1,0:T(8,128)(2,1)S(1)} fusion(bf16[2,2,128,384,1]{3,2,1,4,0:T(8,128)(2,1)} %bitcast.28, bf16[32,2,32,2,128]{4,3,2,1,0:T(2,128)(2,1)S(1)} %bitcast.22), kind=kOutput, calls=%fused_computation.1 | convolution fusion | flops 403046400 | bytes 2228224 | tf_op jit(solution)/shard_map/apbqc,pqco->abo/dot_general | solution.py:257
  33.8 1.3 collective-permute-start
  35.1 6.3 %collective-permute-start.3 = (f32[384]{0:T(512)S(1)}, f32[384]{0:T(512)S(1)}, u32[]{:S(2)}, u32[]{:S(2)}) collective-permute-start(f32[384]{0:T(512)S(1)} %reduce), channel_id=1, source_target_pairs={{0,256},{256,0},{1,257},{257,1},{2,258},{258,2},{3,259},{259,3},{4... | collective-permute-start | bytes 4616 | tf_op jit(solution)/shard_map/ppermute | solution.py:21
  41.5 0.1 fusion.3
  41.6 0.2 maximum_select_fusion.rows_ref
  41.8 1.0 fusion.2
  42.8 2.2 %collective-permute-start.1 = (bf16[34,9,384]{2,1,0:T(8,128)(2,1)}, bf16[34,9,384]{2,1,0:T(8,128)(2,1)S(1)}, u32[]{:S(2)}, u32[]{:S(2)}) collective-permute-start(bf16[34,9,384]{2,1,0:T(8,128)(2,1)} %get-tuple-element.32), channel_id=1, source_target_pairs={{0,4},{4,8},{8,12},{12,16},{16,20},{20,24},{24,28},{1,5},{5,9},{9,... | collective-permute-start | bytes 705032 | tf_op jit(solution)/shard_map/ppermute | solution.py:273
  45.0 1.3 collective-permute-start.2
  46.4 0.3 reshape.92.target_ref
  46.7 6.3 %collective-permute-done.1.left_ref = bf16[34,9,384]{2,1,0:T(8,128)(2,1)S(1)} collective-permute-done((bf16[34,9,384]{2,1,0:T(8,128)(2,1)}, bf16[34,9,384]{2,1,0:T(8,128)(2,1)S(1)}, u32[]{:S(2)}, u32[]{:S(2)}) %collective-permute-start.1) | collective-permute-done | bytes 235040 | tf_op jit(solution)/shard_map/ppermute | solution.py:273
  53.0 3.9 %collective-permute-done.2.right_ref = bf16[34,9,384]{2,1,0:T(8,128)(2,1)S(1)} collective-permute-done((bf16[34,9,384]{2,1,0:T(8,128)(2,1)}, bf16[34,9,384]{2,1,0:T(8,128)(2,1)S(1)}, u32[]{:S(2)}, u32[]{:S(2)}) %collective-permute-start.2) | collective-permute-done | bytes 235040 | tf_op jit(solution)/shard_map/ppermute | solution.py:274
  56.8 5.3 %shard_map.94 = (bf16[34,48,1152]{2,1,0:T(8,128)(2,1)S(1)}, bf16[32,48,384]{2,1,0:T(8,128)(2,1)S(1)}) custom-call(bf16[34,9,384]{2,1,0:T(8,128)(2,1)S(1)} %collective-permute-done.1.left_ref, bf16[34,32,384]{2,1,0:T(8,128)(2,1)S(1)} %maximum_select_fusion.rows_ref, bf16[34,9,384]{2,1,0:T(8,128)(2,1)S(1)} %collective-permute-done.2.right_ref, ...), custom_call_target="tpu_custom_call" | custom-call | tf_op jit(solution)/shard_map/pallas_call | solution.py:279
  62.1 1.9 %copy-done.1 = bf16[34,48,1152]{2,1,0:T(8,128)(2,1)} copy-done((bf16[34,48,1152]{2,1,0:T(8,128)(2,1)}, bf16[34,48,1152]{2,1,0:T(8,128)(2,1)S(1)}, u32[]{:S(2)}) %copy-start.1) | copy-done | bytes 3760152
  64.0 1.0 copy-done.2
  65.0 11.3 %all-gather.2.cloned.1.call-done.weights_ref = bf16[6912,384]{1,0:T(8,128)(2,1)} async-done(((bf16[432,384]{1,0:T(8,128)(2,1)}), bf16[6912,384]{1,0:T(8,128)(2,1)}) %all-gather.2.cloned.1.call-update) | async-done | bytes 5308432 | tf_op jit(solution)/shard_map/all_gather | solution.py:248
  76.3 15.4 %shard_map.95 = (bf16[16,32,384]{2,1,0:T(8,128)(2,1)S(1)}, bf16[16,32,384]{2,1,0:T(8,128)(2,1)S(1)}, bf16[32,24,128]{2,1,0:T(8,128)(2,1)}, f32[8,128]{1,0:T(8,128)S(1)}) custom-call(bf16[34,48,1152]{2,1,0:T(8,128)(2,1)} %copy-done.1, bf16[32,48,384]{2,1,0:T(8,128)(2,1)} %copy-done.2, bf16[6912,384]{1,0:T(8,128)(2,1)} %all-gather.2.cloned.1.call-done.weights_ref, ...), custom_call_target="tpu_custom_call" | custom-call | flops 5435817984 | bytes 5308416 | tf_op jit(solution)/shard_map/pallas_call | solution.py:298
  91.7 9.9 %all-to-all-start.1 = ((bf16[32,24,128]{2,1,0:T(8,128)(2,1)}), bf16[32,24,128]{2,1,0:T(8,128)(2,1)S(1)}, u32[]{:S(2)}, u32[]{:S(2)}) async-start(bf16[32,24,128]{2,1,0:T(8,128)(2,1)} %get-tuple-element.27), calls=%async_computation.1 | async-start | bytes 393216 | tf_op jit(solution)/shard_map/all_to_all | solution.py:326
  101.6 0.1 broadcast_select_fusion
  101.6 2.4 %collective-permute-start.4 = (bf16[16,32,384]{2,1,0:T(8,128)(2,1)S(1)}, bf16[16,32,384]{2,1,0:T(8,128)(2,1)S(1)}, u32[]{:S(2)}, u32[]{:S(2)}) collective-permute-start(bf16[16,32,384]{2,1,0:T(8,128)(2,1)S(1)} %broadcast_select_fusion), channel_id=1, source_target_pairs={{0,256},{256,0},{1,257},{257,1},{2,258},{258,2},{3,259},{259,3},{4... | collective-permute-start | bytes 1179656 | tf_op jit(solution)/shard_map/ppermute | solution.py:21
  104.1 8.1 %all-to-all-done.1.arrived_ref = bf16[32,24,128]{2,1,0:T(8,128)(2,1)S(1)} async-done(((bf16[32,24,128]{2,1,0:T(8,128)(2,1)}), bf16[32,24,128]{2,1,0:T(8,128)(2,1)S(1)}, u32[]{:S(2)}, u32[]{:S(2)}) %all-to-all-start.1) | async-done | bytes 196640 | tf_op jit(solution)/shard_map/all_to_all | solution.py:326
  112.3 13.6 %all_to_all.21.arrived_ref = bf16[16,32,128]{2,1,0:T(8,128)(2,1)S(1)} all-to-all(bf16[16,32,128]{2,1,0:T(8,128)(2,1)S(1)} %shard_map.96), channel_id=1, replica_groups=mesh['section'=2,'sy'=8,'sx'=8,'mb'=4] {'section','sy'}, dimensions={0} | all-to-all | bytes 262144 | tf_op jit(solution)/shard_map/all_to_all | solution.py:326
  125.8 0.8 shard_map.97
  126.6 3.9 %all-to-all-start.3 = ((bf16[32,16,128]{2,1,0:T(8,128)(2,1)}), bf16[32,16,128]{2,1,0:T(8,128)(2,1)S(1)}, u32[]{:S(2)}, u32[]{:S(2)}) async-start(bf16[32,16,128]{2,1,0:T(8,128)(2,1)} %shard_map.97), calls=%async_computation.3 | async-start | bytes 262144 | tf_op jit(solution)/shard_map/all_to_all | solution.py:326
  130.5 1.1 maximum_select_fusion.1
  131.5 8.3 %all-to-all-done.3.arrived_ref = bf16[32,16,128]{2,1,0:T(8,128)(2,1)S(1)} async-done(((bf16[32,16,128]{2,1,0:T(8,128)(2,1)}), bf16[32,16,128]{2,1,0:T(8,128)(2,1)S(1)}, u32[]{:S(2)}, u32[]{:S(2)}) %all-to-all-start.3) | async-done | bytes 131104 | tf_op jit(solution)/shard_map/all_to_all | solution.py:326
  139.9 0.8 shard_map.98
  (22 shorter events, 0.2 us)
Async XLA Ops:
  7.2 24.9 %copy-start = (bf16[1,64,64,128]{3,2,1,0:T(8,128)(2,1)S(1)}, bf16[1,64,64,128]{3,2,1,0:T(8,128)(2,1)}, u32[]{:S(2)}) copy-start(bf16[1,64,64,128]{3,2,1,0:T(8,128)(2,1)} %param.7) | copy-start | bytes 3145732
  7.2 69.1 %all-gather.2.cloned.1.call-start = ((), (), s32[]{:S(2)}) async-start(), calls=%async_computation.4 | async-start | bytes 5640192 | tf_op jit(solution)/shard_map/all_gather | solution.py:248
  31.2 3.9 %copy-start.6 = (f32[1,1,384]{2,1,0:T(1,128)S(1)}, f32[1,1,384]{2,1,0:T(1,128)}, u32[]{:S(2)}) copy-start(f32[1,1,384]{2,1,0:T(1,128)} %param.10) | copy-start | bytes 4612
  31.2 10.3 %copy-start.4 = (bf16[1,32,32,256]{3,2,1,0:T(8,128)(2,1)S(1)}, bf16[1,32,32,256]{3,2,1,0:T(8,128)(2,1)}, u32[]{:S(2)}) copy-start(bf16[1,32,32,256]{3,2,1,0:T(8,128)(2,1)} %param.12) | copy-start | bytes 1572868
  33.8 12.6 %copy-start.5 = (s32[1,32,32]{2,1,0:T(8,128)S(1)}, s32[1,32,32]{2,1,0:T(8,128)}, u32[]{:S(2)}) copy-start(s32[1,32,32]{2,1,0:T(8,128)} %param.13) | copy-start | bytes 12292
  33.8 7.8 %collective-permute-start = (bf16[9,32,384]{2,1,0:T(8,128)(2,1)S(1)}, bf16[9,32,384]{2,1,0:T(8,128)(2,1)S(1)}, u32[]{:S(2)}, u32[]{:S(2)}) collective-permute-start(bf16[9,32,384]{2,1,0:T(8,128)(2,1)S(1)} %slice_select_fusion), channel_id=1, source_target_pairs={{0,32},{32,64},{64,96},{96,128},{128,160},{160,192},{192,224},{288... | collective-permute-start | bytes 663560 | tf_op jit(solution)/shard_map/ppermute | solution.py:265
  35.1 11.5 %collective-permute-start.3 = (f32[384]{0:T(512)S(1)}, f32[384]{0:T(512)S(1)}, u32[]{:S(2)}, u32[]{:S(2)}) collective-permute-start(f32[384]{0:T(512)S(1)} %reduce), channel_id=1, source_target_pairs={{0,256},{256,0},{1,257},{257,1},{2,258},{258,2},{3,259},{259,3},{4... | collective-permute-start | bytes 4616 | tf_op jit(solution)/shard_map/ppermute | solution.py:21
  41.5 34.8 %copy-start.3 = (bf16[384,256]{1,0:T(8,128)(2,1)S(1)}, bf16[384,256]{1,0:T(8,128)(2,1)}, u32[]{:S(2)}) copy-start(bf16[384,256]{1,0:T(8,128)(2,1)} %head_ref) | copy-start | bytes 589828
  42.8 10.1 %collective-permute-start.1 = (bf16[34,9,384]{2,1,0:T(8,128)(2,1)}, bf16[34,9,384]{2,1,0:T(8,128)(2,1)S(1)}, u32[]{:S(2)}, u32[]{:S(2)}) collective-permute-start(bf16[34,9,384]{2,1,0:T(8,128)(2,1)} %get-tuple-element.32), channel_id=1, source_target_pairs={{0,4},{4,8},{8,12},{12,16},{16,20},{20,24},{24,28},{1,5},{5,9},{9,... | collective-permute-start | bytes 705032 | tf_op jit(solution)/shard_map/ppermute | solution.py:273
  45.0 11.8 %collective-permute-start.2 = (bf16[34,9,384]{2,1,0:T(8,128)(2,1)}, bf16[34,9,384]{2,1,0:T(8,128)(2,1)S(1)}, u32[]{:S(2)}, u32[]{:S(2)}) collective-permute-start(bf16[34,9,384]{2,1,0:T(8,128)(2,1)} %get-tuple-element.31), channel_id=1, source_target_pairs={{4,0},{8,4},{12,8},{16,12},{20,16},{24,20},{28,24},{5,1},{9,5},{13... | collective-permute-start | bytes 705032 | tf_op jit(solution)/shard_map/ppermute | solution.py:274
  62.1 1.9 %copy-start.1 = (bf16[34,48,1152]{2,1,0:T(8,128)(2,1)}, bf16[34,48,1152]{2,1,0:T(8,128)(2,1)S(1)}, u32[]{:S(2)}) copy-start(bf16[34,48,1152]{2,1,0:T(8,128)(2,1)S(1)} %get-tuple-element.19.stacked_hbm) | copy-start | bytes 11280388
  64.0 1.0 copy-start.2
  91.7 20.6 %all-to-all-start.1 = ((bf16[32,24,128]{2,1,0:T(8,128)(2,1)}), bf16[32,24,128]{2,1,0:T(8,128)(2,1)S(1)}, u32[]{:S(2)}, u32[]{:S(2)}) async-start(bf16[32,24,128]{2,1,0:T(8,128)(2,1)} %get-tuple-element.27), calls=%async_computation.1 | async-start | bytes 393216 | tf_op jit(solution)/shard_map/all_to_all | solution.py:326
  101.6 28.8 %collective-permute-start.4 = (bf16[16,32,384]{2,1,0:T(8,128)(2,1)S(1)}, bf16[16,32,384]{2,1,0:T(8,128)(2,1)S(1)}, u32[]{:S(2)}, u32[]{:S(2)}) collective-permute-start(bf16[16,32,384]{2,1,0:T(8,128)(2,1)S(1)} %broadcast_select_fusion), channel_id=1, source_target_pairs={{0,256},{256,0},{1,257},{257,1},{2,258},{258,2},{3,259},{259,3},{4... | collective-permute-start | bytes 1179656 | tf_op jit(solution)/shard_map/ppermute | solution.py:21
  126.6 13.3 %all-to-all-start.3 = ((bf16[32,16,128]{2,1,0:T(8,128)(2,1)}), bf16[32,16,128]{2,1,0:T(8,128)(2,1)S(1)}, u32[]{:S(2)}, u32[]{:S(2)}) async-start(bf16[32,16,128]{2,1,0:T(8,128)(2,1)} %shard_map.97), calls=%async_computation.3 | async-start | bytes 262144 | tf_op jit(solution)/shard_map/all_to_all | solution.py:326
Sparse Core Ops, SparseCore 0:
  32.1 44.0 all-gather.1

commit v7 on v6

--- a/solution.py
+++ b/solution.py
@@ -75,14 +75,16 @@
 
     strip(0).start()
 
-    def weights(layer, target, sem):
-        return pltpu.make_async_copy(weights_ref.at[pl.ds(layer * 3 * taps, 3 * taps)], target, sem)
-
-    fetch_0, fetch_1 = weights(0, weight_0, sem_w.at[0]), weights(1, weight_1, sem_w.at[1])
-    fetch_0.start()
+    def third(i):
+        at = pl.ds(i * taps, taps)
+        return pltpu.make_async_copy(weights_ref.at[at], weight_0.at[at], sem_w.at[i])
+
+    fetch_1 = pltpu.make_async_copy(weights_ref.at[pl.ds(3 * taps, 3 * taps)], weight_1, sem_w.at[3])
+    for i in range(3):
+        third(i).start()
     for t in range(1, tall // band):
         strip(t).start()
-    fetch_center = pltpu.make_async_copy(center_hbm, center_ref, sem_w.at[2])
+    fetch_center = pltpu.make_async_copy(center_hbm, center_ref, sem_w.at[4])
     fetch_center.start()
     fetch_1.start()
 
@@ -90,19 +92,26 @@
     column_at = lax.axis_index("sx") * side - far + lax.broadcasted_iota(jnp.int32, (band, wide, 1), 1)
     column_in = (column_at >= 0) & (column_at < side * parts_x)
     gain = gain_ref[...].reshape(1, 1, channels)
-    fetch_0.wait()
+    strip(0).wait()
+    start = jnp.zeros((band * wide, channels), jnp.float32)
+    for i in range(3):
+        third(i).wait()
+        start += jnp.dot(
+            stacked_ref[i : i + band].reshape(band * wide, taps),
+            weight_0[i * taps : (i + 1) * taps],
+            preferred_element_type=jnp.float32,
+        )
+    for t in range(1, tall // band):
+        strip(t).wait()
+    fetch_center.wait()
     for t in range(tall // band):
-        strip(t).wait()
-    for t in range(tall // band):
-        total = jnp.dot(
+        total = start if t == 0 else jnp.dot(
             jnp.concatenate(
                 [stacked_ref[t * band + i : t * band + i + band] for i in range(3)], axis=2
             ).reshape(band * wide, 3 * taps),
             weight_0[...],
             preferred_element_type=jnp.float32,
         )
-        if t == 0:
-            fetch_center.wait()
         total = total.reshape(band, wide, channels) + center_ref[t * band : (t + 1) * band].astype(jnp.float32)
         values = total.astype(jnp.bfloat16).astype(jnp.float32)
         if far <= t * band < far + half:
@@ -312,7 +321,7 @@
             pltpu.VMEM((3 * taps, channels), jnp.bfloat16),
             pltpu.VMEM((tall, side, taps), jnp.bfloat16),
             pltpu.SemaphoreType.DMA((tall // 8,)),
-            pltpu.SemaphoreType.DMA((3,)),
+            pltpu.SemaphoreType.DMA((5,)),
         ],
         compiler_params=pltpu.CompilerParams(vmem_limit_bytes=52 * 2**20),
         cost_estimate=pl.CostEstimate(

time: 149 us -> 148 us (level)
  no operation moved by 1% of the time
where the time goes in v7:
time: 148 us; the launch traced here: 146 us
  waiting for transfers between devices  37.9 us (26%)
  blocking collectives  36.6 us (25%)
  starting transfers between devices  27.3 us (18%)
  Pallas kernels  21.2 us (14%)
  between operations  14.3 us (10%)
  local copies, waits for them, and re-layouts  6.06 us (4%)
  matrix products  1.7 us (1%)
    all_to_all x1, blocking collectives, copies_to(): lax.all_to_all(jnp.broadcast_to(block[None], (count,) + block.shape), axe...  23 us
    all_to_all x2, waiting for transfers between devices, exchange(): return lax.all_to_all(blocks, axes, split_axis=0, concat_axis=0, tiled=True)  16.5 us
    pallas_call x1, Pallas kernels, per_device(): pl.pallas_call(functools.partial(layers_kernel, (far, half, side, 8, slot...  14.3 us
    all_to_all x2, starting transfers between devices, exchange(): return lax.all_to_all(blocks, axes, split_axis=0, concat_axis=0, tiled=True)  13.8 us
    all_to_all x1, blocking collectives, exchange(): return lax.all_to_all(blocks, axes, split_axis=0, concat_axis=0, tiled=True)  13.6 us
    all_gather x1, waiting for transfers between devices, per_device(): lax.all_gather(strip.reshape(parts_x * shard.shape[0], channels), ('secti...  11.3 us
    ppermute x2, starting transfers between devices, swap(): return lax.ppermute(block, 'section', [(0, 1), (1, 0)])  8.76 us
    ppermute x1, waiting for transfers between devices, per_device(): left = lax.ppermute(rows[:, side - reach:], 'sx', forward)  6.28 us
  transfers between devices with their start and end apart: 8, of which 5 were waited for; matrix products, arithmetic and copies ran while one was open for 3% of the time, Pallas kernels for 4%

profile of v7, /device:TPU:1, one launch (start us, length us, event | category | flops | bytes accessed | tf_op | source)
XLA Modules:
  0.0 146.4 jit_solution(3440520953442189947)
XLA Ops:
  7.2 0.0 copy-start
  7.2 0.0 all-gather.2.cloned.1.call-start
  7.2 0.9 broadcast_in_dim.9
  8.1 23.0 %all_to_all.20 = bf16[8,54,384]{2,1,0:T(8,128)(2,1)S(1)} all-to-all(bf16[8,54,384]{2,1,0:T(8,128)(2,1)S(1)} %broadcast_in_dim.9), channel_id=1, replica_groups=mesh['section'=2,'sy'=8,'sx'=8,'mb'=4] {'sx'}, dimensions={0} | all-to-all | bytes 663552 | tf_op jit(solution)/shard_map/all_to_all | solution.py:15
  31.2 0.8 reshape.86
  32.0 0.0 all-gather.2.cloned.1.call-update
  32.0 1.7 %fusion = bf16[32,32,384]{2,1,0:T(8,128)(2,1)S(1)} fusion(bf16[2,2,128,384,1]{3,2,1,4,0:T(8,128)(2,1)} %bitcast.28, bf16[32,2,32,2,128]{4,3,2,1,0:T(2,128)(2,1)S(1)} %bitcast.22), kind=kOutput, calls=%fused_computation.1 | convolution fusion | flops 403046400 | bytes 2228224 | tf_op jit(solution)/shard_map/apbqc,pqco->abo/dot_general | solution.py:266
  33.8 1.3 collective-permute-start
  35.1 6.3 %collective-permute-start.3 = (f32[384]{0:T(512)S(1)}, f32[384]{0:T(512)S(1)}, u32[]{:S(2)}, u32[]{:S(2)}) collective-permute-start(f32[384]{0:T(512)S(1)} %reduce), channel_id=1, source_target_pairs={{0,256},{256,0},{1,257},{257,1},{2,258},{258,2},{3,259},{259,3},{4... | collective-permute-start | bytes 4616 | tf_op jit(solution)/shard_map/ppermute | solution.py:21
  41.5 0.1 fusion.3
  41.6 0.2 maximum_select_fusion.rows_ref
  41.8 1.0 fusion.2
  42.8 2.2 %collective-permute-start.1 = (bf16[34,9,384]{2,1,0:T(8,128)(2,1)}, bf16[34,9,384]{2,1,0:T(8,128)(2,1)S(1)}, u32[]{:S(2)}, u32[]{:S(2)}) collective-permute-start(bf16[34,9,384]{2,1,0:T(8,128)(2,1)} %get-tuple-element.32), channel_id=1, source_target_pairs={{0,4},{4,8},{8,12},{12,16},{16,20},{20,24},{24,28},{1,5},{5,9},{9,... | collective-permute-start | bytes 705032 | tf_op jit(solution)/shard_map/ppermute | solution.py:282
  45.0 1.3 collective-permute-start.2
  46.4 0.3 reshape.92.target_ref
  46.7 6.3 %collective-permute-done.1.left_ref = bf16[34,9,384]{2,1,0:T(8,128)(2,1)S(1)} collective-permute-done((bf16[34,9,384]{2,1,0:T(8,128)(2,1)}, bf16[34,9,384]{2,1,0:T(8,128)(2,1)S(1)}, u32[]{:S(2)}, u32[]{:S(2)}) %collective-permute-start.1) | collective-permute-done | bytes 235040 | tf_op jit(solution)/shard_map/ppermute | solution.py:282
  53.0 3.9 %collective-permute-done.2.right_ref = bf16[34,9,384]{2,1,0:T(8,128)(2,1)S(1)} collective-permute-done((bf16[34,9,384]{2,1,0:T(8,128)(2,1)}, bf16[34,9,384]{2,1,0:T(8,128)(2,1)S(1)}, u32[]{:S(2)}, u32[]{:S(2)}) %collective-permute-start.2) | collective-permute-done | bytes 235040 | tf_op jit(solution)/shard_map/ppermute | solution.py:283
  56.8 5.3 %shard_map.94 = (bf16[34,48,1152]{2,1,0:T(8,128)(2,1)S(1)}, bf16[32,48,384]{2,1,0:T(8,128)(2,1)S(1)}) custom-call(bf16[34,9,384]{2,1,0:T(8,128)(2,1)S(1)} %collective-permute-done.1.left_ref, bf16[34,32,384]{2,1,0:T(8,128)(2,1)S(1)} %maximum_select_fusion.rows_ref, bf16[34,9,384]{2,1,0:T(8,128)(2,1)S(1)} %collective-permute-done.2.right_ref, ...), custom_call_target="tpu_custom_call" | custom-call | tf_op jit(solution)/shard_map/pallas_call | solution.py:288
  62.1 1.9 %copy-done.1 = bf16[34,48,1152]{2,1,0:T(8,128)(2,1)} copy-done((bf16[34,48,1152]{2,1,0:T(8,128)(2,1)}, bf16[34,48,1152]{2,1,0:T(8,128)(2,1)S(1)}, u32[]{:S(2)}) %copy-start.1) | copy-done | bytes 3760152
  64.0 1.0 copy-done.2
  65.0 11.3 %all-gather.2.cloned.1.call-done.weights_ref = bf16[6912,384]{1,0:T(8,128)(2,1)} async-done(((bf16[432,384]{1,0:T(8,128)(2,1)}), bf16[6912,384]{1,0:T(8,128)(2,1)}) %all-gather.2.cloned.1.call-update) | async-done | bytes 5308432 | tf_op jit(solution)/shard_map/all_gather | solution.py:257
  76.3 14.3 %shard_map.95 = (bf16[16,32,384]{2,1,0:T(8,128)(2,1)S(1)}, bf16[16,32,384]{2,1,0:T(8,128)(2,1)S(1)}, bf16[32,24,128]{2,1,0:T(8,128)(2,1)}, f32[8,128]{1,0:T(8,128)S(1)}) custom-call(bf16[34,48,1152]{2,1,0:T(8,128)(2,1)} %copy-done.1, bf16[32,48,384]{2,1,0:T(8,128)(2,1)} %copy-done.2, bf16[6912,384]{1,0:T(8,128)(2,1)} %all-gather.2.cloned.1.call-done.weights_ref, ...), custom_call_target="tpu_custom_call" | custom-call | flops 5435817984 | bytes 5308416 | tf_op jit(solution)/shard_map/pallas_call | solution.py:307
  90.5 9.9 %all-to-all-start.1 = ((bf16[32,24,128]{2,1,0:T(8,128)(2,1)}), bf16[32,24,128]{2,1,0:T(8,128)(2,1)S(1)}, u32[]{:S(2)}, u32[]{:S(2)}) async-start(bf16[32,24,128]{2,1,0:T(8,128)(2,1)} %get-tuple-element.27), calls=%async_computation.1 | async-start | bytes 393216 | tf_op jit(solution)/shard_map/all_to_all | solution.py:335
  100.4 0.1 broadcast_select_fusion
  100.5 2.4 %collective-permute-start.4 = (bf16[16,32,384]{2,1,0:T(8,128)(2,1)S(1)}, bf16[16,32,384]{2,1,0:T(8,128)(2,1)S(1)}, u32[]{:S(2)}, u32[]{:S(2)}) collective-permute-start(bf16[16,32,384]{2,1,0:T(8,128)(2,1)S(1)} %broadcast_select_fusion), channel_id=1, source_target_pairs={{0,256},{256,0},{1,257},{257,1},{2,258},{258,2},{3,259},{259,3},{4... | collective-permute-start | bytes 1179656 | tf_op jit(solution)/shard_map/ppermute | solution.py:21
  102.9 8.2 %all-to-all-done.1.arrived_ref = bf16[32,24,128]{2,1,0:T(8,128)(2,1)S(1)} async-done(((bf16[32,24,128]{2,1,0:T(8,128)(2,1)}), bf16[32,24,128]{2,1,0:T(8,128)(2,1)S(1)}, u32[]{:S(2)}, u32[]{:S(2)}) %all-to-all-start.1) | async-done | bytes 196640 | tf_op jit(solution)/shard_map/all_to_all | solution.py:335
  111.1 13.6 %all_to_all.21.arrived_ref = bf16[16,32,128]{2,1,0:T(8,128)(2,1)S(1)} all-to-all(bf16[16,32,128]{2,1,0:T(8,128)(2,1)S(1)} %shard_map.96), channel_id=1, replica_groups=mesh['section'=2,'sy'=8,'sx'=8,'mb'=4] {'section','sy'}, dimensions={0} | all-to-all | bytes 262144 | tf_op jit(solution)/shard_map/all_to_all | solution.py:335
  124.7 0.8 shard_map.97
  125.5 3.9 %all-to-all-start.3 = ((bf16[32,16,128]{2,1,0:T(8,128)(2,1)}), bf16[32,16,128]{2,1,0:T(8,128)(2,1)S(1)}, u32[]{:S(2)}, u32[]{:S(2)}) async-start(bf16[32,16,128]{2,1,0:T(8,128)(2,1)} %shard_map.97), calls=%async_computation.3 | async-start | bytes 262144 | tf_op jit(solution)/shard_map/all_to_all | solution.py:335
  129.4 1.1 maximum_select_fusion.1
  130.4 8.3 %all-to-all-done.3.arrived_ref = bf16[32,16,128]{2,1,0:T(8,128)(2,1)S(1)} async-done(((bf16[32,16,128]{2,1,0:T(8,128)(2,1)}), bf16[32,16,128]{2,1,0:T(8,128)(2,1)S(1)}, u32[]{:S(2)}, u32[]{:S(2)}) %all-to-all-start.3) | async-done | bytes 131104 | tf_op jit(solution)/shard_map/all_to_all | solution.py:335
  138.7 0.8 shard_map.98
  (22 shorter events, 0.2 us)
Async XLA Ops:
  7.2 24.9 %copy-start = (bf16[1,64,64,128]{3,2,1,0:T(8,128)(2,1)S(1)}, bf16[1,64,64,128]{3,2,1,0:T(8,128)(2,1)}, u32[]{:S(2)}) copy-start(bf16[1,64,64,128]{3,2,1,0:T(8,128)(2,1)} %param.7) | copy-start | bytes 3145732
  7.2 69.1 %all-gather.2.cloned.1.call-start = ((), (), s32[]{:S(2)}) async-start(), calls=%async_computation.4 | async-start | bytes 5640192 | tf_op jit(solution)/shard_map/all_gather | solution.py:257
  31.2 3.9 %copy-start.6 = (f32[1,1,384]{2,1,0:T(1,128)S(1)}, f32[1,1,384]{2,1,0:T(1,128)}, u32[]{:S(2)}) copy-start(f32[1,1,384]{2,1,0:T(1,128)} %param.10) | copy-start | bytes 4612
  31.2 10.3 %copy-start.4 = (bf16[1,32,32,256]{3,2,1,0:T(8,128)(2,1)S(1)}, bf16[1,32,32,256]{3,2,1,0:T(8,128)(2,1)}, u32[]{:S(2)}) copy-start(bf16[1,32,32,256]{3,2,1,0:T(8,128)(2,1)} %param.12) | copy-start | bytes 1572868
  33.8 12.6 %copy-start.5 = (s32[1,32,32]{2,1,0:T(8,128)S(1)}, s32[1,32,32]{2,1,0:T(8,128)}, u32[]{:S(2)}) copy-start(s32[1,32,32]{2,1,0:T(8,128)} %param.13) | copy-start | bytes 12292
  33.8 7.8 %collective-permute-start = (bf16[9,32,384]{2,1,0:T(8,128)(2,1)S(1)}, bf16[9,32,384]{2,1,0:T(8,128)(2,1)S(1)}, u32[]{:S(2)}, u32[]{:S(2)}) collective-permute-start(bf16[9,32,384]{2,1,0:T(8,128)(2,1)S(1)} %slice_select_fusion), channel_id=1, source_target_pairs={{0,32},{32,64},{64,96},{96,128},{128,160},{160,192},{192,224},{288... | collective-permute-start | bytes 663560 | tf_op jit(solution)/shard_map/ppermute | solution.py:274
  35.1 11.5 %collective-permute-start.3 = (f32[384]{0:T(512)S(1)}, f32[384]{0:T(512)S(1)}, u32[]{:S(2)}, u32[]{:S(2)}) collective-permute-start(f32[384]{0:T(512)S(1)} %reduce), channel_id=1, source_target_pairs={{0,256},{256,0},{1,257},{257,1},{2,258},{258,2},{3,259},{259,3},{4... | collective-permute-start | bytes 4616 | tf_op jit(solution)/shard_map/ppermute | solution.py:21
  41.5 34.8 %copy-start.3 = (bf16[384,256]{1,0:T(8,128)(2,1)S(1)}, bf16[384,256]{1,0:T(8,128)(2,1)}, u32[]{:S(2)}) copy-start(bf16[384,256]{1,0:T(8,128)(2,1)} %head_ref) | copy-start | bytes 589828
  42.8 10.1 %collective-permute-start.1 = (bf16[34,9,384]{2,1,0:T(8,128)(2,1)}, bf16[34,9,384]{2,1,0:T(8,128)(2,1)S(1)}, u32[]{:S(2)}, u32[]{:S(2)}) collective-permute-start(bf16[34,9,384]{2,1,0:T(8,128)(2,1)} %get-tuple-element.32), channel_id=1, source_target_pairs={{0,4},{4,8},{8,12},{12,16},{16,20},{20,24},{24,28},{1,5},{5,9},{9,... | collective-permute-start | bytes 705032 | tf_op jit(solution)/shard_map/ppermute | solution.py:282
  45.0 11.8 %collective-permute-start.2 = (bf16[34,9,384]{2,1,0:T(8,128)(2,1)}, bf16[34,9,384]{2,1,0:T(8,128)(2,1)S(1)}, u32[]{:S(2)}, u32[]{:S(2)}) collective-permute-start(bf16[34,9,384]{2,1,0:T(8,128)(2,1)} %get-tuple-element.31), channel_id=1, source_target_pairs={{4,0},{8,4},{12,8},{16,12},{20,16},{24,20},{28,24},{5,1},{9,5},{13... | collective-permute-start | bytes 705032 | tf_op jit(solution)/shard_map/ppermute | solution.py:283
  62.1 1.9 %copy-start.1 = (bf16[34,48,1152]{2,1,0:T(8,128)(2,1)}, bf16[34,48,1152]{2,1,0:T(8,128)(2,1)S(1)}, u32[]{:S(2)}) copy-start(bf16[34,48,1152]{2,1,0:T(8,128)(2,1)S(1)} %get-tuple-element.19.stacked_hbm) | copy-start | bytes 11280388
  64.0 1.0 copy-start.2
  90.5 20.6 %all-to-all-start.1 = ((bf16[32,24,128]{2,1,0:T(8,128)(2,1)}), bf16[32,24,128]{2,1,0:T(8,128)(2,1)S(1)}, u32[]{:S(2)}, u32[]{:S(2)}) async-start(bf16[32,24,128]{2,1,0:T(8,128)(2,1)} %get-tuple-element.27), calls=%async_computation.1 | async-start | bytes 393216 | tf_op jit(solution)/shard_map/all_to_all | solution.py:335
  100.5 28.9 %collective-permute-start.4 = (bf16[16,32,384]{2,1,0:T(8,128)(2,1)S(1)}, bf16[16,32,384]{2,1,0:T(8,128)(2,1)S(1)}, u32[]{:S(2)}, u32[]{:S(2)}) collective-permute-start(bf16[16,32,384]{2,1,0:T(8,128)(2,1)S(1)} %broadcast_select_fusion), channel_id=1, source_target_pairs={{0,256},{256,0},{1,257},{257,1},{2,258},{258,2},{3,259},{259,3},{4... | collective-permute-start | bytes 1179656 | tf_op jit(solution)/shard_map/ppermute | solution.py:21
  125.5 13.3 %all-to-all-start.3 = ((bf16[32,16,128]{2,1,0:T(8,128)(2,1)}), bf16[32,16,128]{2,1,0:T(8,128)(2,1)S(1)}, u32[]{:S(2)}, u32[]{:S(2)}) async-start(bf16[32,16,128]{2,1,0:T(8,128)(2,1)} %shard_map.97), calls=%async_computation.3 | async-start | bytes 262144 | tf_op jit(solution)/shard_map/all_to_all | solution.py:335
Sparse Core Ops, SparseCore 0:
  32.1 44.0 all-gather.1

commit v8 on v7

--- a/solution.py
+++ b/solution.py
@@ -39,6 +39,16 @@
     ):
         under = under * square + term
     return value * over / under
+
+
+def gelu(value):
+    size = jnp.abs(value)
+    inner = 1.0 / (1.0 + (0.3275911 * 0.7071067811865476) * size)
+    half_tail = jnp.float32(0.5 * 1.061405429)
+    for term in (-1.453152027, 1.421413741, -0.284496736, 0.254829592):
+        half_tail = half_tail * inner + 0.5 * term
+    half_tail = half_tail * inner * jnp.exp(-0.5 * value * value)
+    return jnp.maximum(value, 0.0) - size * half_tail
 
 
 def layers_kernel(
@@ -122,7 +132,7 @@
         row_at = row_start + t * band + lax.broadcasted_iota(jnp.int32, (band, wide, 1), 0)
         inside = column_in & (row_at >= 0) & (row_at < side * parts_y)
         normed = offset * jnp.where(inside, lax.rsqrt(spread + 1e-05), 0.0) * gain
-        active = 0.5 * normed * (1.0 + erf(normed * 0.7071067811865476))
+        active = gelu(normed)
         for j in range(3):
             hidden_ref[t * band : (t + 1) * band, :, j * channels : (j + 1) * channels] = active[
                 :, j * far : j * far + side

time: 148 us -> 147 us (level)
  no operation moved by 1% of the time
where the time goes in v8:
time: 147 us; the launch traced here: 146 us
  waiting for transfers between devices  37.9 us (26%)
  blocking collectives  36.6 us (25%)
  starting transfers between devices  27.3 us (19%)
  Pallas kernels  20.7 us (14%)
  between operations  14.3 us (10%)
  local copies, waits for them, and re-layouts  6.06 us (4%)
  matrix products  1.7 us (1%)
    all_to_all x1, blocking collectives, copies_to(): lax.all_to_all(jnp.broadcast_to(block[None], (count,) + block.shape), axe...  23 us
    all_to_all x2, waiting for transfers between devices, exchange(): return lax.all_to_all(blocks, axes, split_axis=0, concat_axis=0, tiled=True)  16.5 us
    all_to_all x2, starting transfers between devices, exchange(): return lax.all_to_all(blocks, axes, split_axis=0, concat_axis=0, tiled=True)  13.8 us
    pallas_call x1, Pallas kernels, per_device(): pl.pallas_call(functools.partial(layers_kernel, (far, half, side, 8, slot...  13.7 us
    all_to_all x1, blocking collectives, exchange(): return lax.all_to_all(blocks, axes, split_axis=0, concat_axis=0, tiled=True)  13.6 us
    all_gather x1, waiting for transfers between devices, per_device(): lax.all_gather(strip.reshape(parts_x * shard.shape[0], channels), ('secti...  11.3 us
    ppermute x2, starting transfers between devices, swap(): return lax.ppermute(block, 'section', [(0, 1), (1, 0)])  8.76 us
    ppermute x1, waiting for transfers between devices, per_device(): left = lax.ppermute(rows[:, side - reach:], 'sx', forward)  6.28 us
  transfers between devices with their start and end apart: 8, of which 5 were waited for; matrix products, arithmetic and copies ran while one was open for 3% of the time, Pallas kernels for 4%

profile of v8, /device:TPU:1, one launch (start us, length us, event | category | flops | bytes accessed | tf_op | source)
XLA Modules:
  0.0 145.9 jit_solution(11493352854537574284)
XLA Ops:
  7.2 0.0 copy-start
  7.2 0.0 all-gather.2.cloned.1.call-start
  7.2 0.9 broadcast_in_dim.9
  8.1 23.0 %all_to_all.20 = bf16[8,54,384]{2,1,0:T(8,128)(2,1)S(1)} all-to-all(bf16[8,54,384]{2,1,0:T(8,128)(2,1)S(1)} %broadcast_in_dim.9), channel_id=1, replica_groups=mesh['section'=2,'sy'=8,'sx'=8,'mb'=4] {'sx'}, dimensions={0} | all-to-all | bytes 663552 | tf_op jit(solution)/shard_map/all_to_all | solution.py:15
  31.2 0.8 reshape.86
  32.0 0.0 all-gather.2.cloned.1.call-update
  32.0 1.7 %fusion = bf16[32,32,384]{2,1,0:T(8,128)(2,1)S(1)} fusion(bf16[2,2,128,384,1]{3,2,1,4,0:T(8,128)(2,1)} %bitcast.28, bf16[32,2,32,2,128]{4,3,2,1,0:T(2,128)(2,1)S(1)} %bitcast.22), kind=kOutput, calls=%fused_computation.1 | convolution fusion | flops 403046400 | bytes 2228224 | tf_op jit(solution)/shard_map/apbqc,pqco->abo/dot_general | solution.py:276
  33.8 1.3 collective-permute-start
  35.1 6.3 %collective-permute-start.3 = (f32[384]{0:T(512)S(1)}, f32[384]{0:T(512)S(1)}, u32[]{:S(2)}, u32[]{:S(2)}) collective-permute-start(f32[384]{0:T(512)S(1)} %reduce), channel_id=1, source_target_pairs={{0,256},{256,0},{1,257},{257,1},{2,258},{258,2},{3,259},{259,3},{4... | collective-permute-start | bytes 4616 | tf_op jit(solution)/shard_map/ppermute | solution.py:21
  41.5 0.1 fusion.3
  41.6 0.2 maximum_select_fusion.rows_ref
  41.8 1.0 fusion.2
  42.8 2.2 %collective-permute-start.1 = (bf16[34,9,384]{2,1,0:T(8,128)(2,1)}, bf16[34,9,384]{2,1,0:T(8,128)(2,1)S(1)}, u32[]{:S(2)}, u32[]{:S(2)}) collective-permute-start(bf16[34,9,384]{2,1,0:T(8,128)(2,1)} %get-tuple-element.32), channel_id=1, source_target_pairs={{0,4},{4,8},{8,12},{12,16},{16,20},{20,24},{24,28},{1,5},{5,9},{9,... | collective-permute-start | bytes 705032 | tf_op jit(solution)/shard_map/ppermute | solution.py:292
  45.0 1.3 collective-permute-start.2
  46.4 0.3 reshape.92.target_ref
  46.7 6.3 %collective-permute-done.1.left_ref = bf16[34,9,384]{2,1,0:T(8,128)(2,1)S(1)} collective-permute-done((bf16[34,9,384]{2,1,0:T(8,128)(2,1)}, bf16[34,9,384]{2,1,0:T(8,128)(2,1)S(1)}, u32[]{:S(2)}, u32[]{:S(2)}) %collective-permute-start.1) | collective-permute-done | bytes 235040 | tf_op jit(solution)/shard_map/ppermute | solution.py:292
  53.0 3.9 %collective-permute-done.2.right_ref = bf16[34,9,384]{2,1,0:T(8,128)(2,1)S(1)} collective-permute-done((bf16[34,9,384]{2,1,0:T(8,128)(2,1)}, bf16[34,9,384]{2,1,0:T(8,128)(2,1)S(1)}, u32[]{:S(2)}, u32[]{:S(2)}) %collective-permute-start.2) | collective-permute-done | bytes 235040 | tf_op jit(solution)/shard_map/ppermute | solution.py:293
  56.8 5.3 %shard_map.94 = (bf16[34,48,1152]{2,1,0:T(8,128)(2,1)S(1)}, bf16[32,48,384]{2,1,0:T(8,128)(2,1)S(1)}) custom-call(bf16[34,9,384]{2,1,0:T(8,128)(2,1)S(1)} %collective-permute-done.1.left_ref, bf16[34,32,384]{2,1,0:T(8,128)(2,1)S(1)} %maximum_select_fusion.rows_ref, bf16[34,9,384]{2,1,0:T(8,128)(2,1)S(1)} %collective-permute-done.2.right_ref, ...), custom_call_target="tpu_custom_call" | custom-call | tf_op jit(solution)/shard_map/pallas_call | solution.py:298
  62.1 1.9 %copy-done.1 = bf16[34,48,1152]{2,1,0:T(8,128)(2,1)} copy-done((bf16[34,48,1152]{2,1,0:T(8,128)(2,1)}, bf16[34,48,1152]{2,1,0:T(8,128)(2,1)S(1)}, u32[]{:S(2)}) %copy-start.1) | copy-done | bytes 3760152
  64.0 1.0 copy-done.2
  65.0 11.3 %all-gather.2.cloned.1.call-done.weights_ref = bf16[6912,384]{1,0:T(8,128)(2,1)} async-done(((bf16[432,384]{1,0:T(8,128)(2,1)}), bf16[6912,384]{1,0:T(8,128)(2,1)}) %all-gather.2.cloned.1.call-update) | async-done | bytes 5308432 | tf_op jit(solution)/shard_map/all_gather | solution.py:267
  76.3 13.7 %shard_map.95 = (bf16[16,32,384]{2,1,0:T(8,128)(2,1)S(1)}, bf16[16,32,384]{2,1,0:T(8,128)(2,1)S(1)}, bf16[32,24,128]{2,1,0:T(8,128)(2,1)}, f32[8,128]{1,0:T(8,128)S(1)}) custom-call(bf16[34,48,1152]{2,1,0:T(8,128)(2,1)} %copy-done.1, bf16[32,48,384]{2,1,0:T(8,128)(2,1)} %copy-done.2, bf16[6912,384]{1,0:T(8,128)(2,1)} %all-gather.2.cloned.1.call-done.weights_ref, ...), custom_call_target="tpu_custom_call" | custom-call | flops 5435817984 | bytes 5308416 | tf_op jit(solution)/shard_map/pallas_call | solution.py:317
  90.0 9.9 %all-to-all-start.1 = ((bf16[32,24,128]{2,1,0:T(8,128)(2,1)}), bf16[32,24,128]{2,1,0:T(8,128)(2,1)S(1)}, u32[]{:S(2)}, u32[]{:S(2)}) async-start(bf16[32,24,128]{2,1,0:T(8,128)(2,1)} %get-tuple-element.27), calls=%async_computation.1 | async-start | bytes 393216 | tf_op jit(solution)/shard_map/all_to_all | solution.py:345
  99.9 0.1 broadcast_select_fusion
  99.9 2.4 %collective-permute-start.4 = (bf16[16,32,384]{2,1,0:T(8,128)(2,1)S(1)}, bf16[16,32,384]{2,1,0:T(8,128)(2,1)S(1)}, u32[]{:S(2)}, u32[]{:S(2)}) collective-permute-start(bf16[16,32,384]{2,1,0:T(8,128)(2,1)S(1)} %broadcast_select_fusion), channel_id=1, source_target_pairs={{0,256},{256,0},{1,257},{257,1},{2,258},{258,2},{3,259},{259,3},{4... | collective-permute-start | bytes 1179656 | tf_op jit(solution)/shard_map/ppermute | solution.py:21
  102.4 8.2 %all-to-all-done.1.arrived_ref = bf16[32,24,128]{2,1,0:T(8,128)(2,1)S(1)} async-done(((bf16[32,24,128]{2,1,0:T(8,128)(2,1)}), bf16[32,24,128]{2,1,0:T(8,128)(2,1)S(1)}, u32[]{:S(2)}, u32[]{:S(2)}) %all-to-all-start.1) | async-done | bytes 196640 | tf_op jit(solution)/shard_map/all_to_all | solution.py:345
  110.6 13.6 %all_to_all.21.arrived_ref = bf16[16,32,128]{2,1,0:T(8,128)(2,1)S(1)} all-to-all(bf16[16,32,128]{2,1,0:T(8,128)(2,1)S(1)} %shard_map.96), channel_id=1, replica_groups=mesh['section'=2,'sy'=8,'sx'=8,'mb'=4] {'section','sy'}, dimensions={0} | all-to-all | bytes 262144 | tf_op jit(solution)/shard_map/all_to_all | solution.py:345
  124.1 0.8 shard_map.97
  124.9 3.9 %all-to-all-start.3 = ((bf16[32,16,128]{2,1,0:T(8,128)(2,1)}), bf16[32,16,128]{2,1,0:T(8,128)(2,1)S(1)}, u32[]{:S(2)}, u32[]{:S(2)}) async-start(bf16[32,16,128]{2,1,0:T(8,128)(2,1)} %shard_map.97), calls=%async_computation.3 | async-start | bytes 262144 | tf_op jit(solution)/shard_map/all_to_all | solution.py:345
  128.8 1.1 maximum_select_fusion.1
  129.8 8.3 %all-to-all-done.3.arrived_ref = bf16[32,16,128]{2,1,0:T(8,128)(2,1)S(1)} async-done(((bf16[32,16,128]{2,1,0:T(8,128)(2,1)}), bf16[32,16,128]{2,1,0:T(8,128)(2,1)S(1)}, u32[]{:S(2)}, u32[]{:S(2)}) %all-to-all-start.3) | async-done | bytes 131104 | tf_op jit(solution)/shard_map/all_to_all | solution.py:345
  138.2 0.8 shard_map.98
  (22 shorter events, 0.2 us)
Async XLA Ops:
  7.2 24.9 %copy-start = (bf16[1,64,64,128]{3,2,1,0:T(8,128)(2,1)S(1)}, bf16[1,64,64,128]{3,2,1,0:T(8,128)(2,1)}, u32[]{:S(2)}) copy-start(bf16[1,64,64,128]{3,2,1,0:T(8,128)(2,1)} %param.7) | copy-start | bytes 3145732
  7.2 69.1 %all-gather.2.cloned.1.call-start = ((), (), s32[]{:S(2)}) async-start(), calls=%async_computation.4 | async-start | bytes 5640192 | tf_op jit(solution)/shard_map/all_gather | solution.py:267
  31.2 3.9 %copy-start.6 = (f32[1,1,384]{2,1,0:T(1,128)S(1)}, f32[1,1,384]{2,1,0:T(1,128)}, u32[]{:S(2)}) copy-start(f32[1,1,384]{2,1,0:T(1,128)} %param.10) | copy-start | bytes 4612
  31.2 10.3 %copy-start.4 = (bf16[1,32,32,256]{3,2,1,0:T(8,128)(2,1)S(1)}, bf16[1,32,32,256]{3,2,1,0:T(8,128)(2,1)}, u32[]{:S(2)}) copy-start(bf16[1,32,32,256]{3,2,1,0:T(8,128)(2,1)} %param.12) | copy-start | bytes 1572868
  33.8 12.6 %copy-start.5 = (s32[1,32,32]{2,1,0:T(8,128)S(1)}, s32[1,32,32]{2,1,0:T(8,128)}, u32[]{:S(2)}) copy-start(s32[1,32,32]{2,1,0:T(8,128)} %param.13) | copy-start | bytes 12292
  33.8 7.8 %collective-permute-start = (bf16[9,32,384]{2,1,0:T(8,128)(2,1)S(1)}, bf16[9,32,384]{2,1,0:T(8,128)(2,1)S(1)}, u32[]{:S(2)}, u32[]{:S(2)}) collective-permute-start(bf16[9,32,384]{2,1,0:T(8,128)(2,1)S(1)} %slice_select_fusion), channel_id=1, source_target_pairs={{0,32},{32,64},{64,96},{96,128},{128,160},{160,192},{192,224},{288... | collective-permute-start | bytes 663560 | tf_op jit(solution)/shard_map/ppermute | solution.py:284
  35.1 11.5 %collective-permute-start.3 = (f32[384]{0:T(512)S(1)}, f32[384]{0:T(512)S(1)}, u32[]{:S(2)}, u32[]{:S(2)}) collective-permute-start(f32[384]{0:T(512)S(1)} %reduce), channel_id=1, source_target_pairs={{0,256},{256,0},{1,257},{257,1},{2,258},{258,2},{3,259},{259,3},{4... | collective-permute-start | bytes 4616 | tf_op jit(solution)/shard_map/ppermute | solution.py:21
  41.5 34.8 %copy-start.3 = (bf16[384,256]{1,0:T(8,128)(2,1)S(1)}, bf16[384,256]{1,0:T(8,128)(2,1)}, u32[]{:S(2)}) copy-start(bf16[384,256]{1,0:T(8,128)(2,1)} %head_ref) | copy-start | bytes 589828
  42.8 10.1 %collective-permute-start.1 = (bf16[34,9,384]{2,1,0:T(8,128)(2,1)}, bf16[34,9,384]{2,1,0:T(8,128)(2,1)S(1)}, u32[]{:S(2)}, u32[]{:S(2)}) collective-permute-start(bf16[34,9,384]{2,1,0:T(8,128)(2,1)} %get-tuple-element.32), channel_id=1, source_target_pairs={{0,4},{4,8},{8,12},{12,16},{16,20},{20,24},{24,28},{1,5},{5,9},{9,... | collective-permute-start | bytes 705032 | tf_op jit(solution)/shard_map/ppermute | solution.py:292
  45.0 11.8 %collective-permute-start.2 = (bf16[34,9,384]{2,1,0:T(8,128)(2,1)}, bf16[34,9,384]{2,1,0:T(8,128)(2,1)S(1)}, u32[]{:S(2)}, u32[]{:S(2)}) collective-permute-start(bf16[34,9,384]{2,1,0:T(8,128)(2,1)} %get-tuple-element.31), channel_id=1, source_target_pairs={{4,0},{8,4},{12,8},{16,12},{20,16},{24,20},{28,24},{5,1},{9,5},{13... | collective-permute-start | bytes 705032 | tf_op jit(solution)/shard_map/ppermute | solution.py:293
  62.1 1.9 %copy-start.1 = (bf16[34,48,1152]{2,1,0:T(8,128)(2,1)}, bf16[34,48,1152]{2,1,0:T(8,128)(2,1)S(1)}, u32[]{:S(2)}) copy-start(bf16[34,48,1152]{2,1,0:T(8,128)(2,1)S(1)} %get-tuple-element.19.stacked_hbm) | copy-start | bytes 11280388
  64.0 1.0 copy-start.2
  90.0 20.6 %all-to-all-start.1 = ((bf16[32,24,128]{2,1,0:T(8,128)(2,1)}), bf16[32,24,128]{2,1,0:T(8,128)(2,1)S(1)}, u32[]{:S(2)}, u32[]{:S(2)}) async-start(bf16[32,24,128]{2,1,0:T(8,128)(2,1)} %get-tuple-element.27), calls=%async_computation.1 | async-start | bytes 393216 | tf_op jit(solution)/shard_map/all_to_all | solution.py:345
  99.9 28.9 %collective-permute-start.4 = (bf16[16,32,384]{2,1,0:T(8,128)(2,1)S(1)}, bf16[16,32,384]{2,1,0:T(8,128)(2,1)S(1)}, u32[]{:S(2)}, u32[]{:S(2)}) collective-permute-start(bf16[16,32,384]{2,1,0:T(8,128)(2,1)S(1)} %broadcast_select_fusion), channel_id=1, source_target_pairs={{0,256},{256,0},{1,257},{257,1},{2,258},{258,2},{3,259},{259,3},{4... | collective-permute-start | bytes 1179656 | tf_op jit(solution)/shard_map/ppermute | solution.py:21
  124.9 13.3 %all-to-all-start.3 = ((bf16[32,16,128]{2,1,0:T(8,128)(2,1)}), bf16[32,16,128]{2,1,0:T(8,128)(2,1)S(1)}, u32[]{:S(2)}, u32[]{:S(2)}) async-start(bf16[32,16,128]{2,1,0:T(8,128)(2,1)} %shard_map.97), calls=%async_computation.3 | async-start | bytes 262144 | tf_op jit(solution)/shard_map/all_to_all | solution.py:345
Sparse Core Ops, SparseCore 0:
  32.1 44.0 all-gather.1

commit v9 on v8

--- a/solution.py
+++ b/solution.py
@@ -155,7 +155,8 @@
     hit = target_ref[...] == lax.broadcasted_iota(jnp.int32, (cells, bins), 1)
     picked = jnp.sum(jnp.where(hit, shifted, 0.0), axis=1, keepdims=True)
     loss = jnp.sum(jnp.log(exp_total) - picked, axis=0, keepdims=True)
-    delta = (exp_terms / exp_total - hit.astype(jnp.float32)).astype(jnp.bfloat16)
+    softmax = exp_terms * (1.0 / exp_total)
+    delta = jnp.where(hit, softmax - 1.0, softmax).astype(jnp.bfloat16)
     gradient = lax.dot_general(
         flat, delta, (((0,), (0,)), ((), ())), preferred_element_type=jnp.float32
     )

time: 147 us -> 147 us (level)
  no operation moved by 1% of the time
where the time goes in v9:
time: 147 us; the launch traced here: 146 us
  waiting for transfers between devices  37.9 us (26%)
  blocking collectives  36.6 us (25%)
  starting transfers between devices  27.3 us (19%)
  Pallas kernels  20.7 us (14%)
  between operations  14.3 us (10%)
  local copies, waits for them, and re-layouts  6.06 us (4%)
  matrix products  1.7 us (1%)
    all_to_all x1, blocking collectives, copies_to(): lax.all_to_all(jnp.broadcast_to(block[None], (count,) + block.shape), axe...  23 us
    all_to_all x2, waiting for transfers between devices, exchange(): return lax.all_to_all(blocks, axes, split_axis=0, concat_axis=0, tiled=True)  16.5 us
    all_to_all x2, starting transfers between devices, exchange(): return lax.all_to_all(blocks, axes, split_axis=0, concat_axis=0, tiled=True)  13.8 us
    pallas_call x1, Pallas kernels, per_device(): pl.pallas_call(functools.partial(layers_kernel, (far, half, side, 8, slot...  13.7 us
    all_to_all x1, blocking collectives, exchange(): return lax.all_to_all(blocks, axes, split_axis=0, concat_axis=0, tiled=True)  13.6 us
    all_gather x1, waiting for transfers between devices, per_device(): lax.all_gather(strip.reshape(parts_x * shard.shape[0], channels), ('secti...  11.3 us
    ppermute x2, starting transfers between devices, swap(): return lax.ppermute(block, 'section', [(0, 1), (1, 0)])  8.76 us
    ppermute x1, waiting for transfers between devices, per_device(): left = lax.ppermute(rows[:, side - reach:], 'sx', forward)  6.28 us
  transfers between devices with their start and end apart: 8, of which 5 were waited for; matrix products, arithmetic and copies ran while one was open for 3% of the time, Pallas kernels for 4%

profile of v9, /device:TPU:1, one launch (start us, length us, event | category | flops | bytes accessed | tf_op | source)
XLA Modules:
  0.0 145.9 jit_solution(17708217667397352073)
XLA Ops:
  7.2 0.0 copy-start
  7.2 0.0 all-gather.2.cloned.1.call-start
  7.2 0.9 broadcast_in_dim.9
  8.1 23.0 %all_to_all.20 = bf16[8,54,384]{2,1,0:T(8,128)(2,1)S(1)} all-to-all(bf16[8,54,384]{2,1,0:T(8,128)(2,1)S(1)} %broadcast_in_dim.9), channel_id=1, replica_groups=mesh['section'=2,'sy'=8,'sx'=8,'mb'=4] {'sx'}, dimensions={0} | all-to-all | bytes 663552 | tf_op jit(solution)/shard_map/all_to_all | solution.py:15
  31.2 0.8 reshape.86
  32.0 0.0 all-gather.2.cloned.1.call-update
  32.0 1.7 %fusion = bf16[32,32,384]{2,1,0:T(8,128)(2,1)S(1)} fusion(bf16[2,2,128,384,1]{3,2,1,4,0:T(8,128)(2,1)} %bitcast.28, bf16[32,2,32,2,128]{4,3,2,1,0:T(2,128)(2,1)S(1)} %bitcast.22), kind=kOutput, calls=%fused_computation.1 | convolution fusion | flops 403046400 | bytes 2228224 | tf_op jit(solution)/shard_map/apbqc,pqco->abo/dot_general | solution.py:277
  33.8 1.3 collective-permute-start
  35.1 6.3 %collective-permute-start.3 = (f32[384]{0:T(512)S(1)}, f32[384]{0:T(512)S(1)}, u32[]{:S(2)}, u32[]{:S(2)}) collective-permute-start(f32[384]{0:T(512)S(1)} %reduce), channel_id=1, source_target_pairs={{0,256},{256,0},{1,257},{257,1},{2,258},{258,2},{3,259},{259,3},{4... | collective-permute-start | bytes 4616 | tf_op jit(solution)/shard_map/ppermute | solution.py:21
  41.5 0.1 fusion.3
  41.6 0.2 maximum_select_fusion.rows_ref
  41.8 1.0 fusion.2
  42.8 2.2 %collective-permute-start.1 = (bf16[34,9,384]{2,1,0:T(8,128)(2,1)}, bf16[34,9,384]{2,1,0:T(8,128)(2,1)S(1)}, u32[]{:S(2)}, u32[]{:S(2)}) collective-permute-start(bf16[34,9,384]{2,1,0:T(8,128)(2,1)} %get-tuple-element.32), channel_id=1, source_target_pairs={{0,4},{4,8},{8,12},{12,16},{16,20},{20,24},{24,28},{1,5},{5,9},{9,... | collective-permute-start | bytes 705032 | tf_op jit(solution)/shard_map/ppermute | solution.py:293
  45.0 1.3 collective-permute-start.2
  46.4 0.3 reshape.92.target_ref
  46.7 6.3 %collective-permute-done.1.left_ref = bf16[34,9,384]{2,1,0:T(8,128)(2,1)S(1)} collective-permute-done((bf16[34,9,384]{2,1,0:T(8,128)(2,1)}, bf16[34,9,384]{2,1,0:T(8,128)(2,1)S(1)}, u32[]{:S(2)}, u32[]{:S(2)}) %collective-permute-start.1) | collective-permute-done | bytes 235040 | tf_op jit(solution)/shard_map/ppermute | solution.py:293
  53.0 3.9 %collective-permute-done.2.right_ref = bf16[34,9,384]{2,1,0:T(8,128)(2,1)S(1)} collective-permute-done((bf16[34,9,384]{2,1,0:T(8,128)(2,1)}, bf16[34,9,384]{2,1,0:T(8,128)(2,1)S(1)}, u32[]{:S(2)}, u32[]{:S(2)}) %collective-permute-start.2) | collective-permute-done | bytes 235040 | tf_op jit(solution)/shard_map/ppermute | solution.py:294
  56.8 5.3 %shard_map.94 = (bf16[34,48,1152]{2,1,0:T(8,128)(2,1)S(1)}, bf16[32,48,384]{2,1,0:T(8,128)(2,1)S(1)}) custom-call(bf16[34,9,384]{2,1,0:T(8,128)(2,1)S(1)} %collective-permute-done.1.left_ref, bf16[34,32,384]{2,1,0:T(8,128)(2,1)S(1)} %maximum_select_fusion.rows_ref, bf16[34,9,384]{2,1,0:T(8,128)(2,1)S(1)} %collective-permute-done.2.right_ref, ...), custom_call_target="tpu_custom_call" | custom-call | tf_op jit(solution)/shard_map/pallas_call | solution.py:299
  62.1 1.9 %copy-done.1 = bf16[34,48,1152]{2,1,0:T(8,128)(2,1)} copy-done((bf16[34,48,1152]{2,1,0:T(8,128)(2,1)}, bf16[34,48,1152]{2,1,0:T(8,128)(2,1)S(1)}, u32[]{:S(2)}) %copy-start.1) | copy-done | bytes 3760152
  64.0 1.0 copy-done.2
  65.0 11.3 %all-gather.2.cloned.1.call-done.weights_ref = bf16[6912,384]{1,0:T(8,128)(2,1)} async-done(((bf16[432,384]{1,0:T(8,128)(2,1)}), bf16[6912,384]{1,0:T(8,128)(2,1)}) %all-gather.2.cloned.1.call-update) | async-done | bytes 5308432 | tf_op jit(solution)/shard_map/all_gather | solution.py:268
  76.3 13.7 %shard_map.95 = (bf16[16,32,384]{2,1,0:T(8,128)(2,1)S(1)}, bf16[16,32,384]{2,1,0:T(8,128)(2,1)S(1)}, bf16[32,24,128]{2,1,0:T(8,128)(2,1)}, f32[8,128]{1,0:T(8,128)S(1)}) custom-call(bf16[34,48,1152]{2,1,0:T(8,128)(2,1)} %copy-done.1, bf16[32,48,384]{2,1,0:T(8,128)(2,1)} %copy-done.2, bf16[6912,384]{1,0:T(8,128)(2,1)} %all-gather.2.cloned.1.call-done.weights_ref, ...), custom_call_target="tpu_custom_call" | custom-call | flops 5435817984 | bytes 5308416 | tf_op jit(solution)/shard_map/pallas_call | solution.py:318
  90.0 9.9 %all-to-all-start.1 = ((bf16[32,24,128]{2,1,0:T(8,128)(2,1)}), bf16[32,24,128]{2,1,0:T(8,128)(2,1)S(1)}, u32[]{:S(2)}, u32[]{:S(2)}) async-start(bf16[32,24,128]{2,1,0:T(8,128)(2,1)} %get-tuple-element.27), calls=%async_computation.1 | async-start | bytes 393216 | tf_op jit(solution)/shard_map/all_to_all | solution.py:346
  99.9 0.1 broadcast_select_fusion
  99.9 2.4 %collective-permute-start.4 = (bf16[16,32,384]{2,1,0:T(8,128)(2,1)S(1)}, bf16[16,32,384]{2,1,0:T(8,128)(2,1)S(1)}, u32[]{:S(2)}, u32[]{:S(2)}) collective-permute-start(bf16[16,32,384]{2,1,0:T(8,128)(2,1)S(1)} %broadcast_select_fusion), channel_id=1, source_target_pairs={{0,256},{256,0},{1,257},{257,1},{2,258},{258,2},{3,259},{259,3},{4... | collective-permute-start | bytes 1179656 | tf_op jit(solution)/shard_map/ppermute | solution.py:21
  102.4 8.2 %all-to-all-done.1.arrived_ref = bf16[32,24,128]{2,1,0:T(8,128)(2,1)S(1)} async-done(((bf16[32,24,128]{2,1,0:T(8,128)(2,1)}), bf16[32,24,128]{2,1,0:T(8,128)(2,1)S(1)}, u32[]{:S(2)}, u32[]{:S(2)}) %all-to-all-start.1) | async-done | bytes 196640 | tf_op jit(solution)/shard_map/all_to_all | solution.py:346
  110.6 13.6 %all_to_all.21.arrived_ref = bf16[16,32,128]{2,1,0:T(8,128)(2,1)S(1)} all-to-all(bf16[16,32,128]{2,1,0:T(8,128)(2,1)S(1)} %shard_map.96), channel_id=1, replica_groups=mesh['section'=2,'sy'=8,'sx'=8,'mb'=4] {'section','sy'}, dimensions={0} | all-to-all | bytes 262144 | tf_op jit(solution)/shard_map/all_to_all | solution.py:346
  124.1 0.8 shard_map.97
  124.9 3.9 %all-to-all-start.3 = ((bf16[32,16,128]{2,1,0:T(8,128)(2,1)}), bf16[32,16,128]{2,1,0:T(8,128)(2,1)S(1)}, u32[]{:S(2)}, u32[]{:S(2)}) async-start(bf16[32,16,128]{2,1,0:T(8,128)(2,1)} %shard_map.97), calls=%async_computation.3 | async-start | bytes 262144 | tf_op jit(solution)/shard_map/all_to_all | solution.py:346
  128.8 1.1 maximum_select_fusion.1
  129.8 8.3 %all-to-all-done.3.arrived_ref = bf16[32,16,128]{2,1,0:T(8,128)(2,1)S(1)} async-done(((bf16[32,16,128]{2,1,0:T(8,128)(2,1)}), bf16[32,16,128]{2,1,0:T(8,128)(2,1)S(1)}, u32[]{:S(2)}, u32[]{:S(2)}) %all-to-all-start.3) | async-done | bytes 131104 | tf_op jit(solution)/shard_map/all_to_all | solution.py:346
  138.2 0.8 shard_map.98
  (22 shorter events, 0.2 us)
Async XLA Ops:
  7.2 24.9 %copy-start = (bf16[1,64,64,128]{3,2,1,0:T(8,128)(2,1)S(1)}, bf16[1,64,64,128]{3,2,1,0:T(8,128)(2,1)}, u32[]{:S(2)}) copy-start(bf16[1,64,64,128]{3,2,1,0:T(8,128)(2,1)} %param.7) | copy-start | bytes 3145732
  7.2 69.1 %all-gather.2.cloned.1.call-start = ((), (), s32[]{:S(2)}) async-start(), calls=%async_computation.4 | async-start | bytes 5640192 | tf_op jit(solution)/shard_map/all_gather | solution.py:268
  31.2 3.9 %copy-start.6 = (f32[1,1,384]{2,1,0:T(1,128)S(1)}, f32[1,1,384]{2,1,0:T(1,128)}, u32[]{:S(2)}) copy-start(f32[1,1,384]{2,1,0:T(1,128)} %param.10) | copy-start | bytes 4612
  31.2 10.3 %copy-start.4 = (bf16[1,32,32,256]{3,2,1,0:T(8,128)(2,1)S(1)}, bf16[1,32,32,256]{3,2,1,0:T(8,128)(2,1)}, u32[]{:S(2)}) copy-start(bf16[1,32,32,256]{3,2,1,0:T(8,128)(2,1)} %param.12) | copy-start | bytes 1572868
  33.8 12.6 %copy-start.5 = (s32[1,32,32]{2,1,0:T(8,128)S(1)}, s32[1,32,32]{2,1,0:T(8,128)}, u32[]{:S(2)}) copy-start(s32[1,32,32]{2,1,0:T(8,128)} %param.13) | copy-start | bytes 12292
  33.8 7.8 %collective-permute-start = (bf16[9,32,384]{2,1,0:T(8,128)(2,1)S(1)}, bf16[9,32,384]{2,1,0:T(8,128)(2,1)S(1)}, u32[]{:S(2)}, u32[]{:S(2)}) collective-permute-start(bf16[9,32,384]{2,1,0:T(8,128)(2,1)S(1)} %slice_select_fusion), channel_id=1, source_target_pairs={{0,32},{32,64},{64,96},{96,128},{128,160},{160,192},{192,224},{288... | collective-permute-start | bytes 663560 | tf_op jit(solution)/shard_map/ppermute | solution.py:285
  35.1 11.5 %collective-permute-start.3 = (f32[384]{0:T(512)S(1)}, f32[384]{0:T(512)S(1)}, u32[]{:S(2)}, u32[]{:S(2)}) collective-permute-start(f32[384]{0:T(512)S(1)} %reduce), channel_id=1, source_target_pairs={{0,256},{256,0},{1,257},{257,1},{2,258},{258,2},{3,259},{259,3},{4... | collective-permute-start | bytes 4616 | tf_op jit(solution)/shard_map/ppermute | solution.py:21
  41.5 34.8 %copy-start.3 = (bf16[384,256]{1,0:T(8,128)(2,1)S(1)}, bf16[384,256]{1,0:T(8,128)(2,1)}, u32[]{:S(2)}) copy-start(bf16[384,256]{1,0:T(8,128)(2,1)} %head_ref) | copy-start | bytes 589828
  42.8 10.1 %collective-permute-start.1 = (bf16[34,9,384]{2,1,0:T(8,128)(2,1)}, bf16[34,9,384]{2,1,0:T(8,128)(2,1)S(1)}, u32[]{:S(2)}, u32[]{:S(2)}) collective-permute-start(bf16[34,9,384]{2,1,0:T(8,128)(2,1)} %get-tuple-element.32), channel_id=1, source_target_pairs={{0,4},{4,8},{8,12},{12,16},{16,20},{20,24},{24,28},{1,5},{5,9},{9,... | collective-permute-start | bytes 705032 | tf_op jit(solution)/shard_map/ppermute | solution.py:293
  45.0 11.8 %collective-permute-start.2 = (bf16[34,9,384]{2,1,0:T(8,128)(2,1)}, bf16[34,9,384]{2,1,0:T(8,128)(2,1)S(1)}, u32[]{:S(2)}, u32[]{:S(2)}) collective-permute-start(bf16[34,9,384]{2,1,0:T(8,128)(2,1)} %get-tuple-element.31), channel_id=1, source_target_pairs={{4,0},{8,4},{12,8},{16,12},{20,16},{24,20},{28,24},{5,1},{9,5},{13... | collective-permute-start | bytes 705032 | tf_op jit(solution)/shard_map/ppermute | solution.py:294
  62.1 1.9 %copy-start.1 = (bf16[34,48,1152]{2,1,0:T(8,128)(2,1)}, bf16[34,48,1152]{2,1,0:T(8,128)(2,1)S(1)}, u32[]{:S(2)}) copy-start(bf16[34,48,1152]{2,1,0:T(8,128)(2,1)S(1)} %get-tuple-element.19.stacked_hbm) | copy-start | bytes 11280388
  64.0 1.0 copy-start.2
  90.0 20.6 %all-to-all-start.1 = ((bf16[32,24,128]{2,1,0:T(8,128)(2,1)}), bf16[32,24,128]{2,1,0:T(8,128)(2,1)S(1)}, u32[]{:S(2)}, u32[]{:S(2)}) async-start(bf16[32,24,128]{2,1,0:T(8,128)(2,1)} %get-tuple-element.27), calls=%async_computation.1 | async-start | bytes 393216 | tf_op jit(solution)/shard_map/all_to_all | solution.py:346
  99.9 28.9 %collective-permute-start.4 = (bf16[16,32,384]{2,1,0:T(8,128)(2,1)S(1)}, bf16[16,32,384]{2,1,0:T(8,128)(2,1)S(1)}, u32[]{:S(2)}, u32[]{:S(2)}) collective-permute-start(bf16[16,32,384]{2,1,0:T(8,128)(2,1)S(1)} %broadcast_select_fusion), channel_id=1, source_target_pairs={{0,256},{256,0},{1,257},{257,1},{2,258},{258,2},{3,259},{259,3},{4... | collective-permute-start | bytes 1179656 | tf_op jit(solution)/shard_map/ppermute | solution.py:21
  124.9 13.3 %all-to-all-start.3 = ((bf16[32,16,128]{2,1,0:T(8,128)(2,1)}), bf16[32,16,128]{2,1,0:T(8,128)(2,1)S(1)}, u32[]{:S(2)}, u32[]{:S(2)}) async-start(bf16[32,16,128]{2,1,0:T(8,128)(2,1)} %shard_map.97), calls=%async_computation.3 | async-start | bytes 262144 | tf_op jit(solution)/shard_map/all_to_all | solution.py:346
Sparse Core Ops, SparseCore 0:
  32.1 44.0 all-gather.1
